TPU v7x, 512 devices: a whole 4x8x8 slice. The times are simulated.
512 devices in a mesh: fsdp: 64 (over y_lo, z, core), tp: 8 (over x, y_hi).
Axes of the slice: x: 4, y: 8 (y_hi: 2, y_lo: 4; y = y_hi * 4 + y_lo), z: 8, core: 2. Of those that a mesh axis runs over, the one named last changes fastest.
Arguments:
- images: bfloat16 [64, 256, 6144], P('fsdp', None, 'tp'), may hold values from -6 to 6
- keep_index: int32 [64, 64], P('fsdp'), may hold values from 0 to 255, as said below
- teacher_weight: float32 [6144, 3072], P('fsdp', 'tp'), may hold values from -0.078125 to 0.078125
- student_weight: float32 [6144, 3072], P('fsdp', 'tp'), may hold values from -0.078125 to 0.078125
Outputs:
- teacher_next: float32 [6144, 3072], P('fsdp', 'tp')
- student_grad: float32 [6144, 3072], P('fsdp', 'tp')
Inputs may be any that keep to these rules, and one draw needn't show every extreme that they name: `keep_index`: each image's 64 indices are distinct and increasing.
All inputs are finite; a program needn't handle non-finite values.
Results may differ from a plain program's by a relative error of at most 0.0048.
Values may be sent and summed in bfloat16 or wider, within the bound.
No kernel may reach another device: no remote copies, remote signals or barrier semaphores. Data moves between devices by JAX's collectives and lax.ppermute only.
A program may use at most 64 MiB of HBM per device.

v0:
```python
import math

import jax
import jax.numpy as jnp
from jax import lax
from jax.sharding import PartitionSpec as P

D = 6144


def layer_norm(values):
    floats = values.astype(jnp.float32)
    centre = jnp.mean(floats, axis=-1, keepdims=True)
    centred = floats - centre
    spread = jnp.mean(centred * centred, axis=-1, keepdims=True)
    return (centred * lax.rsqrt(spread + 1e-06)).astype(jnp.bfloat16)


def pick_rows(table, index):
    return jax.vmap(lambda block, rows: block[rows])(table, index)


def row_product(features, piece):
    return jnp.dot(features, piece, preferred_element_type=jnp.float32)


def shards(images, keep_index, teacher_weight, student_weight):
    img_count = images.shape[0]
    patch_count = images.shape[1]
    keep_count = keep_index.shape[1]
    columns_dev = teacher_weight.shape[1]
    teacher_next = 0.999 * teacher_weight + (1.0 - 0.999) * student_weight
    teacher_panel = teacher_next.astype(jnp.bfloat16)
    student_panel = student_weight.astype(jnp.bfloat16)
    whole = lax.all_gather(images, "tp", axis=2, tiled=True)
    normed = layer_norm(whole)
    flat_all = normed.reshape(img_count * patch_count, D)
    picked = pick_rows(normed, keep_index).reshape(img_count * keep_count, D)
    teacher_out = row_product(flat_all, lax.all_gather(teacher_panel, "fsdp", axis=0, tiled=True))
    student_out = row_product(picked, lax.all_gather(student_panel, "fsdp", axis=0, tiled=True))
    teacher_out = teacher_out.reshape(img_count, patch_count, columns_dev)
    centre = jnp.mean(teacher_out, axis=1, keepdims=True)
    centred_out = teacher_out - centre
    spread = jnp.mean(centred_out * centred_out, axis=1, keepdims=True)
    target = centred_out * lax.rsqrt(spread + 1e-05)
    target_kept = pick_rows(target, keep_index).reshape(img_count * keep_count, columns_dev)
    total_kept = img_count * keep_count * lax.axis_size("fsdp")
    error = ((student_out - target_kept) * (1.0 / math.sqrt(total_kept))).astype(jnp.bfloat16)
    owned = lax.all_to_all(picked, "fsdp", split_axis=1, concat_axis=0, tiled=True)
    student_grad = lax.dot_general(
        owned,
        lax.all_gather(error, "fsdp", axis=0, tiled=True),
        (((0,), (0,)), ((), ())),
        preferred_element_type=jnp.float32,
    )
    return (teacher_next, student_grad)


def solution(mesh):
    placed = (P("fsdp", None, "tp"), P("fsdp", None), P("fsdp", "tp"), P("fsdp", "tp"))
    return jax.shard_map(
        shards,
        mesh=mesh,
        in_specs=placed,
        out_specs=(P("fsdp", "tp"), P("fsdp", "tp")),
        check_vma=False,
    )
```

profile of v0, /device:TPU:1, one launch (start us, length us, event | category | flops | bytes accessed | tf_op | source)
XLA Modules:
  0.0 498.9 jit_solution(11816537188644948361)
XLA Ops:
  7.2 0.0 all-gather.5.cloned.1.call-start
  7.2 0.7 all-gather.5.cloned.1.call-update
  7.9 0.0 all-gather.9.cloned.1.call-start
  7.9 1.8 fusion.9
  9.7 0.0 all-gather.9.cloned.1.call-update
  9.7 0.0 all-gather.7.cloned.1.call-start
  9.8 0.7 all-gather.7.cloned.1.call-update
  10.5 0.0 all-gather.11.cloned.1.call-start
  10.5 0.7 fusion.8
  11.2 97.9 %all-gather.5.cloned.1.call-done = bf16[1,256,6144]{2,1,0:T(8,128)(2,1)} async-done(((bf16[1,256,768]{2,1,0:T(8,128)(2,1)}), bf16[1,256,6144]{2,1,0:T(8,128)(2,1)}) %all-gather.5.cloned.1.call-update) | async-done | bytes 3145744 | tf_op jit(solution)/shard_map/all_gather | solution.py:35
  109.1 0.0 copy-start
  109.1 2.5 convert_reduce_fusion
  111.7 0.3 copy-done
  111.9 1.0 fusion.2
  112.9 1.2 fusion.3
  114.1 3.8 gather_fusion
  117.9 114.0 %all-gather.9.cloned.1.call-done = bf16[6144,384]{1,0:T(8,128)(2,1)} async-done(((bf16[96,384]{1,0:T(8,128)(2,1)}), bf16[6144,384]{1,0:T(8,128)(2,1)}) %all-gather.9.cloned.1.call-update) | async-done | bytes 4718608 | tf_op jit(solution)/shard_map/all_gather | solution.py:39
  231.9 4.3 fusion.10
  236.2 0.0 copy-start.1
  236.2 0.1 multiply_reduce_fusion
  236.3 0.8 gather_fusion.1
  237.1 116.3 %all-gather.7.cloned.1.call-done = bf16[6144,384]{1,0:T(8,128)(2,1)} async-done(((bf16[96,384]{1,0:T(8,128)(2,1)}), bf16[6144,384]{1,0:T(8,128)(2,1)}) %all-gather.7.cloned.1.call-update) | async-done | bytes 4718608 | tf_op jit(solution)/shard_map/all_gather | solution.py:40
  353.4 4.0 fusion.7
  357.4 0.0 all-gather.11.cloned.1.call-update
  357.4 0.0 copy-done.1
  357.4 1.0 all_to_all.14
  358.5 0.7 copy.6
  359.2 36.8 %all_to_all.19 = bf16[64,64,96]{2,0,1:T(8,128)(2,1)S(1)} all-to-all(bf16[64,64,96]{2,0,1:T(8,128)(2,1)S(1)} %copy.6), channel_id=1, replica_groups=mesh['fsdp'=64,'tp'=8] {'fsdp'}, dimensions={1} | all-to-all | bytes 1572864 | tf_op jit(solution)/shard_map/all_to_all | solution.py:49
  396.0 93.2 %all-gather.11.cloned.1.call-done = bf16[4096,384]{1,0:T(8,128)(2,1)} async-done(((bf16[64,384]{1,0:T(8,128)(2,1)}), bf16[4096,384]{1,0:T(8,128)(2,1)}) %all-gather.11.cloned.1.call-update) | async-done | bytes 3145744 | tf_op jit(solution)/shard_map/all_gather | solution.py:52
  489.2 3.3 fusion.11
  (7 shorter events, 0.1 us)
Async XLA Ops:
  7.2 101.9 %all-gather.5.cloned.1.call-start = ((), (), s32[]{:S(2)}) async-start(), calls=%async_computation.1 | async-start | bytes 3538944 | tf_op jit(solution)/shard_map/all_gather | solution.py:35
  7.9 224.0 %all-gather.9.cloned.1.call-start = ((), (), s32[]{:S(2)}) async-start(), calls=%async_computation.3 | async-start | bytes 4792320 | tf_op jit(solution)/shard_map/all_gather | solution.py:39
  9.7 343.6 %all-gather.7.cloned.1.call-start = ((), (), s32[]{:S(2)}) async-start(), calls=%async_computation.2 | async-start | bytes 4792320 | tf_op jit(solution)/shard_map/all_gather | solution.py:40
  10.5 478.7 %all-gather.11.cloned.1.call-start = ((), (), s32[]{:S(2)}) async-start(), calls=%async_computation.4 | async-start | bytes 3194880 | tf_op jit(solution)/shard_map/all_gather | solution.py:52
  109.1 2.8 copy-start
  236.2 121.3 %copy-start.1 = (bf16[64,6144]{1,0:T(8,128)(2,1)S(1)}, bf16[64,6144]{1,0:T(8,128)(2,1)}, u32[]{:S(2)}) copy-start(bf16[64,6144]{1,0:T(8,128)(2,1)} %gather_fusion) | copy-start | bytes 2359300
Sparse Core Ops, SparseCore 0:
  11.1 97.9 all-gather.4
  111.8 120.0 all-gather.8
  234.0 119.2 all-gather.6
  357.5 131.5 all-gather.10
where the time goes:
time: 499 us
  waiting for transfers between devices  423 us (85%)
  blocking collectives  36.8 us (7%)
  between operations  13.8 us (3%)
  matrix products  11.5 us (2%)
  other arithmetic  7.33 us (1%)
  local copies, waits for them, and re-layouts  6.58 us (1%)
    all_gather x1, waiting for transfers between devices, shards(): lax.all_gather(student_panel, 'fsdp', axis=0, tiled=True)  116 us
    all_gather x1, waiting for transfers between devices, shards(): lax.all_gather(teacher_panel, 'fsdp', axis=0, tiled=True)  114 us
    all_gather x1, waiting for transfers between devices, shards(): whole = lax.all_gather(images, 'tp', axis=2, tiled=True)  97.9 us
    all_gather x1, waiting for transfers between devices, shards(): lax.all_gather(error, 'fsdp', axis=0, tiled=True)  93.2 us
    all_to_all x1, blocking collectives, shards(): lax.all_to_all(picked, 'fsdp', split_axis=1, concat_axis=0, tiled=True)  36.8 us
  transfers between devices with their start and end apart: 4, of which 4 were waited for; matrix products, arithmetic and copies ran while one was open for 3% of the time, Pallas kernels for 0%

commit v1 on v0

v1 whole, which is shorter than its diff:
```python
import math

import jax
import jax.numpy as jnp
from jax import lax
from jax.experimental import pallas as pl
from jax.experimental.pallas import tpu as pltpu
from jax.sharding import Mesh
from jax.sharding import PartitionSpec as P

D = 6144
Y, Z, C, X, H = 4, 8, 2, 4, 2
BF, F32 = jnp.bfloat16, jnp.float32
MB = 1024 * 1024


def normalise_kernel(image_ref, centre_ref, scale_ref, select_ref, normed_ref, picked_ref):
    values = image_ref[0].astype(F32)
    normed = ((values - centre_ref[...]) * scale_ref[...]).astype(BF)
    normed_ref[0] = normed
    picked_ref[0] = jnp.dot(select_ref[...], normed, preferred_element_type=F32).astype(BF)


def normalise(chunks, centre, scale, select):
    n, patches, width = chunks.shape
    keep = select.shape[0]
    small = pl.BlockSpec((patches, 1), lambda k: (0, 0))
    return pl.pallas_call(
        normalise_kernel,
        grid=(n,),
        in_specs=[
            pl.BlockSpec((1, patches, width), lambda k: (k, 0, 0)),
            small,
            small,
            pl.BlockSpec((keep, patches), lambda k: (0, 0)),
        ],
        out_specs=[
            pl.BlockSpec((1, patches, width), lambda k: (k, 0, 0)),
            pl.BlockSpec((1, keep, width), lambda k: (k, 0, 0)),
        ],
        out_shape=[
            jax.ShapeDtypeStruct((n, patches, width), BF),
            jax.ShapeDtypeStruct((n, keep, width), BF),
        ],
        compiler_params=pltpu.CompilerParams(vmem_limit_bytes=24 * MB),
        cost_estimate=pl.CostEstimate(
            flops=2 * n * keep * patches * width, bytes_accessed=2 * n * width * (2 * patches + keep), transcendentals=0
        ),
    )(chunks, centre, scale, select)


def error_kernel(factor, normed_ref, picked_ref, panel_ref, error_ref, teacher_acc, kept_acc):
    step = pl.program_id(0)
    columns = error_ref.shape[1]

    @pl.when(step == 0)
    def _():
        teacher_acc[...] = jnp.zeros_like(teacher_acc)
        kept_acc[...] = jnp.zeros_like(kept_acc)

    panel = panel_ref[:, 0].reshape(-1, 2 * columns)
    teacher_acc[...] += jnp.dot(normed_ref[0], panel[:, :columns], preferred_element_type=F32)
    kept_acc[...] += jnp.dot(picked_ref[0], panel, preferred_element_type=F32)

    @pl.when(step == pl.num_programs(0) - 1)
    def _():
        teacher = teacher_acc[...]
        centre = jnp.mean(teacher, axis=0, keepdims=True)
        centred = teacher - centre
        spread = jnp.mean(centred * centred, axis=0, keepdims=True)
        target = (kept_acc[:, :columns] - centre) * lax.rsqrt(spread + 1e-05)
        error_ref[...] = ((kept_acc[:, columns:] - target) * factor).astype(BF)


def make_error(normed, picked, panels, factor):
    n, patches, width = normed.shape
    keep = picked.shape[1]
    blocks, _, rows, both = panels.shape
    columns = both // 2

    def body(*refs):
        error_kernel(factor, *refs)

    return pl.pallas_call(
        body,
        grid=(n,),
        in_specs=[
            pl.BlockSpec((1, patches, width), lambda k: (k, 0, 0)),
            pl.BlockSpec((1, keep, width), lambda k: (k, 0, 0)),
            pl.BlockSpec((blocks, 1, rows, both), lambda k: (0, k, 0, 0)),
        ],
        out_specs=pl.BlockSpec((keep, columns), lambda k: (0, 0)),
        out_shape=jax.ShapeDtypeStruct((keep, columns), BF),
        scratch_shapes=[pltpu.VMEM((patches, columns), F32), pltpu.VMEM((keep, both), F32)],
        compiler_params=pltpu.CompilerParams(vmem_limit_bytes=56 * MB),
        cost_estimate=pl.CostEstimate(
            flops=2 * n * width * (patches * columns + keep * both),
            bytes_accessed=2 * n * width * (patches + keep + both),
            transcendentals=columns,
        ),
    )(normed, picked, panels)


def spread_to_all(values, axes, size):
    return lax.all_to_all(jnp.broadcast_to(values[None], (size, *values.shape)), axes, split_axis=0, concat_axis=0)


def shards(images, keep_index, teacher_weight, student_weight):
    patches, slice_width = images.shape[1:]
    keep_count = keep_index.shape[1]
    rows, columns = teacher_weight.shape
    image = images[0]

    teacher_next = 0.999 * teacher_weight + (1.0 - 0.999) * student_weight
    panel = jnp.concatenate([teacher_next, student_weight], axis=1).astype(BF)
    other = lax.ppermute(image, "yh", [(0, 1), (1, 0)])
    panels = lax.all_gather(panel, "yl", axis=0, tiled=True)
    panels, other = lax.optimization_barrier((panels, other))
    panels = lax.all_gather(panels, ("z", "c"), axis=0, tiled=True).reshape(Z * C, Y, rows, 2 * columns)

    pair = jnp.where(
        lax.axis_index("yh") == 0,
        jnp.concatenate([image, other], axis=1),
        jnp.concatenate([other, image], axis=1),
    )
    whole = lax.all_gather(pair, "x", axis=0, tiled=False)

    floats = image.astype(F32)
    own_mean = jnp.mean(floats, axis=1)
    own_moment = jnp.sum(jnp.square(floats - own_mean[:, None]), axis=1)
    parts = spread_to_all(jnp.stack([own_mean, own_moment]), ("x", "yh"), X * H)
    centre = jnp.mean(parts[:, 0], axis=0)
    moment = jnp.sum(parts[:, 1], axis=0) + slice_width * jnp.sum(jnp.square(parts[:, 0] - centre), axis=0)
    scale = lax.rsqrt(moment / D + 1e-06)
    centre, scale = centre[:, None], scale[:, None]

    select = (keep_index[0][:, None] == lax.broadcasted_iota(jnp.int32, (keep_count, patches), 1)).astype(BF)

    _, picked_pair = normalise(pair[None], centre, scale, select)
    pieces = picked_pair[0].reshape(keep_count, Z * C, rows).transpose(1, 0, 2)
    pieces = lax.all_to_all(pieces, ("z", "c"), split_axis=0, concat_axis=0)
    owned = spread_to_all(pieces, "x", X)
    owned = owned.reshape(Y, Z * C * keep_count, rows).transpose(0, 2, 1).reshape(Y * rows, Z * C * keep_count)

    normed, picked = normalise(whole, centre, scale, select)
    total_kept = keep_count * Y * Z * C
    error = make_error(normed, picked, panels, 1.0 / math.sqrt(total_kept))
    errors = lax.all_gather(error, ("z", "c"), axis=0, tiled=True)
    partial = jnp.dot(owned, errors, preferred_element_type=F32).astype(BF).reshape(Y, rows, columns)
    partial = lax.all_to_all(partial, "yl", split_axis=0, concat_axis=0)
    student_grad = jnp.sum(partial.astype(F32), axis=0)
    return (teacher_next, student_grad)


def solution(mesh):
    fine = Mesh(mesh.devices.reshape(Y, Z, C, X, H), ("yl", "z", "c", "x", "yh"))
    rows, cols = ("yl", "z", "c"), ("x", "yh")
    return jax.shard_map(
        shards,
        mesh=fine,
        in_specs=(P(rows, None, cols), P(rows, None), P(rows, cols), P(rows, cols)),
        out_specs=(P(rows, cols), P(rows, cols)),
        check_vma=False,
    )
```

time: 499 us -> 219 us (0.44)
  waiting for transfers between devices: 423 us -> 66.4 us
  blocking collectives: 36.8 us -> 103 us
  starting transfers between devices: 0.16 us -> 13.2 us
  matrix products: 11.5 us -> 0.58 us
  Pallas kernels: 0 us -> 10.6 us
    all_gather x4 -> x2, waiting for transfers between devices: 421 us -> 56.8 us  [the longest x1 56.8 us: shards(): lax.all_gather(panels, ('z', 'c'), axis=0, tiled=True)]
    all_gather x0 -> x2, blocking collectives: none -> 44.7 us  [the longest x1 26.8 us: shards(): panels = lax.all_gather(panel, 'yl', axis=0, tiled=True)]
    all_to_all x1 -> x3, blocking collectives: 36.8 us -> 58 us  [the longest x1 27.1 us: shards(): pieces = lax.all_to_all(pieces, ('z', 'c'), split_axis=0, concat_axis=0)]
    dot_general x3 -> x1, matrix products: 11.5 us -> 0.58 us  [shards(): jnp.dot(owned, errors, preferred_element_type=F32).astype(BF)]
    pallas_call x0 -> x3, Pallas kernels: none -> 10.6 us  [the longest x1 7.71 us: make_error(): pl.pallas_call(body, grid=(n,), in_specs=[pl.BlockSpec((1, patches, width...]
    all_to_all x0 -> x1, waiting for transfers between devices: none -> 8.88 us  [spread_to_all(): lax.all_to_all(jnp.broadcast_to(values[None], (size, *values.shape)), axe...]
    ppermute x0 -> x1, starting transfers between devices: none -> 8.41 us  [shards(): other = lax.ppermute(image, 'yh', [(0, 1), (1, 0)])]
  transfers between devices with their start and end apart: 4 -> 4, of which waited for: 4 -> 2; matrix products, arithmetic and copies ran while one was open for 3% -> 2% of each run, Pallas kernels for 0% -> 1%
where the time goes in v1:
time: 219 us; the launch traced here: 218 us
  blocking collectives  103 us (47%)
  waiting for transfers between devices  66.4 us (30%)
  between operations  14.2 us (6%)
  starting transfers between devices  13.2 us (6%)
  Pallas kernels  10.6 us (5%)
  local copies, waits for them, and re-layouts  6.38 us (3%)
  other arithmetic  4.09 us (2%)
    all_gather x1, waiting for transfers between devices, shards(): lax.all_gather(panels, ('z', 'c'), axis=0, tiled=True)  56.8 us
    all_to_all x1, blocking collectives, shards(): pieces = lax.all_to_all(pieces, ('z', 'c'), split_axis=0, concat_axis=0)  27.1 us
    all_gather x1, blocking collectives, shards(): panels = lax.all_gather(panel, 'yl', axis=0, tiled=True)  26.8 us
    all_to_all x1, blocking collectives, spread_to_all(): lax.all_to_all(jnp.broadcast_to(values[None], (size, *values.shape)), axe...  18 us
    all_gather x1, blocking collectives, shards(): errors = lax.all_gather(error, ('z', 'c'), axis=0, tiled=True)  17.9 us
    all_to_all x1, blocking collectives, shards(): partial = lax.all_to_all(partial, 'yl', split_axis=0, concat_axis=0)  12.8 us
    all_to_all x1, waiting for transfers between devices, spread_to_all(): lax.all_to_all(jnp.broadcast_to(values[None], (size, *values.shape)), axe...  8.88 us
    ppermute x1, starting transfers between devices, shards(): other = lax.ppermute(image, 'yh', [(0, 1), (1, 0)])  8.41 us
  transfers between devices with their start and end apart: 4, of which 2 were waited for; matrix products, arithmetic and copies ran while one was open for 2% of the time, Pallas kernels for 1%

profile of v1, /device:TPU:1, one launch (start us, length us, event | category | flops | bytes accessed | tf_op | source)
XLA Modules:
  0.0 218.1 jit_solution(15850801807981892405)
XLA Ops:
  7.2 0.0 copy-start.4
  7.2 0.0 all-gather.3.cloned.1.call-start
  7.2 8.4 %collective-permute-start = (bf16[256,768]{1,0:T(8,128)(2,1)}, bf16[256,768]{1,0:T(8,128)(2,1)S(1)}, u32[]{:S(2)}, u32[]{:S(2)}) collective-permute-start(bf16[256,768]{1,0:T(8,128)(2,1)} %bitcast.28), channel_id=1, source_target_pairs={{0,1},{1,0},{2,3},{3,2},{4,5},{5,4},{6,7},{7,6},{8,9},{9,8},{10,11... | collective-permute-start | bytes 1179656 | tf_op jit(solution)/shard_map/ppermute | solution.py:116
  15.6 1.7 fusion.5
  17.4 26.8 %all_gather.13 = bf16[384,768]{1,0:T(8,128)(2,1)} all-gather(bf16[96,768]{1,0:T(8,128)(2,1)S(1)} %pad_maximum_fusion), channel_id=1, replica_groups=mesh['yl'=4,'z'=8,'c'=2,'x'=4,'yh'=2] {'yl'}, dimensions={0}, use_global_device_ids=true | all-gather | bytes 737280 | tf_op jit(solution)/shard_map/all_gather | solution.py:117
  44.2 0.0 collective-permute-done
  44.2 0.0 copy-done.4
  44.2 0.0 copy-start.5
  44.2 1.1 maximum_select_fusion.image_ref
  45.3 0.0 copy-start
  45.3 0.0 all-gather.3.cloned.1.call-update
  45.3 0.0 all-gather.5.cloned.1.call-start
  45.4 0.7 all-gather.5.cloned.1.call-update
  46.1 0.1 convert_reduce_fusion
  46.2 0.2 fusion.1
  46.5 0.6 broadcast_in_dim.4
  47.1 4.7 %all-to-all-start = ((f32[8,2,256]{2,1,0:T(2,128)}), f32[8,2,256]{2,1,0:T(2,128)S(1)}, u32[]{:S(2)}, u32[]{:S(2)}) async-start(f32[8,2,256]{2,1,0:T(2,128)} %broadcast_in_dim.4), calls=%async_computation | async-start | bytes 32768 | tf_op jit(solution)/shard_map/all_to_all | solution.py:105
  51.8 0.0 copy-done.5
  51.8 0.1 fusion.2.select_ref
  51.8 8.9 %all-to-all-done = f32[8,2,256]{2,1,0:T(2,128)S(1)} async-done(((f32[8,2,256]{2,1,0:T(2,128)}), f32[8,2,256]{2,1,0:T(2,128)S(1)}, u32[]{:S(2)}, u32[]{:S(2)}) %all-to-all-start) | async-done | bytes 16416 | tf_op jit(solution)/shard_map/all_to_all | solution.py:105
  60.8 0.1 copy.32.centre_ref
  61.0 0.1 copy.33.scale_ref
  61.1 0.0 copy-done
  61.1 1.2 shard_map.59
  62.3 0.2 reshape_squeeze.3
  62.5 0.1 copy.43
  62.6 27.1 %all_to_all.20 = bf16[16,64,96]{2,1,0:T(8,128)(2,1)S(1)} all-to-all(bf16[16,64,96]{2,1,0:T(8,128)(2,1)S(1)} %bitcast.29), channel_id=1, replica_groups=mesh['yl'=4,'z'=8,'c'=2,'x'=4,'yh'=2] {'z','c'}, dimensions={0} | all-to-all | bytes 393216 | tf_op jit(solution)/shard_map/all_to_all | solution.py:141
  89.7 0.2 broadcast_in_dim.5
  90.0 18.0 %all_to_all.21 = bf16[4,16,64,96]{3,2,1,0:T(8,128)(2,1)S(1)} all-to-all(bf16[4,16,64,96]{3,2,1,0:T(8,128)(2,1)S(1)} %broadcast_in_dim.5), channel_id=1, replica_groups=mesh['yl'=4,'z'=8,'c'=2,'x'=4,'yh'=2] {'x'}, dimensions={0} | all-to-all | bytes 1572864 | tf_op jit(solution)/shard_map/all_to_all | solution.py:105
  108.0 0.5 copy.35
  108.5 0.0 all-gather.3.cloned.1.call-done.image_ref
  108.6 0.0 copy-start.1
  108.6 1.9 copy-done.1
  110.5 1.7 shard_map.60
  112.2 0.0 copy-start.2
  112.2 1.6 copy-done.2
  113.8 0.0 copy-start.3
  113.8 0.9 copy-done.3
  114.7 56.8 %all-gather.5.cloned.1.call-done = bf16[6144,768]{1,0:T(8,128)(2,1)} async-done(((bf16[384,768]{1,0:T(8,128)(2,1)}), bf16[6144,768]{1,0:T(8,128)(2,1)}) %all-gather.5.cloned.1.call-update) | async-done | bytes 9437200 | tf_op jit(solution)/shard_map/all_gather | solution.py:119
  171.5 7.7 %shard_map.61 = bf16[64,384]{1,0:T(8,128)(2,1)} custom-call(bf16[4,256,1536]{2,1,0:T(8,128)(2,1)} %copy-done.2, bf16[4,64,1536]{2,1,0:T(8,128)(2,1)} %copy-done.3, bf16[16,4,96,768]{3,2,1,0:T(8,128)(2,1)} %bitcast.26), custom_call_target="tpu_custom_call" | custom-call | flops 1811939328 | bytes 13369344 | tf_op jit(solution)/shard_map/pallas_call | solution.py:84
  179.2 17.9 %all_gather.16 = bf16[1024,384]{1,0:T(8,128)(2,1)S(1)} all-gather(bf16[64,384]{1,0:T(8,128)(2,1)} %shard_map.61), channel_id=1, replica_groups=mesh['yl'=4,'z'=8,'c'=2,'x'=4,'yh'=2] {'z','c'}, dimensions={0}, use_global_device_ids=true | all-gather | bytes 835584 | tf_op jit(solution)/shard_map/all_gather | solution.py:148
  197.1 0.6 convolution_convert_fusion
  197.7 12.8 %all_to_all.22 = bf16[4,96,384]{2,1,0:T(8,128)(2,1)S(1)} all-to-all(bf16[4,96,384]{2,1,0:T(8,128)(2,1)S(1)} %bitcast.32), channel_id=1, replica_groups=mesh['yl'=4,'z'=8,'c'=2,'x'=4,'yh'=2] {'yl'}, dimensions={0} | all-to-all | bytes 589824 | tf_op jit(solution)/shard_map/all_to_all | solution.py:150
  210.5 0.7 convert_reduce_fusion.1
  (7 shorter events, 0.1 us)
Async XLA Ops:
  7.2 37.0 %copy-start.4 = (bf16[1,256,768]{2,1,0:T(8,128)(2,1)S(1)}, bf16[1,256,768]{2,1,0:T(8,128)(2,1)}, u32[]{:S(2)}) copy-start(bf16[1,256,768]{2,1,0:T(8,128)(2,1)} %param.4) | copy-start | bytes 1179652
  7.2 101.4 %all-gather.3.cloned.1.call-start = ((), (), s32[]{:S(2)}) async-start(), calls=%async_computation.4 | async-start | bytes 3932160 | tf_op jit(solution)/shard_map/all_gather | solution.py:126
  7.2 37.0 %collective-permute-start = (bf16[256,768]{1,0:T(8,128)(2,1)}, bf16[256,768]{1,0:T(8,128)(2,1)S(1)}, u32[]{:S(2)}, u32[]{:S(2)}) collective-permute-start(bf16[256,768]{1,0:T(8,128)(2,1)} %bitcast.28), channel_id=1, source_target_pairs={{0,1},{1,0},{2,3},{3,2},{4,5},{5,4},{6,7},{7,6},{8,9},{9,8},{10,11... | collective-permute-start | bytes 1179656 | tf_op jit(solution)/shard_map/ppermute | solution.py:116
  44.2 7.6 %copy-start.5 = (s32[1,64]{1,0:T(1,128)S(1)}, s32[1,64]{1,0:T(1,128)}, u32[]{:S(2)}) copy-start(s32[1,64]{1,0:T(1,128)} %param.5) | copy-start | bytes 772
  45.3 15.8 %copy-start = (bf16[1,256,1536]{2,1,0:T(8,128)(2,1)S(1)}, bf16[1,256,1536]{2,1,0:T(8,128)(2,1)}, u32[]{:S(2)}) copy-start(bf16[1,256,1536]{2,1,0:T(8,128)(2,1)} %maximum_select_fusion.image_ref) | copy-start | bytes 2359300
  45.3 126.2 %all-gather.5.cloned.1.call-start = ((), (), s32[]{:S(2)}) async-start(), calls=%async_computation.5 | async-start | bytes 10027008 | tf_op jit(solution)/shard_map/all_gather | solution.py:119
  47.1 13.6 %all-to-all-start = ((f32[8,2,256]{2,1,0:T(2,128)}), f32[8,2,256]{2,1,0:T(2,128)S(1)}, u32[]{:S(2)}, u32[]{:S(2)}) async-start(f32[8,2,256]{2,1,0:T(2,128)} %broadcast_in_dim.4), calls=%async_computation | async-start | bytes 32768 | tf_op jit(solution)/shard_map/all_to_all | solution.py:105
  108.6 1.9 copy-start.1
  112.2 1.6 copy-start.2
  113.8 0.9 copy-start.3
Sparse Core Ops, SparseCore 0:
  45.5 49.2 all-gather.2
  96.9 74.5 all-gather.4

commit v2 on v1

--- a/solution.py
+++ b/solution.py
@@ -49,20 +49,24 @@
     )(chunks, centre, scale, select)
 
 
-def error_kernel(factor, normed_ref, picked_ref, panel_ref, error_ref, teacher_acc, kept_acc):
+def error_kernel(factor, first_ref, *refs):
+    n = pl.num_programs(0)
+    count = (len(refs) - 4) // 2
+    normed_refs, picked_refs = refs[:count], refs[count : 2 * count]
+    panel_ref, error_ref, teacher_acc, kept_acc = refs[2 * count :]
     step = pl.program_id(0)
     columns = error_ref.shape[1]
+    panel = panel_ref[:, 0].reshape(-1, 2 * columns)
+    for k in range(count):
 
-    @pl.when(step == 0)
-    def _():
-        teacher_acc[...] = jnp.zeros_like(teacher_acc)
-        kept_acc[...] = jnp.zeros_like(kept_acc)
+        @pl.when(step == k)
+        def _(k=k):
+            teacher = jnp.dot(normed_refs[k][0], panel[:, :columns], preferred_element_type=F32)
+            kept = jnp.dot(picked_refs[k][0], panel, preferred_element_type=F32)
+            teacher_acc[...] = teacher if k == 0 else teacher_acc[...] + teacher
+            kept_acc[...] = kept if k == 0 else kept_acc[...] + kept
 
-    panel = panel_ref[:, 0].reshape(-1, 2 * columns)
-    teacher_acc[...] += jnp.dot(normed_ref[0], panel[:, :columns], preferred_element_type=F32)
-    kept_acc[...] += jnp.dot(picked_ref[0], panel, preferred_element_type=F32)
-
-    @pl.when(step == pl.num_programs(0) - 1)
+    @pl.when(step == n - 1)
     def _():
         teacher = teacher_acc[...]
         centre = jnp.mean(teacher, axis=0, keepdims=True)
@@ -72,9 +76,10 @@
         error_ref[...] = ((kept_acc[:, columns:] - target) * factor).astype(BF)
 
 
-def make_error(normed, picked, panels, factor):
-    n, patches, width = normed.shape
-    keep = picked.shape[1]
+def make_error(normed, picked, panels, first, factor):
+    n = len(normed)
+    _, patches, width = normed[0].shape
+    keep = picked[0].shape[1]
     blocks, _, rows, both = panels.shape
     columns = both // 2
 
@@ -83,22 +88,23 @@
 
     return pl.pallas_call(
         body,
-        grid=(n,),
-        in_specs=[
-            pl.BlockSpec((1, patches, width), lambda k: (k, 0, 0)),
-            pl.BlockSpec((1, keep, width), lambda k: (k, 0, 0)),
-            pl.BlockSpec((blocks, 1, rows, both), lambda k: (0, k, 0, 0)),
-        ],
-        out_specs=pl.BlockSpec((keep, columns), lambda k: (0, 0)),
+        grid_spec=pltpu.PrefetchScalarGridSpec(
+            num_scalar_prefetch=1,
+            grid=(n,),
+            in_specs=[pl.BlockSpec((1, patches, width), lambda k, first: (0, 0, 0))] * n
+            + [pl.BlockSpec((1, keep, width), lambda k, first: (0, 0, 0))] * n
+            + [pl.BlockSpec((blocks, 1, rows, both), lambda k, first: (0, lax.rem(first[0] + n - k, n), 0, 0))],
+            out_specs=pl.BlockSpec((keep, columns), lambda k, first: (0, 0)),
+            scratch_shapes=[pltpu.VMEM((patches, columns), F32), pltpu.VMEM((keep, both), F32)],
+        ),
         out_shape=jax.ShapeDtypeStruct((keep, columns), BF),
-        scratch_shapes=[pltpu.VMEM((patches, columns), F32), pltpu.VMEM((keep, both), F32)],
         compiler_params=pltpu.CompilerParams(vmem_limit_bytes=56 * MB),
         cost_estimate=pl.CostEstimate(
             flops=2 * n * width * (patches * columns + keep * both),
             bytes_accessed=2 * n * width * (patches + keep + both),
             transcendentals=columns,
         ),
-    )(normed, picked, panels)
+    )(first, *normed, *picked, panels)
 
 
 def spread_to_all(values, axes, size):
@@ -113,9 +119,9 @@
 
     teacher_next = 0.999 * teacher_weight + (1.0 - 0.999) * student_weight
     panel = jnp.concatenate([teacher_next, student_weight], axis=1).astype(BF)
+    panels = lax.all_gather(panel, "yl", axis=0, tiled=True)
+    panels, image = lax.optimization_barrier((panels, image))
     other = lax.ppermute(image, "yh", [(0, 1), (1, 0)])
-    panels = lax.all_gather(panel, "yl", axis=0, tiled=True)
-    panels, other = lax.optimization_barrier((panels, other))
     panels = lax.all_gather(panels, ("z", "c"), axis=0, tiled=True).reshape(Z * C, Y, rows, 2 * columns)
 
     pair = jnp.where(
@@ -123,7 +129,7 @@
         jnp.concatenate([image, other], axis=1),
         jnp.concatenate([other, image], axis=1),
     )
-    whole = lax.all_gather(pair, "x", axis=0, tiled=False)
+    arrived = [lax.ppermute(pair, "x", [(i, (i + s) % X) for i in range(X)]) for s in range(1, X)]
 
     floats = image.astype(F32)
     own_mean = jnp.mean(floats, axis=1)
@@ -136,15 +142,17 @@
 
     select = (keep_index[0][:, None] == lax.broadcasted_iota(jnp.int32, (keep_count, patches), 1)).astype(BF)
 
-    _, picked_pair = normalise(pair[None], centre, scale, select)
-    pieces = picked_pair[0].reshape(keep_count, Z * C, rows).transpose(1, 0, 2)
+    halves = [normalise(pair[None], centre, scale, select)]
+    pieces = halves[0][1][0].reshape(keep_count, Z * C, rows).transpose(1, 0, 2)
     pieces = lax.all_to_all(pieces, ("z", "c"), split_axis=0, concat_axis=0)
     owned = spread_to_all(pieces, "x", X)
     owned = owned.reshape(Y, Z * C * keep_count, rows).transpose(0, 2, 1).reshape(Y * rows, Z * C * keep_count)
 
-    normed, picked = normalise(whole, centre, scale, select)
+    halves += [normalise(chunk[None], centre, scale, select) for chunk in arrived]
+    normed, picked = zip(*halves)
+    first = lax.axis_index("x").reshape(1)
     total_kept = keep_count * Y * Z * C
-    error = make_error(normed, picked, panels, 1.0 / math.sqrt(total_kept))
+    error = make_error(normed, picked, panels, first, 1.0 / math.sqrt(total_kept))
     errors = lax.all_gather(error, ("z", "c"), axis=0, tiled=True)
     partial = jnp.dot(owned, errors, preferred_element_type=F32).astype(BF).reshape(Y, rows, columns)
     partial = lax.all_to_all(partial, "yl", split_axis=0, concat_axis=0)

time: 219 us -> 169 us (0.77)
  blocking collectives: 103 us -> 47 us
  starting transfers between devices: 13.2 us -> 37.4 us
  waiting for transfers between devices: 66.4 us -> 45.8 us
  local copies, waits for them, and re-layouts: 6.38 us -> 9.29 us
    all_gather x1, waiting for transfers between devices: 56.8 us -> 0.02 us  [shards(): lax.all_gather(panels, ('z', 'c'), axis=0, tiled=True)]
    all_to_all x2 -> x0, blocking collectives: 45.2 us -> none  [the longest x1 27.1 us: shards(): pieces = lax.all_to_all(pieces, ('z', 'c'), split_axis=0, concat_axis=0)]
    ppermute x0 -> x3, waiting for transfers between devices: none -> 17.9 us  [shards(): lax.ppermute(pair, 'x', [(i, (i + s) % X) for i in range(X)])]
    all_to_all x1 -> x2, waiting for transfers between devices: 8.88 us -> 22.8 us  [spread_to_all(): lax.all_to_all(jnp.broadcast_to(values[None], (size, *values.shape)), axe...]
    all_to_all x0 -> x1, starting transfers between devices: none -> 12.8 us  [shards(): pieces = lax.all_to_all(pieces, ('z', 'c'), split_axis=0, concat_axis=0)]
    all_gather x1, blocking collectives: 26.8 us -> 15.4 us  [shards(): panels = lax.all_gather(panel, 'yl', axis=0, tiled=True)]
    ppermute x0 -> x3, starting transfers between devices: none -> 8.45 us  [shards(): lax.ppermute(pair, 'x', [(i, (i + s) % X) for i in range(X)])]
    all_to_all x1 -> x2, starting transfers between devices: 4.66 us -> 9.97 us  [spread_to_all(): lax.all_to_all(jnp.broadcast_to(values[None], (size, *values.shape)), axe...]
  transfers between devices with their start and end apart: 4 -> 8, of which waited for: 2 -> 5; matrix products, arithmetic and copies ran while one was open for 2% -> 4% of each run, Pallas kernels for 1% -> 1%
where the time goes in v2:
time: 169 us
  blocking collectives  47 us (28%)
  waiting for transfers between devices  45.8 us (27%)
  starting transfers between devices  37.4 us (22%)
  between operations  14.2 us (8%)
  Pallas kernels  10.3 us (6%)
  local copies, waits for them, and re-layouts  9.29 us (5%)
  other arithmetic  4.27 us (3%)
    all_to_all x2, waiting for transfers between devices, spread_to_all(): lax.all_to_all(jnp.broadcast_to(values[None], (size, *values.shape)), axe...  22.8 us
    all_gather x1, blocking collectives, shards(): errors = lax.all_gather(error, ('z', 'c'), axis=0, tiled=True)  20.1 us
    ppermute x3, waiting for transfers between devices, shards(): lax.ppermute(pair, 'x', [(i, (i + s) % X) for i in range(X)])  17.9 us
    all_gather x1, blocking collectives, shards(): panels = lax.all_gather(panel, 'yl', axis=0, tiled=True)  15.4 us
    all_to_all x1, starting transfers between devices, shards(): pieces = lax.all_to_all(pieces, ('z', 'c'), split_axis=0, concat_axis=0)  12.8 us
    all_to_all x1, blocking collectives, shards(): partial = lax.all_to_all(partial, 'yl', split_axis=0, concat_axis=0)  11.5 us
    all_to_all x2, starting transfers between devices, spread_to_all(): lax.all_to_all(jnp.broadcast_to(values[None], (size, *values.shape)), axe...  9.97 us
    pallas_call x1, Pallas kernels, make_error(): pl.pallas_call(body, grid_spec=pltpu.PrefetchScalarGridSpec(num_scalar_pr...  8.52 us
  transfers between devices with their start and end apart: 8, of which 5 were waited for; matrix products, arithmetic and copies ran while one was open for 4% of the time, Pallas kernels for 1%

profile of v2, /device:TPU:1, one launch (start us, length us, event | category | flops | bytes accessed | tf_op | source)
XLA Modules:
  0.0 168.8 jit_solution(8656063086570832858)
XLA Ops:
  7.2 0.0 copy-start.8
  7.2 0.0 copy-start.9
  7.2 0.0 all-gather.2.cloned.1.call-start
  7.2 1.8 %fusion.5 = (bf16[96,384]{1,0:T(8,128)(2,1)S(1)}, f32[96,384]{1,0:T(8,128)}, bf16[96,384]{1,0:T(8,128)(2,1)S(1)}) fusion(f32[96,384]{1,0:T(8,128)} %param.7, f32[96,384]{1,0:T(8,128)} %param.6), kind=kLoop, calls=%fused_computation.22 | loop fusion | flops 184320 | bytes 589824 | tf_op jit(solution)/shard_map/convert
  9.0 15.4 %all_gather.9 = bf16[384,768]{1,0:T(8,128)(2,1)} all-gather(bf16[96,768]{1,0:T(8,128)(2,1)S(1)} %pad_maximum_fusion), channel_id=1, replica_groups=mesh['yl'=4,'z'=8,'c'=2,'x'=4,'yh'=2] {'yl'}, dimensions={0}, use_global_device_ids=true | all-gather | bytes 737280 | tf_op jit(solution)/shard_map/all_gather | solution.py:122
  24.4 0.0 all-gather.2.cloned.1.call-update
  24.5 6.1 %collective-permute-start = (bf16[256,768]{1,0:T(8,128)(2,1)S(1)}, bf16[256,768]{1,0:T(8,128)(2,1)S(1)}, u32[]{:S(2)}, u32[]{:S(2)}) collective-permute-start(bf16[256,768]{1,0:T(8,128)(2,1)S(1)} %bitcast.33), channel_id=1, source_target_pairs={{0,1},{1,0},{2,3},{3,2},{4,5},{5,4},{6,7},{7,6},{8,9},{9,8},{10,11... | collective-permute-start | bytes 1179656 | tf_op jit(solution)/shard_map/ppermute | solution.py:124
  30.6 0.1 convert_reduce_fusion
  30.7 0.2 fusion.1
  31.0 0.6 broadcast_in_dim.10
  31.6 5.7 %all-to-all-start = ((f32[8,2,256]{2,1,0:T(2,128)}), f32[8,2,256]{2,1,0:T(2,128)S(1)}, u32[]{:S(2)}, u32[]{:S(2)}) async-start(f32[8,2,256]{2,1,0:T(2,128)} %broadcast_in_dim.10), calls=%async_computation | async-start | bytes 32768 | tf_op jit(solution)/shard_map/all_to_all | solution.py:111
  37.3 0.1 fusion.2.select_ref
  37.4 13.9 %all-to-all-done = f32[8,2,256]{2,1,0:T(2,128)S(1)} async-done(((f32[8,2,256]{2,1,0:T(2,128)}), f32[8,2,256]{2,1,0:T(2,128)S(1)}, u32[]{:S(2)}, u32[]{:S(2)}) %all-to-all-start) | async-done | bytes 16416 | tf_op jit(solution)/shard_map/all_to_all | solution.py:111
  51.4 0.1 copy.49.scale_ref
  51.5 0.1 copy.48.centre_ref
  51.7 0.0 collective-permute-done
  51.7 0.2 maximum_select_fusion.image_ref
  51.9 0.4 shard_map.59
  52.3 0.9 copy-done
  53.2 0.2 reshape_squeeze.3
  53.4 0.8 copy.63
  54.2 12.8 %all-to-all-start.1 = ((bf16[16,64,96]{2,1,0:T(8,128)(2,1)}), bf16[16,64,96]{2,1,0:T(8,128)(2,1)S(1)}, u32[]{:S(2)}, u32[]{:S(2)}) async-start(bf16[16,64,96]{2,1,0:T(8,128)(2,1)} %bitcast.28), calls=%async_computation.1 | async-start | bytes 524288 | tf_op jit(solution)/shard_map/all_to_all | solution.py:147
  67.0 1.1 maximum_select_fusion.1
  68.1 2.9 %collective-permute-start.2 = (bf16[256,1536]{1,0:T(8,128)(2,1)}, bf16[256,1536]{1,0:T(8,128)(2,1)S(1)}, u32[]{:S(2)}, u32[]{:S(2)}) collective-permute-start(bf16[256,1536]{1,0:T(8,128)(2,1)} %maximum_select_fusion.1), channel_id=1, source_target_pairs={{0,4},{2,6},{4,0},{6,2},{1,5},{3,7},{5,1},{7,3},{8,12},{10,14},{12... | collective-permute-start | bytes 2359304 | tf_op jit(solution)/shard_map/ppermute | solution.py:132
  71.0 3.7 %collective-permute-start.3 = (bf16[256,1536]{1,0:T(8,128)(2,1)}, bf16[256,1536]{1,0:T(8,128)(2,1)S(1)}, u32[]{:S(2)}, u32[]{:S(2)}) collective-permute-start(bf16[256,1536]{1,0:T(8,128)(2,1)} %maximum_select_fusion.1), channel_id=1, source_target_pairs={{0,6},{2,0},{4,2},{6,4},{1,7},{3,1},{5,3},{7,5},{8,14},{10,8},{12,... | collective-permute-start | bytes 2359304 | tf_op jit(solution)/shard_map/ppermute | solution.py:132
  74.6 1.9 %collective-permute-start.1 = (bf16[256,1536]{1,0:T(8,128)(2,1)}, bf16[256,1536]{1,0:T(8,128)(2,1)S(1)}, u32[]{:S(2)}, u32[]{:S(2)}) collective-permute-start(bf16[256,1536]{1,0:T(8,128)(2,1)} %maximum_select_fusion.1), channel_id=1, source_target_pairs={{0,2},{2,4},{4,6},{6,0},{1,3},{3,5},{5,7},{7,1},{8,10},{10,12},{12... | collective-permute-start | bytes 2359304 | tf_op jit(solution)/shard_map/ppermute | solution.py:132
  76.6 5.0 %all-to-all-done.1 = bf16[16,64,96]{2,1,0:T(8,128)(2,1)S(1)} async-done(((bf16[16,64,96]{2,1,0:T(8,128)(2,1)}), bf16[16,64,96]{2,1,0:T(8,128)(2,1)S(1)}, u32[]{:S(2)}, u32[]{:S(2)}) %all-to-all-start.1) | async-done | bytes 196640 | tf_op jit(solution)/shard_map/all_to_all | solution.py:147
  81.6 1.2 broadcast_in_dim.11
  82.8 4.3 %all-to-all-start.2 = ((bf16[4,16,64,96]{3,2,1,0:T(8,128)(2,1)}), bf16[4,16,64,96]{3,2,1,0:T(8,128)(2,1)}, u32[]{:S(2)}, u32[]{:S(2)}) async-start(bf16[4,16,64,96]{3,2,1,0:T(8,128)(2,1)} %broadcast_in_dim.11), calls=%async_computation.2 | async-start | bytes 2097152 | tf_op jit(solution)/shard_map/all_to_all | solution.py:111
  87.1 3.7 %collective-permute-done.2 = bf16[256,1536]{1,0:T(8,128)(2,1)S(1)} collective-permute-done((bf16[256,1536]{1,0:T(8,128)(2,1)}, bf16[256,1536]{1,0:T(8,128)(2,1)S(1)}, u32[]{:S(2)}, u32[]{:S(2)}) %collective-permute-start.2) | collective-permute-done | bytes 786464 | tf_op jit(solution)/shard_map/ppermute | solution.py:132
  90.8 0.4 shard_map.61
  91.3 0.7 copy-done.5
  92.0 14.2 %collective-permute-done.3 = bf16[256,1536]{1,0:T(8,128)(2,1)S(1)} collective-permute-done((bf16[256,1536]{1,0:T(8,128)(2,1)}, bf16[256,1536]{1,0:T(8,128)(2,1)S(1)}, u32[]{:S(2)}, u32[]{:S(2)}) %collective-permute-start.3) | collective-permute-done | bytes 786464 | tf_op jit(solution)/shard_map/ppermute | solution.py:132
  106.2 0.4 shard_map.62
  106.6 0.9 copy-done.2
  107.5 0.7 copy-done.6
  108.2 0.0 collective-permute-done.1
  108.2 0.4 shard_map.60
  108.6 0.9 copy-done.3
  109.5 0.7 copy-done.7
  110.2 8.9 %all-to-all-done.2 = bf16[4,16,64,96]{3,2,1,0:T(8,128)(2,1)} async-done(((bf16[4,16,64,96]{3,2,1,0:T(8,128)(2,1)}), bf16[4,16,64,96]{3,2,1,0:T(8,128)(2,1)}, u32[]{:S(2)}, u32[]{:S(2)}) %all-to-all-start.2) | async-done | bytes 786464 | tf_op jit(solution)/shard_map/all_to_all | solution.py:111
  119.0 1.5 copy.51
  120.5 0.0 all-gather.2.cloned.1.call-done
  120.5 8.5 %shard_map.63 = bf16[64,384]{1,0:T(8,128)(2,1)} custom-call(s32[1]{0:T(128)} %bitcast.12.refs_0_, bf16[1,256,1536]{2,1,0:T(8,128)(2,1)} %copy-done, bf16[1,256,1536]{2,1,0:T(8,128)(2,1)} %copy-done.3, bf16[1,256,1536]{2,1,0:T(8,128)(2,1)} %copy-done.1, bf16[1,256,1536]{2,1,0:T(8,128)(2,1)} %copy-done.2, bf16[1,64,1536]{2,1,0:T(8,128)(2,1)} %copy-done.4, ...), custom_call_target="tpu_custom_call" | custom-call | flops 1811939328 | bytes 13369344 | tf_op jit(solution)/shard_map/pallas_call | solution.py:89
  129.1 20.1 %all_gather.11 = bf16[1024,384]{1,0:T(8,128)(2,1)S(1)} all-gather(bf16[64,384]{1,0:T(8,128)(2,1)} %shard_map.63), channel_id=1, replica_groups=mesh['yl'=4,'z'=8,'c'=2,'x'=4,'yh'=2] {'z','c'}, dimensions={0}, use_global_device_ids=true | all-gather | bytes 835584 | tf_op jit(solution)/shard_map/all_gather | solution.py:156
  149.1 0.6 convolution_convert_fusion
  149.7 11.5 %all_to_all.20 = bf16[4,96,384]{2,1,0:T(8,128)(2,1)S(1)} all-to-all(bf16[4,96,384]{2,1,0:T(8,128)(2,1)S(1)} %bitcast.39), channel_id=1, replica_groups=mesh['yl'=4,'z'=8,'c'=2,'x'=4,'yh'=2] {'yl'}, dimensions={0} | all-to-all | bytes 589824 | tf_op jit(solution)/shard_map/all_to_all | solution.py:158
  161.2 0.7 convert_reduce_fusion.1
  (19 shorter events, 0.1 us)
Async XLA Ops:
  7.2 17.3 %copy-start.8 = (bf16[1,256,768]{2,1,0:T(8,128)(2,1)S(1)}, bf16[1,256,768]{2,1,0:T(8,128)(2,1)}, u32[]{:S(2)}) copy-start(bf16[1,256,768]{2,1,0:T(8,128)(2,1)} %param.4) | copy-start | bytes 1179652
  7.2 30.1 %copy-start.9 = (s32[1,64]{1,0:T(1,128)S(1)}, s32[1,64]{1,0:T(1,128)}, u32[]{:S(2)}) copy-start(s32[1,64]{1,0:T(1,128)} %param.5) | copy-start | bytes 772
  7.2 113.3 %all-gather.2.cloned.1.call-start = ((), (), s32[]{:S(2)}) async-start(), calls=%async_computation.4 | async-start | bytes 10027008 | tf_op jit(solution)/shard_map/all_gather | solution.py:125
  24.5 27.2 %collective-permute-start = (bf16[256,768]{1,0:T(8,128)(2,1)S(1)}, bf16[256,768]{1,0:T(8,128)(2,1)S(1)}, u32[]{:S(2)}, u32[]{:S(2)}) collective-permute-start(bf16[256,768]{1,0:T(8,128)(2,1)S(1)} %bitcast.33), channel_id=1, source_target_pairs={{0,1},{1,0},{2,3},{3,2},{4,5},{5,4},{6,7},{7,6},{8,9},{9,8},{10,11... | collective-permute-start | bytes 1179656 | tf_op jit(solution)/shard_map/ppermute | solution.py:124
  31.6 19.7 %all-to-all-start = ((f32[8,2,256]{2,1,0:T(2,128)}), f32[8,2,256]{2,1,0:T(2,128)S(1)}, u32[]{:S(2)}, u32[]{:S(2)}) async-start(f32[8,2,256]{2,1,0:T(2,128)} %broadcast_in_dim.10), calls=%async_computation | async-start | bytes 32768 | tf_op jit(solution)/shard_map/all_to_all | solution.py:111
  52.3 0.9 copy-start
  53.2 29.6 %copy-start.4 = (bf16[1,64,1536]{2,1,0:T(8,128)(2,1)}, bf16[1,64,1536]{2,1,0:T(8,128)(2,1)S(1)}, u32[]{:S(2)}) copy-start(bf16[1,64,1536]{2,1,0:T(8,128)(2,1)S(1)} %get-tuple-element.13.refs_5_) | copy-start | bytes 589828
  54.2 27.3 %all-to-all-start.1 = ((bf16[16,64,96]{2,1,0:T(8,128)(2,1)}), bf16[16,64,96]{2,1,0:T(8,128)(2,1)S(1)}, u32[]{:S(2)}, u32[]{:S(2)}) async-start(bf16[16,64,96]{2,1,0:T(8,128)(2,1)} %bitcast.28), calls=%async_computation.1 | async-start | bytes 524288 | tf_op jit(solution)/shard_map/all_to_all | solution.py:147
  68.1 22.7 %collective-permute-start.2 = (bf16[256,1536]{1,0:T(8,128)(2,1)}, bf16[256,1536]{1,0:T(8,128)(2,1)S(1)}, u32[]{:S(2)}, u32[]{:S(2)}) collective-permute-start(bf16[256,1536]{1,0:T(8,128)(2,1)} %maximum_select_fusion.1), channel_id=1, source_target_pairs={{0,4},{2,6},{4,0},{6,2},{1,5},{3,7},{5,1},{7,3},{8,12},{10,14},{12... | collective-permute-start | bytes 2359304 | tf_op jit(solution)/shard_map/ppermute | solution.py:132
  71.0 35.2 %collective-permute-start.3 = (bf16[256,1536]{1,0:T(8,128)(2,1)}, bf16[256,1536]{1,0:T(8,128)(2,1)S(1)}, u32[]{:S(2)}, u32[]{:S(2)}) collective-permute-start(bf16[256,1536]{1,0:T(8,128)(2,1)} %maximum_select_fusion.1), channel_id=1, source_target_pairs={{0,6},{2,0},{4,2},{6,4},{1,7},{3,1},{5,3},{7,5},{8,14},{10,8},{12,... | collective-permute-start | bytes 2359304 | tf_op jit(solution)/shard_map/ppermute | solution.py:132
  74.6 33.5 %collective-permute-start.1 = (bf16[256,1536]{1,0:T(8,128)(2,1)}, bf16[256,1536]{1,0:T(8,128)(2,1)S(1)}, u32[]{:S(2)}, u32[]{:S(2)}) collective-permute-start(bf16[256,1536]{1,0:T(8,128)(2,1)} %maximum_select_fusion.1), channel_id=1, source_target_pairs={{0,2},{2,4},{4,6},{6,0},{1,3},{3,5},{5,7},{7,1},{8,10},{10,12},{12... | collective-permute-start | bytes 2359304 | tf_op jit(solution)/shard_map/ppermute | solution.py:132
  82.8 36.2 %all-to-all-start.2 = ((bf16[4,16,64,96]{3,2,1,0:T(8,128)(2,1)}), bf16[4,16,64,96]{3,2,1,0:T(8,128)(2,1)}, u32[]{:S(2)}, u32[]{:S(2)}) async-start(bf16[4,16,64,96]{3,2,1,0:T(8,128)(2,1)} %broadcast_in_dim.11), calls=%async_computation.2 | async-start | bytes 2097152 | tf_op jit(solution)/shard_map/all_to_all | solution.py:111
  91.3 0.7 copy-start.5
  92.0 16.2 %copy-start.1 = (bf16[1,256,1536]{2,1,0:T(8,128)(2,1)}, bf16[1,256,1536]{2,1,0:T(8,128)(2,1)S(1)}, u32[]{:S(2)}) copy-start(bf16[1,256,1536]{2,1,0:T(8,128)(2,1)S(1)} %get-tuple-element.16.refs_3_) | copy-start | bytes 2359300
  106.6 0.9 copy-start.2
  107.5 0.7 copy-start.6
  108.6 0.9 copy-start.3
  109.5 0.7 copy-start.7
Sparse Core Ops, SparseCore 0:
  24.6 77.6 all-gather.1

commit v3 on v2

v3 whole, which is shorter than its diff:
```python
import math

import jax
import jax.numpy as jnp
from jax import lax
from jax.experimental import pallas as pl
from jax.experimental.pallas import tpu as pltpu
from jax.sharding import Mesh
from jax.sharding import PartitionSpec as P

D = 6144
Y, Z, C, X, H = 4, 8, 2, 4, 2
BF, F32 = jnp.bfloat16, jnp.float32
MB = 1024 * 1024


def normalise_kernel(image_ref, centre_ref, scale_ref, select_ref, normed_ref):
    patches = image_ref.shape[0]
    normed = ((image_ref[...].astype(F32) - centre_ref[...]) * scale_ref[...]).astype(BF)
    normed_ref[:patches] = normed
    normed_ref[patches:] = jnp.dot(select_ref[...], normed, preferred_element_type=F32).astype(BF)


def normalise(chunk, centre, scale, select):
    patches, width = chunk.shape
    keep = select.shape[0]
    return pl.pallas_call(
        normalise_kernel,
        out_shape=jax.ShapeDtypeStruct((patches + keep, width), BF),
        compiler_params=pltpu.CompilerParams(vmem_limit_bytes=16 * MB),
        cost_estimate=pl.CostEstimate(
            flops=2 * keep * patches * width, bytes_accessed=2 * width * (2 * patches + keep), transcendentals=0
        ),
    )(chunk, centre, scale, select)


def error_kernel(factor, patches, where_ref, *refs):
    n = pl.num_programs(0)
    normed_refs, block_refs = refs[:Y], refs[Y:-4]
    error_ref, panel_ref, teacher_acc, student_acc = refs[-4:]
    step = pl.program_id(0)
    columns = error_ref.shape[1]
    z, c = where_ref[1], where_ref[2]
    for ref, offsets, core in block_refs_of(block_refs, c):
        for slot, offset in enumerate(offsets):
            panel_ref[lax.rem(z + Z + offset, Z) * C + core] = ref[slot, 0]
    panel = panel_ref[...].reshape(-1, 2 * columns)
    for k in range(Y):

        @pl.when(step == k)
        def _(k=k):
            teacher = jnp.dot(normed_refs[k][...], panel[:, :columns], preferred_element_type=F32)
            student = jnp.dot(normed_refs[k][patches:], panel[:, columns:], preferred_element_type=F32)
            teacher_acc[...] = teacher if k == 0 else teacher_acc[...] + teacher
            student_acc[...] = student if k == 0 else student_acc[...] + student

    @pl.when(step == n - 1)
    def _():
        teacher = teacher_acc[:patches]
        centre = jnp.mean(teacher, axis=0, keepdims=True)
        centred = teacher - centre
        spread = jnp.mean(centred * centred, axis=0, keepdims=True)
        target = (teacher_acc[patches:] - centre) * lax.rsqrt(spread + 1e-05)
        error_ref[...] = ((student_acc[...] - target) * factor).astype(BF)


NEAR, FAR = (0, -1, 1), (-2, 2, -3, 3, 4)


def block_refs_of(refs, c):
    return zip(refs, (NEAR, NEAR, FAR, FAR), (c, 1 - c, c, 1 - c))


def make_error(normed, patches, where, blocks, factor):
    n = len(normed)
    rows_in, width = normed[0].shape
    keep = rows_in - patches
    rows, both = blocks[0].shape[2:]
    columns = both // 2

    def body(*refs):
        error_kernel(factor, patches, *refs)

    return pl.pallas_call(
        body,
        grid_spec=pltpu.PrefetchScalarGridSpec(
            num_scalar_prefetch=1,
            grid=(n,),
            in_specs=[pl.BlockSpec((rows_in, width), lambda k, where: (0, 0))] * n
            + [
                pl.BlockSpec((len(b), 1, rows, both), lambda k, where: (0, lax.rem(where[0] + n - k, n), 0, 0))
                for b in blocks
            ],
            out_specs=pl.BlockSpec((keep, columns), lambda k, where: (0, 0)),
            scratch_shapes=[
                pltpu.VMEM((Z * C, rows, both), BF),
                pltpu.VMEM((rows_in, columns), F32),
                pltpu.VMEM((keep, columns), F32),
            ],
        ),
        out_shape=jax.ShapeDtypeStruct((keep, columns), BF),
        compiler_params=pltpu.CompilerParams(vmem_limit_bytes=40 * MB),
        cost_estimate=pl.CostEstimate(
            flops=2 * n * width * (rows_in + keep) * columns,
            bytes_accessed=2 * n * width * (rows_in + both),
            transcendentals=columns,
        ),
    )(where, *normed, *blocks)


def ring(size, step):
    return [(i, (i + step) % size) for i in range(size)]


def both_ways(up, down):
    return lax.ppermute(up, "z", ring(Z, 1)), lax.ppermute(down, "z", ring(Z, -1))


def spread_to_all(values, axes, size):
    return lax.all_to_all(jnp.broadcast_to(values[None], (size, *values.shape)), axes, split_axis=0, concat_axis=0)


def shards(images, keep_index, teacher_weight, student_weight):
    patches, slice_width = images.shape[1:]
    keep_count = keep_index.shape[1]
    rows, columns = teacher_weight.shape
    image = images[0]

    teacher_next = 0.999 * teacher_weight + (1.0 - 0.999) * student_weight
    panel = jnp.concatenate([teacher_next, student_weight], axis=1).astype(BF)
    panels = lax.all_gather(panel, "yl", axis=0, tiled=True)
    panels, image = lax.optimization_barrier((panels, image))
    own = panels.reshape(Y, rows, 2 * columns)
    up1, down1 = both_ways(own, own)
    other = lax.ppermute(image, "yh", ring(H, 1))
    up1, down1, other = lax.optimization_barrier((up1, down1, other))
    near = jnp.stack([own, up1, down1])
    near_other = lax.ppermute(near, "c", ring(C, 1))
    up2, down2 = both_ways(up1, down1)

    pair = jnp.where(
        lax.axis_index("yh") == 0,
        jnp.concatenate([image, other], axis=1),
        jnp.concatenate([other, image], axis=1),
    )
    arrived = [lax.ppermute(pair, "x", ring(X, step)) for step in range(1, X)]

    floats = image.astype(F32)
    own_mean = jnp.mean(floats, axis=1)
    own_moment = jnp.sum(jnp.square(floats - own_mean[:, None]), axis=1)
    parts = spread_to_all(jnp.stack([own_mean, own_moment]), ("x", "yh"), X * H)
    up2, down2, parts, pair, near_other = lax.optimization_barrier((up2, down2, parts, pair, near_other))
    up3, down3 = both_ways(up2, down2)
    centre = jnp.mean(parts[:, 0], axis=0)
    moment = jnp.sum(parts[:, 1], axis=0) + slice_width * jnp.sum(jnp.square(parts[:, 0] - centre), axis=0)
    scale = lax.rsqrt(moment / D + 1e-06)
    centre, scale = centre[:, None], scale[:, None]

    select = (keep_index[0][:, None] == lax.broadcasted_iota(jnp.int32, (keep_count, patches), 1)).astype(BF)

    normed = [normalise(pair, centre, scale, select)]
    pieces = normed[0][patches:].reshape(keep_count, Z * C, rows).transpose(1, 0, 2)
    pieces = lax.all_to_all(pieces, ("z", "c"), split_axis=0, concat_axis=0)
    up3, down3, pieces, arrived = lax.optimization_barrier((up3, down3, pieces, arrived))
    last_up, last_down = both_ways(up3[..., :columns], down3[..., columns:])
    far = jnp.stack([up2, down2, up3, down3, jnp.concatenate([last_up, last_down], axis=-1)])
    owned = spread_to_all(pieces, "x", X)
    owned = owned.reshape(Y, Z * C * keep_count, rows).transpose(0, 2, 1).reshape(Y * rows, Z * C * keep_count)

    normed += [normalise(chunk, centre, scale, select) for chunk in arrived]
    blocks = near, near_other, far, lax.ppermute(far, "c", ring(C, 1))
    where = jnp.stack([lax.axis_index("x"), lax.axis_index("z"), lax.axis_index("c")])
    total_kept = keep_count * Y * Z * C
    error = make_error(normed, patches, where, blocks, 1.0 / math.sqrt(total_kept))
    errors = lax.all_gather(error, ("z", "c"), axis=0, tiled=True)
    partial = jnp.dot(owned, errors, preferred_element_type=F32).astype(BF).reshape(Y, rows, columns)
    partial = lax.all_to_all(partial, "yl", split_axis=0, concat_axis=0)
    student_grad = jnp.sum(partial.astype(F32), axis=0)
    return (teacher_next, student_grad)


def solution(mesh):
    fine = Mesh(mesh.devices.reshape(Y, Z, C, X, H), ("yl", "z", "c", "x", "yh"))
    rows, cols = ("yl", "z", "c"), ("x", "yh")
    return jax.shard_map(
        shards,
        mesh=fine,
        in_specs=(P(rows, None, cols), P(rows, None), P(rows, cols), P(rows, cols)),
        out_specs=(P(rows, cols), P(rows, cols)),
        check_vma=False,
    )
```

time: 169 us -> 210 us (1.24)
  starting transfers between devices: 37.4 us -> 79.7 us
  local copies, waits for them, and re-layouts: 9.29 us -> 25.7 us
  between operations: 14.2 us -> 0.97 us
  waiting for transfers between devices: 45.8 us -> 32.7 us
  other arithmetic: 4.27 us -> 9.19 us
  Pallas kernels: 10.3 us -> 13 us
    ppermute x4 -> x14, starting transfers between devices: 14.5 us -> 61.6 us  [the longest x4 22.3 us: both_ways(): lax.ppermute(down, 'z', ring(Z, -1))]
    all_to_all x2, waiting for transfers between devices: 22.8 us -> 7.63 us  [spread_to_all(): lax.all_to_all(jnp.broadcast_to(values[None], (size, *values.shape)), axe...]
    unnamed x20 -> x30, local copies, waits for them, and re-layouts: 4.69 us -> 18.3 us
    ppermute x4 -> x14, waiting for transfers between devices: 17.9 us -> 25.1 us  [the longest x1 15.7 us: shards(): other = lax.ppermute(image, 'yh', ring(H, 1))]
    all_to_all x1, starting transfers between devices: 12.8 us -> 6.73 us  [shards(): pieces = lax.all_to_all(pieces, ('z', 'c'), split_axis=0, concat_axis=0)]
    all_to_all x1, waiting for transfers between devices: 5 us -> 0.01 us  [shards(): pieces = lax.all_to_all(pieces, ('z', 'c'), split_axis=0, concat_axis=0)]
    pallas_call x4, Pallas kernels: 1.74 us -> 6.23 us  [normalise(): pl.pallas_call(normalise_kernel, out_shape=jax.ShapeDtypeStruct((patches...]
    another operation x1 -> x4, other arithmetic: 1.79 us -> 4.17 us
  transfers between devices with their start and end apart: 8 -> 17, of which waited for: 5 -> 3; matrix products, arithmetic and copies ran while one was open for 4% -> 9% of each run, Pallas kernels for 1% -> 3%
where the time goes in v3:
time: 210 us; the launch traced here: 208 us
  starting transfers between devices  79.7 us (38%)
  blocking collectives  46.2 us (22%)
  waiting for transfers between devices  32.7 us (16%)
  local copies, waits for them, and re-layouts  25.7 us (12%)
  Pallas kernels  13 us (6%)
  other arithmetic  9.19 us (4%)
    ppermute x4, starting transfers between devices, both_ways(): lax.ppermute(down, 'z', ring(Z, -1))  22.3 us
    all_gather x1, blocking collectives, shards(): errors = lax.all_gather(error, ('z', 'c'), axis=0, tiled=True)  20.6 us
    unnamed x30, local copies, waits for them, and re-layouts  18.3 us
    ppermute x1, waiting for transfers between devices, shards(): other = lax.ppermute(image, 'yh', ring(H, 1))  15.7 us
    all_gather x1, blocking collectives, shards(): panels = lax.all_gather(panel, 'yl', axis=0, tiled=True)  14.6 us
    all_to_all x2, starting transfers between devices, spread_to_all(): lax.all_to_all(jnp.broadcast_to(values[None], (size, *values.shape)), axe...  11.3 us
    all_to_all x1, blocking collectives, shards(): partial = lax.all_to_all(partial, 'yl', split_axis=0, concat_axis=0)  11 us
    ppermute x4, starting transfers between devices, both_ways(): lax.ppermute(up, 'z', ring(Z, 1))  10.9 us
  transfers between devices with their start and end apart: 17, of which 3 were waited for; matrix products, arithmetic and copies ran while one was open for 9% of the time, Pallas kernels for 3%

profile of v3, /device:TPU:1, one launch (start us, length us, event | category | flops | bytes accessed | tf_op | source)
XLA Modules:
  0.0 208.0 jit_solution(3277937915943770662)
XLA Ops:
  0.6 1.8 fusion.6
  2.5 14.6 %all_gather.6 = bf16[384,768]{1,0:T(8,128)(2,1)S(1)} all-gather(bf16[96,768]{1,0:T(8,128)(2,1)S(1)} %pad_maximum_fusion.1), channel_id=1, replica_groups=mesh['yl'=4,'z'=8,'c'=2,'x'=4,'yh'=2] {'yl'}, dimensions={0}, use_global_device_ids=true | all-gather | bytes 737280 | tf_op jit(solution)/shard_map/all_gather | solution.py:131
  17.0 5.2 %collective-permute-start = (bf16[4,96,768]{2,1,0:T(8,128)(2,1)S(1)}, bf16[4,96,768]{2,1,0:T(8,128)(2,1)}, u32[]{:S(2)}, u32[]{:S(2)}) collective-permute-start(bf16[4,96,768]{2,1,0:T(8,128)(2,1)S(1)} %bitcast.45), channel_id=1, source_target_pairs={{0,16},{16,32},{32,48},{48,64},{64,80},{80,96},{96,112},{112,0},{1... | collective-permute-start | bytes 1769480 | tf_op jit(solution)/shard_map/ppermute | solution.py:116
  22.2 8.6 %collective-permute-start.1 = (bf16[4,96,768]{2,1,0:T(8,128)(2,1)S(1)}, bf16[4,96,768]{2,1,0:T(8,128)(2,1)}, u32[]{:S(2)}, u32[]{:S(2)}) collective-permute-start(bf16[4,96,768]{2,1,0:T(8,128)(2,1)S(1)} %bitcast.46), channel_id=1, source_target_pairs={{0,112},{16,0},{32,16},{48,32},{64,48},{80,64},{96,80},{112,96},{1... | collective-permute-start | bytes 1769480 | tf_op jit(solution)/shard_map/ppermute | solution.py:116
  30.8 5.1 %collective-permute-start.2 = (bf16[256,768]{1,0:T(8,128)(2,1)}, bf16[256,768]{1,0:T(8,128)(2,1)S(1)}, u32[]{:S(2)}, u32[]{:S(2)}) collective-permute-start(bf16[256,768]{1,0:T(8,128)(2,1)} %bitcast.41), channel_id=1, source_target_pairs={{0,1},{1,0},{2,3},{3,2},{4,5},{5,4},{6,7},{7,6},{8,9},{9,8},{10,11... | collective-permute-start | bytes 1179656 | tf_op jit(solution)/shard_map/ppermute | solution.py:135
  35.9 15.7 %collective-permute-done.2 = bf16[256,768]{1,0:T(8,128)(2,1)S(1)} collective-permute-done((bf16[256,768]{1,0:T(8,128)(2,1)}, bf16[256,768]{1,0:T(8,128)(2,1)S(1)}, u32[]{:S(2)}, u32[]{:S(2)}) %collective-permute-start.2) | collective-permute-done | bytes 393248 | tf_op jit(solution)/shard_map/ppermute | solution.py:135
  52.3 1.4 pad_maximum_fusion.refs_5_
  53.8 7.1 %collective-permute-start.5 = (bf16[3,4,96,768]{3,2,1,0:T(8,128)(2,1)S(1)}, bf16[3,4,96,768]{3,2,1,0:T(8,128)(2,1)S(1)}, u32[]{:S(2)}, u32[]{:S(2)}) collective-permute-start(bf16[3,4,96,768]{3,2,1,0:T(8,128)(2,1)S(1)} %pad_maximum_fusion.refs_5_), channel_id=1, source_target_pairs={{0,8},{8,0},{1,9},{9,1},{2,10},{10,2},{3,11},{11,3},{4,12},{12,4},... | collective-permute-start | bytes 5308424 | tf_op jit(solution)/shard_map/ppermute | solution.py:138
  61.0 1.9 collective-permute-start.3
  63.0 4.6 %collective-permute-start.4 = (bf16[4,96,768]{2,1,0:T(8,128)(2,1)}, bf16[4,96,768]{2,1,0:T(8,128)(2,1)}, u32[]{:S(2)}, u32[]{:S(2)}) collective-permute-start(bf16[4,96,768]{2,1,0:T(8,128)(2,1)} %collective-permute-done.1), channel_id=1, source_target_pairs={{0,112},{16,0},{32,16},{48,32},{64,48},{80,64},{96,80},{112,96},{1... | collective-permute-start | bytes 1769480 | tf_op jit(solution)/shard_map/ppermute | solution.py:116
  68.4 7.0 %all-to-all-start = ((f32[8,2,256]{2,1,0:T(2,128)}), f32[8,2,256]{2,1,0:T(2,128)S(1)}, u32[]{:S(2)}, u32[]{:S(2)}) async-start(f32[8,2,256]{2,1,0:T(2,128)} %broadcast_in_dim.4), calls=%async_computation | async-start | bytes 32768 | tf_op jit(solution)/shard_map/all_to_all | solution.py:120
  75.5 1.3 fusion.3.select_ref
  76.8 2.5 %maximum_select_fusion.image_ref = bf16[256,1536]{1,0:T(8,128)(2,1)} fusion(bf16[256,768]{1,0:T(8,128)(2,1)} %copy-done.12, bf16[256,768]{1,0:T(8,128)(2,1)} %bitcast.42, pred[]{:T(512)S(6)} %eq.13), kind=kLoop, calls=%fused_computation.6 | loop fusion | flops 3538944 | bytes 1572865 | tf_op jit(solution)/shard_map/jit(_where)/select_n | solution.py:141
  79.3 4.6 %collective-permute-start.10 = (bf16[256,1536]{1,0:T(8,128)(2,1)}, bf16[256,1536]{1,0:T(8,128)(2,1)}, u32[]{:S(2)}, u32[]{:S(2)}) collective-permute-start(bf16[256,1536]{1,0:T(8,128)(2,1)} %maximum_select_fusion.image_ref), channel_id=1, source_target_pairs={{0,6},{2,0},{4,2},{6,4},{1,7},{3,1},{5,3},{7,5},{8,14},{10,8},{12,... | collective-permute-start | bytes 2359304 | tf_op jit(solution)/shard_map/ppermute | solution.py:146
  83.9 1.9 collective-permute-start.8
  85.8 3.7 %collective-permute-start.9 = (bf16[256,1536]{1,0:T(8,128)(2,1)}, bf16[256,1536]{1,0:T(8,128)(2,1)}, u32[]{:S(2)}, u32[]{:S(2)}) collective-permute-start(bf16[256,1536]{1,0:T(8,128)(2,1)} %maximum_select_fusion.image_ref), channel_id=1, source_target_pairs={{0,4},{2,6},{4,0},{6,2},{1,5},{3,7},{5,1},{7,3},{8,12},{10,14},{12... | collective-permute-start | bytes 2359304 | tf_op jit(solution)/shard_map/ppermute | solution.py:146
  89.5 1.2 copy-done.6
  90.8 1.9 collective-permute-start.6
  92.7 4.6 %collective-permute-start.7 = (bf16[4,96,768]{2,1,0:T(8,128)(2,1)}, bf16[4,96,768]{2,1,0:T(8,128)(2,1)}, u32[]{:S(2)}, u32[]{:S(2)}) collective-permute-start(bf16[4,96,768]{2,1,0:T(8,128)(2,1)} %collective-permute-done.4), channel_id=1, source_target_pairs={{0,112},{16,0},{32,16},{48,32},{64,48},{80,64},{96,80},{112,96},{1... | collective-permute-start | bytes 1769480 | tf_op jit(solution)/shard_map/ppermute | solution.py:116
  98.4 1.6 shard_map.59.refs_1_
  101.0 6.7 %all-to-all-start.1 = ((bf16[16,64,96]{2,1,0:T(8,128)(2,1)}), bf16[16,64,96]{2,1,0:T(8,128)(2,1)S(1)}, u32[]{:S(2)}, u32[]{:S(2)}) async-start(bf16[16,64,96]{2,1,0:T(8,128)(2,1)} %bitcast.48), calls=%async_computation.1 | async-start | bytes 524288 | tf_op jit(solution)/shard_map/all_to_all | solution.py:163
  107.7 1.9 bitcast_dynamic-update-slice_fusion.3
  109.6 1.9 bitcast_dynamic-update-slice_fusion.2
  111.5 9.4 %collective-permute-done.9.image_ref = bf16[256,1536]{1,0:T(8,128)(2,1)} collective-permute-done((bf16[256,1536]{1,0:T(8,128)(2,1)}, bf16[256,1536]{1,0:T(8,128)(2,1)}, u32[]{:S(2)}, u32[]{:S(2)}) %collective-permute-start.9) | collective-permute-done | bytes 786464 | tf_op jit(solution)/shard_map/ppermute | solution.py:146
  120.9 1.0 slice.19
  121.9 1.9 collective-permute-start.11
  123.8 1.0 slice.20
  124.8 4.6 %collective-permute-start.12 = (bf16[4,96,384]{2,1,0:T(8,128)(2,1)S(1)}, bf16[4,96,384]{2,1,0:T(8,128)(2,1)S(1)}, u32[]{:S(2)}, u32[]{:S(2)}) collective-permute-start(bf16[4,96,384]{2,1,0:T(8,128)(2,1)S(1)} %slice.20), channel_id=1, source_target_pairs={{0,112},{16,0},{32,16},{48,32},{64,48},{80,64},{96,80},{112,96},{1... | collective-permute-start | bytes 884744 | tf_op jit(solution)/shard_map/ppermute | solution.py:116
  129.4 1.9 bitcast_dynamic-update-slice_fusion.1
  131.4 1.9 bitcast_dynamic-update-slice_fusion
  134.2 6.0 %collective-permute-start.13 = (bf16[5,4,96,768]{3,2,1,0:T(8,128)(2,1)}, bf16[5,4,96,768]{3,2,1,0:T(8,128)(2,1)}, u32[]{:S(2)}, u32[]{:S(2)}) collective-permute-start(bf16[5,4,96,768]{3,2,1,0:T(8,128)(2,1)} %fusion.2.refs_7_), channel_id=1, source_target_pairs={{0,8},{8,0},{1,9},{9,1},{2,10},{10,2},{3,11},{11,3},{4,12},{12,4},... | collective-permute-start | bytes 8847368 | tf_op jit(solution)/shard_map/ppermute | solution.py:171
  140.2 1.3 broadcast_in_dim.5
  141.5 4.2 %all-to-all-start.2 = ((bf16[4,16,64,96]{3,2,1,0:T(8,128)(2,1)}), bf16[4,16,64,96]{3,2,1,0:T(8,128)(2,1)}, u32[]{:S(2)}, u32[]{:S(2)}) async-start(bf16[4,16,64,96]{3,2,1,0:T(8,128)(2,1)} %broadcast_in_dim.5), calls=%async_computation.2 | async-start | bytes 2097152 | tf_op jit(solution)/shard_map/all_to_all | solution.py:120
  145.8 1.6 shard_map.62.refs_4_
  147.4 1.0 copy-done
  148.4 1.6 shard_map.61.refs_3_
  149.9 0.9 copy-done.2
  150.9 1.6 shard_map.60.refs_2_
  152.4 1.0 copy-done.4
  153.4 7.6 %all-to-all-done.2 = bf16[4,16,64,96]{3,2,1,0:T(8,128)(2,1)} async-done(((bf16[4,16,64,96]{3,2,1,0:T(8,128)(2,1)}), bf16[4,16,64,96]{3,2,1,0:T(8,128)(2,1)}, u32[]{:S(2)}, u32[]{:S(2)}) %all-to-all-start.2) | async-done | bytes 786464 | tf_op jit(solution)/shard_map/all_to_all | solution.py:120
  161.0 2.2 %copy.51 = bf16[4,96,1024]{2,1,0:T(8,128)(2,1)} copy(bf16[4,96,1024]{1,2,0:T(8,128)(2,1)} %bitcast.12) | data formatting | bytes 1572864 | tf_op jit(solution)/shard_map/transpose | solution.py:168
  163.2 1.2 copy-done.1
  164.5 1.2 copy-done.3
  165.7 1.2 copy-done.5
  166.9 1.5 copy-done.7
  168.3 6.8 %shard_map.63 = bf16[64,384]{1,0:T(8,128)(2,1)S(1)} custom-call(s32[3]{0:T(128)S(1)} %pad_add_fusion.refs_0_, bf16[320,1536]{1,0:T(8,128)(2,1)S(1)} %shard_map.59.refs_1_, bf16[320,1536]{1,0:T(8,128)(2,1)S(1)} %copy-done.5, bf16[320,1536]{1,0:T(8,128)(2,1)S(1)} %copy-done.3, bf16[320,1536]{1,0:T(8,128)(2,1)S(1)} %copy-done.1, ...), custom_call_target="tpu_custom_call" | custom-call | flops 1811939328 | bytes 13369344 | tf_op jit(solution)/shard_map/pallas_call | solution.py:84
  175.1 20.6 %all_gather.7 = bf16[1024,384]{1,0:T(8,128)(2,1)S(1)} all-gather(bf16[64,384]{1,0:T(8,128)(2,1)S(1)} %shard_map.63), channel_id=1, replica_groups=mesh['yl'=4,'z'=8,'c'=2,'x'=4,'yh'=2] {'z','c'}, dimensions={0}, use_global_device_ids=true | all-gather | bytes 835584 | tf_op jit(solution)/shard_map/all_gather | solution.py:175
  196.3 11.0 %all_to_all.20 = bf16[4,96,384]{2,1,0:T(8,128)(2,1)S(1)} all-to-all(bf16[4,96,384]{2,1,0:T(8,128)(2,1)S(1)} %bitcast.50), channel_id=1, replica_groups=mesh['yl'=4,'z'=8,'c'=2,'x'=4,'yh'=2] {'yl'}, dimensions={0} | all-to-all | bytes 589824 | tf_op jit(solution)/shard_map/all_to_all | solution.py:177
  (51 shorter events, 6.1 us)
Async XLA Ops:
  0.6 60.3 %copy-start.10 = (bf16[1,256,768]{2,1,0:T(8,128)(2,1)S(1)}, bf16[1,256,768]{2,1,0:T(8,128)(2,1)}, u32[]{:S(2)}) copy-start(bf16[1,256,768]{2,1,0:T(8,128)(2,1)} %param.4) | copy-start | bytes 1179652
  17.0 34.6 %collective-permute-start = (bf16[4,96,768]{2,1,0:T(8,128)(2,1)S(1)}, bf16[4,96,768]{2,1,0:T(8,128)(2,1)}, u32[]{:S(2)}, u32[]{:S(2)}) collective-permute-start(bf16[4,96,768]{2,1,0:T(8,128)(2,1)S(1)} %bitcast.45), channel_id=1, source_target_pairs={{0,16},{16,32},{32,48},{48,64},{64,80},{80,96},{96,112},{112,0},{1... | collective-permute-start | bytes 1769480 | tf_op jit(solution)/shard_map/ppermute | solution.py:116
  22.2 29.4 %collective-permute-start.1 = (bf16[4,96,768]{2,1,0:T(8,128)(2,1)S(1)}, bf16[4,96,768]{2,1,0:T(8,128)(2,1)}, u32[]{:S(2)}, u32[]{:S(2)}) collective-permute-start(bf16[4,96,768]{2,1,0:T(8,128)(2,1)S(1)} %bitcast.46), channel_id=1, source_target_pairs={{0,112},{16,0},{32,16},{48,32},{64,48},{80,64},{96,80},{112,96},{1... | collective-permute-start | bytes 1769480 | tf_op jit(solution)/shard_map/ppermute | solution.py:116
  30.8 20.8 %collective-permute-start.2 = (bf16[256,768]{1,0:T(8,128)(2,1)}, bf16[256,768]{1,0:T(8,128)(2,1)S(1)}, u32[]{:S(2)}, u32[]{:S(2)}) collective-permute-start(bf16[256,768]{1,0:T(8,128)(2,1)} %bitcast.41), channel_id=1, source_target_pairs={{0,1},{1,0},{2,3},{3,2},{4,5},{5,4},{6,7},{7,6},{8,9},{9,8},{10,11... | collective-permute-start | bytes 1179656 | tf_op jit(solution)/shard_map/ppermute | solution.py:135
  51.6 0.7 copy-start.12
  53.8 35.7 %collective-permute-start.5 = (bf16[3,4,96,768]{3,2,1,0:T(8,128)(2,1)S(1)}, bf16[3,4,96,768]{3,2,1,0:T(8,128)(2,1)S(1)}, u32[]{:S(2)}, u32[]{:S(2)}) collective-permute-start(bf16[3,4,96,768]{3,2,1,0:T(8,128)(2,1)S(1)} %pad_maximum_fusion.refs_5_), channel_id=1, source_target_pairs={{0,8},{8,0},{1,9},{9,1},{2,10},{10,2},{3,11},{11,3},{4,12},{12,4},... | collective-permute-start | bytes 5308424 | tf_op jit(solution)/shard_map/ppermute | solution.py:138
  61.0 24.8 %collective-permute-start.3 = (bf16[4,96,768]{2,1,0:T(8,128)(2,1)}, bf16[4,96,768]{2,1,0:T(8,128)(2,1)}, u32[]{:S(2)}, u32[]{:S(2)}) collective-permute-start(bf16[4,96,768]{2,1,0:T(8,128)(2,1)} %collective-permute-done), channel_id=1, source_target_pairs={{0,16},{16,32},{32,48},{48,64},{64,80},{80,96},{96,112},{112,0},{1... | collective-permute-start | bytes 1769480 | tf_op jit(solution)/shard_map/ppermute | solution.py:116
  63.0 26.5 %collective-permute-start.4 = (bf16[4,96,768]{2,1,0:T(8,128)(2,1)}, bf16[4,96,768]{2,1,0:T(8,128)(2,1)}, u32[]{:S(2)}, u32[]{:S(2)}) collective-permute-start(bf16[4,96,768]{2,1,0:T(8,128)(2,1)} %collective-permute-done.1), channel_id=1, source_target_pairs={{0,112},{16,0},{32,16},{48,32},{64,48},{80,64},{96,80},{112,96},{1... | collective-permute-start | bytes 1769480 | tf_op jit(solution)/shard_map/ppermute | solution.py:116
  68.4 21.1 %all-to-all-start = ((f32[8,2,256]{2,1,0:T(2,128)}), f32[8,2,256]{2,1,0:T(2,128)S(1)}, u32[]{:S(2)}, u32[]{:S(2)}) async-start(f32[8,2,256]{2,1,0:T(2,128)} %broadcast_in_dim.4), calls=%async_computation | async-start | bytes 32768 | tf_op jit(solution)/shard_map/all_to_all | solution.py:120
  79.3 32.2 %collective-permute-start.10 = (bf16[256,1536]{1,0:T(8,128)(2,1)}, bf16[256,1536]{1,0:T(8,128)(2,1)}, u32[]{:S(2)}, u32[]{:S(2)}) collective-permute-start(bf16[256,1536]{1,0:T(8,128)(2,1)} %maximum_select_fusion.image_ref), channel_id=1, source_target_pairs={{0,6},{2,0},{4,2},{6,4},{1,7},{3,1},{5,3},{7,5},{8,14},{10,8},{12,... | collective-permute-start | bytes 2359304 | tf_op jit(solution)/shard_map/ppermute | solution.py:146
  83.9 27.6 %collective-permute-start.8 = (bf16[256,1536]{1,0:T(8,128)(2,1)}, bf16[256,1536]{1,0:T(8,128)(2,1)}, u32[]{:S(2)}, u32[]{:S(2)}) collective-permute-start(bf16[256,1536]{1,0:T(8,128)(2,1)} %maximum_select_fusion.image_ref), channel_id=1, source_target_pairs={{0,2},{2,4},{4,6},{6,0},{1,3},{3,5},{5,7},{7,1},{8,10},{10,12},{12... | collective-permute-start | bytes 2359304 | tf_op jit(solution)/shard_map/ppermute | solution.py:146
  85.8 35.1 %collective-permute-start.9 = (bf16[256,1536]{1,0:T(8,128)(2,1)}, bf16[256,1536]{1,0:T(8,128)(2,1)}, u32[]{:S(2)}, u32[]{:S(2)}) collective-permute-start(bf16[256,1536]{1,0:T(8,128)(2,1)} %maximum_select_fusion.image_ref), channel_id=1, source_target_pairs={{0,4},{2,6},{4,0},{6,2},{1,5},{3,7},{5,1},{7,3},{8,12},{10,14},{12... | collective-permute-start | bytes 2359304 | tf_op jit(solution)/shard_map/ppermute | solution.py:146
  89.5 1.2 copy-start.6
  90.8 30.1 %collective-permute-start.6 = (bf16[4,96,768]{2,1,0:T(8,128)(2,1)}, bf16[4,96,768]{2,1,0:T(8,128)(2,1)}, u32[]{:S(2)}, u32[]{:S(2)}) collective-permute-start(bf16[4,96,768]{2,1,0:T(8,128)(2,1)} %collective-permute-done.3), channel_id=1, source_target_pairs={{0,16},{16,32},{32,48},{48,64},{64,80},{80,96},{96,112},{112,0},{1... | collective-permute-start | bytes 1769480 | tf_op jit(solution)/shard_map/ppermute | solution.py:116
  92.7 28.2 %collective-permute-start.7 = (bf16[4,96,768]{2,1,0:T(8,128)(2,1)}, bf16[4,96,768]{2,1,0:T(8,128)(2,1)}, u32[]{:S(2)}, u32[]{:S(2)}) collective-permute-start(bf16[4,96,768]{2,1,0:T(8,128)(2,1)} %collective-permute-done.4), channel_id=1, source_target_pairs={{0,112},{16,0},{32,16},{48,32},{64,48},{80,64},{96,80},{112,96},{1... | collective-permute-start | bytes 1769480 | tf_op jit(solution)/shard_map/ppermute | solution.py:116
  97.6 0.8 copy-start.8
  101.0 19.9 %all-to-all-start.1 = ((bf16[16,64,96]{2,1,0:T(8,128)(2,1)}), bf16[16,64,96]{2,1,0:T(8,128)(2,1)S(1)}, u32[]{:S(2)}, u32[]{:S(2)}) async-start(bf16[16,64,96]{2,1,0:T(8,128)(2,1)} %bitcast.48), calls=%async_computation.1 | async-start | bytes 524288 | tf_op jit(solution)/shard_map/all_to_all | solution.py:163
  121.9 11.4 %collective-permute-start.11 = (bf16[4,96,384]{2,1,0:T(8,128)(2,1)S(1)}, bf16[4,96,384]{2,1,0:T(8,128)(2,1)S(1)}, u32[]{:S(2)}, u32[]{:S(2)}) collective-permute-start(bf16[4,96,384]{2,1,0:T(8,128)(2,1)S(1)} %slice.19), channel_id=1, source_target_pairs={{0,16},{16,32},{32,48},{48,64},{64,80},{80,96},{96,112},{112,0},{1... | collective-permute-start | bytes 884744 | tf_op jit(solution)/shard_map/ppermute | solution.py:116
  124.8 8.4 %collective-permute-start.12 = (bf16[4,96,384]{2,1,0:T(8,128)(2,1)S(1)}, bf16[4,96,384]{2,1,0:T(8,128)(2,1)S(1)}, u32[]{:S(2)}, u32[]{:S(2)}) collective-permute-start(bf16[4,96,384]{2,1,0:T(8,128)(2,1)S(1)} %slice.20), channel_id=1, source_target_pairs={{0,112},{16,0},{32,16},{48,32},{64,48},{80,64},{96,80},{112,96},{1... | collective-permute-start | bytes 884744 | tf_op jit(solution)/shard_map/ppermute | solution.py:116
  131.4 14.5 %copy-start.9 = (bf16[64,256]{1,0:T(8,128)(2,1)S(1)}, bf16[64,256]{1,0:T(8,128)(2,1)}, u32[]{:S(2)}) copy-start(bf16[64,256]{1,0:T(8,128)(2,1)} %fusion.3.select_ref) | copy-start | bytes 98308
  134.2 29.1 %collective-permute-start.13 = (bf16[5,4,96,768]{3,2,1,0:T(8,128)(2,1)}, bf16[5,4,96,768]{3,2,1,0:T(8,128)(2,1)}, u32[]{:S(2)}, u32[]{:S(2)}) collective-permute-start(bf16[5,4,96,768]{3,2,1,0:T(8,128)(2,1)} %fusion.2.refs_7_), channel_id=1, source_target_pairs={{0,8},{8,0},{1,9},{9,1},{2,10},{10,2},{3,11},{11,3},{4,12},{12,4},... | collective-permute-start | bytes 8847368 | tf_op jit(solution)/shard_map/ppermute | solution.py:171
  141.5 19.6 %all-to-all-start.2 = ((bf16[4,16,64,96]{3,2,1,0:T(8,128)(2,1)}), bf16[4,16,64,96]{3,2,1,0:T(8,128)(2,1)}, u32[]{:S(2)}, u32[]{:S(2)}) async-start(bf16[4,16,64,96]{3,2,1,0:T(8,128)(2,1)} %broadcast_in_dim.5), calls=%async_computation.2 | async-start | bytes 2097152 | tf_op jit(solution)/shard_map/all_to_all | solution.py:120
  147.4 1.0 copy-start
  149.9 1.0 copy-start.2
  152.4 1.0 copy-start.4
  163.2 1.2 copy-start.1
  164.4 1.2 copy-start.3
  165.7 1.2 copy-start.5
  166.9 1.5 copy-start.7
  168.3 27.4 %copy-start.11 = (bf16[4,96,1024]{2,1,0:T(8,128)(2,1)S(1)}, bf16[4,96,1024]{2,1,0:T(8,128)(2,1)}, u32[]{:S(2)}) copy-start(bf16[4,96,1024]{2,1,0:T(8,128)(2,1)} %copy.51) | copy-start | bytes 2359300

commit v4 on v3

--- a/solution.py
+++ b/solution.py
@@ -34,17 +34,13 @@
     )(chunk, centre, scale, select)
 
 
-def error_kernel(factor, patches, where_ref, *refs):
+def error_kernel(factor, patches, x_ref, *refs):
     n = pl.num_programs(0)
-    normed_refs, block_refs = refs[:Y], refs[Y:-4]
-    error_ref, panel_ref, teacher_acc, student_acc = refs[-4:]
+    normed_refs = refs[:Y]
+    panel_ref, error_ref, teacher_acc, student_acc = refs[Y:]
     step = pl.program_id(0)
     columns = error_ref.shape[1]
-    z, c = where_ref[1], where_ref[2]
-    for ref, offsets, core in block_refs_of(block_refs, c):
-        for slot, offset in enumerate(offsets):
-            panel_ref[lax.rem(z + Z + offset, Z) * C + core] = ref[slot, 0]
-    panel = panel_ref[...].reshape(-1, 2 * columns)
+    panel = panel_ref[:, 0].reshape(-1, 2 * columns)
     for k in range(Y):
 
         @pl.when(step == k)
@@ -64,18 +60,11 @@
         error_ref[...] = ((student_acc[...] - target) * factor).astype(BF)
 
 
-NEAR, FAR = (0, -1, 1), (-2, 2, -3, 3, 4)
-
-
-def block_refs_of(refs, c):
-    return zip(refs, (NEAR, NEAR, FAR, FAR), (c, 1 - c, c, 1 - c))
-
-
-def make_error(normed, patches, where, blocks, factor):
+def make_error(normed, patches, x, panels, factor):
     n = len(normed)
     rows_in, width = normed[0].shape
     keep = rows_in - patches
-    rows, both = blocks[0].shape[2:]
+    blocks, _, rows, both = panels.shape
     columns = both // 2
 
     def body(*refs):
@@ -86,34 +75,23 @@
         grid_spec=pltpu.PrefetchScalarGridSpec(
             num_scalar_prefetch=1,
             grid=(n,),
-            in_specs=[pl.BlockSpec((rows_in, width), lambda k, where: (0, 0))] * n
-            + [
-                pl.BlockSpec((len(b), 1, rows, both), lambda k, where: (0, lax.rem(where[0] + n - k, n), 0, 0))
-                for b in blocks
-            ],
-            out_specs=pl.BlockSpec((keep, columns), lambda k, where: (0, 0)),
-            scratch_shapes=[
-                pltpu.VMEM((Z * C, rows, both), BF),
-                pltpu.VMEM((rows_in, columns), F32),
-                pltpu.VMEM((keep, columns), F32),
-            ],
+            in_specs=[pl.BlockSpec((rows_in, width), lambda k, x: (0, 0))] * n
+            + [pl.BlockSpec((blocks, 1, rows, both), lambda k, x: (0, lax.rem(x[0] + n - k, n), 0, 0))],
+            out_specs=pl.BlockSpec((keep, columns), lambda k, x: (0, 0)),
+            scratch_shapes=[pltpu.VMEM((rows_in, columns), F32), pltpu.VMEM((keep, columns), F32)],
         ),
         out_shape=jax.ShapeDtypeStruct((keep, columns), BF),
-        compiler_params=pltpu.CompilerParams(vmem_limit_bytes=40 * MB),
+        compiler_params=pltpu.CompilerParams(vmem_limit_bytes=56 * MB),
         cost_estimate=pl.CostEstimate(
             flops=2 * n * width * (rows_in + keep) * columns,
             bytes_accessed=2 * n * width * (rows_in + both),
             transcendentals=columns,
         ),
-    )(where, *normed, *blocks)
+    )(x, *normed, panels)
 
 
 def ring(size, step):
     return [(i, (i + step) % size) for i in range(size)]
-
-
-def both_ways(up, down):
-    return lax.ppermute(up, "z", ring(Z, 1)), lax.ppermute(down, "z", ring(Z, -1))
 
 
 def spread_to_all(values, axes, size):
@@ -130,14 +108,9 @@
     panel = jnp.concatenate([teacher_next, student_weight], axis=1).astype(BF)
     panels = lax.all_gather(panel, "yl", axis=0, tiled=True)
     panels, image = lax.optimization_barrier((panels, image))
-    own = panels.reshape(Y, rows, 2 * columns)
-    up1, down1 = both_ways(own, own)
+    panels = lax.all_gather(panels, ("z", "c"), axis=0, tiled=True).reshape(Z * C, Y, rows, 2 * columns)
+
     other = lax.ppermute(image, "yh", ring(H, 1))
-    up1, down1, other = lax.optimization_barrier((up1, down1, other))
-    near = jnp.stack([own, up1, down1])
-    near_other = lax.ppermute(near, "c", ring(C, 1))
-    up2, down2 = both_ways(up1, down1)
-
     pair = jnp.where(
         lax.axis_index("yh") == 0,
         jnp.concatenate([image, other], axis=1),
@@ -149,8 +122,6 @@
     own_mean = jnp.mean(floats, axis=1)
     own_moment = jnp.sum(jnp.square(floats - own_mean[:, None]), axis=1)
     parts = spread_to_all(jnp.stack([own_mean, own_moment]), ("x", "yh"), X * H)
-    up2, down2, parts, pair, near_other = lax.optimization_barrier((up2, down2, parts, pair, near_other))
-    up3, down3 = both_ways(up2, down2)
     centre = jnp.mean(parts[:, 0], axis=0)
     moment = jnp.sum(parts[:, 1], axis=0) + slice_width * jnp.sum(jnp.square(parts[:, 0] - centre), axis=0)
     scale = lax.rsqrt(moment / D + 1e-06)
@@ -161,17 +132,13 @@
     normed = [normalise(pair, centre, scale, select)]
     pieces = normed[0][patches:].reshape(keep_count, Z * C, rows).transpose(1, 0, 2)
     pieces = lax.all_to_all(pieces, ("z", "c"), split_axis=0, concat_axis=0)
-    up3, down3, pieces, arrived = lax.optimization_barrier((up3, down3, pieces, arrived))
-    last_up, last_down = both_ways(up3[..., :columns], down3[..., columns:])
-    far = jnp.stack([up2, down2, up3, down3, jnp.concatenate([last_up, last_down], axis=-1)])
-    owned = spread_to_all(pieces, "x", X)
-    owned = owned.reshape(Y, Z * C * keep_count, rows).transpose(0, 2, 1).reshape(Y * rows, Z * C * keep_count)
+    pieces = pieces.reshape(Z * C * keep_count, rows).T
+    pieces, arrived = lax.optimization_barrier((pieces, arrived))
+    owned = spread_to_all(pieces, "x", X).reshape(Y * rows, Z * C * keep_count)
 
     normed += [normalise(chunk, centre, scale, select) for chunk in arrived]
-    blocks = near, near_other, far, lax.ppermute(far, "c", ring(C, 1))
-    where = jnp.stack([lax.axis_index("x"), lax.axis_index("z"), lax.axis_index("c")])
     total_kept = keep_count * Y * Z * C
-    error = make_error(normed, patches, where, blocks, 1.0 / math.sqrt(total_kept))
+    error = make_error(normed, patches, lax.axis_index("x").reshape(1), panels, 1.0 / math.sqrt(total_kept))
     errors = lax.all_gather(error, ("z", "c"), axis=0, tiled=True)
     partial = jnp.dot(owned, errors, preferred_element_type=F32).astype(BF).reshape(Y, rows, columns)
     partial = lax.all_to_all(partial, "yl", split_axis=0, concat_axis=0)

time: 210 us -> 160 us (0.76)
  starting transfers between devices: 79.7 us -> 25.4 us
  blocking collectives: 46.2 us -> 80.8 us
  local copies, waits for them, and re-layouts: 25.7 us -> 5.21 us
  waiting for transfers between devices: 32.7 us -> 17 us
  between operations: 0.97 us -> 14.2 us
  other arithmetic: 9.19 us -> 3.22 us
    ppermute x10 -> x0, starting transfers between devices: 46.4 us -> none  [the longest x4 22.3 us: both_ways(): lax.ppermute(down, 'z', ring(Z, -1))]
    all_to_all x0 -> x1, blocking collectives: none -> 28 us  [shards(): pieces = lax.all_to_all(pieces, ('z', 'c'), split_axis=0, concat_axis=0)]
    ppermute x1, waiting for transfers between devices: 15.7 us -> 0.01 us  [shards(): other = lax.ppermute(image, 'yh', ring(H, 1))]
    unnamed x30 -> x12, local copies, waits for them, and re-layouts: 18.3 us -> 2.88 us
    all_to_all x1 -> x0, starting transfers between devices: 6.73 us -> none  [shards(): pieces = lax.all_to_all(pieces, ('z', 'c'), split_axis=0, concat_axis=0)]
    ppermute x3, waiting for transfers between devices: 9.39 us -> 3.03 us  [shards(): arrived = [lax.ppermute(pair, 'x', ring(X, step)) for step in range(1, X)]]
    all_to_all x2, waiting for transfers between devices: 7.63 us -> 13.9 us  [spread_to_all(): lax.all_to_all(jnp.broadcast_to(values[None], (size, *values.shape)), axe...]
    all_gather x1, blocking collectives: 20.6 us -> 26.2 us  [shards(): errors = lax.all_gather(error, ('z', 'c'), axis=0, tiled=True)]
  transfers between devices with their start and end apart: 17 -> 7, of which waited for: 3 -> 2; matrix products, arithmetic and copies ran while one was open for 9% -> 2% of each run, Pallas kernels for 3% -> 8%
where the time goes in v4:
time: 160 us; the launch traced here: 159 us
  blocking collectives  80.8 us (50%)
  starting transfers between devices  25.4 us (16%)
  waiting for transfers between devices  17 us (11%)
  between operations  14.2 us (9%)
  Pallas kernels  12.4 us (8%)
  local copies, waits for them, and re-layouts  5.21 us (3%)
  other arithmetic  3.22 us (2%)
    all_to_all x1, blocking collectives, shards(): pieces = lax.all_to_all(pieces, ('z', 'c'), split_axis=0, concat_axis=0)  28 us
    all_gather x1, blocking collectives, shards(): errors = lax.all_gather(error, ('z', 'c'), axis=0, tiled=True)  26.2 us
    all_gather x1, blocking collectives, shards(): panels = lax.all_gather(panel, 'yl', axis=0, tiled=True)  15.4 us
    all_to_all x2, waiting for transfers between devices, spread_to_all(): lax.all_to_all(jnp.broadcast_to(values[None], (size, *values.shape)), axe...  13.9 us
    all_to_all x1, blocking collectives, shards(): partial = lax.all_to_all(partial, 'yl', split_axis=0, concat_axis=0)  11.2 us
    all_to_all x2, starting transfers between devices, spread_to_all(): lax.all_to_all(jnp.broadcast_to(values[None], (size, *values.shape)), axe...  10.5 us
    ppermute x3, starting transfers between devices, shards(): arrived = [lax.ppermute(pair, 'x', ring(X, step)) for step in range(1, X)]  8.77 us
    pallas_call x1, Pallas kernels, make_error(): pl.pallas_call(body, grid_spec=pltpu.PrefetchScalarGridSpec(num_scalar_pr...  8.38 us
  transfers between devices with their start and end apart: 7, of which 2 were waited for; matrix products, arithmetic and copies ran while one was open for 2% of the time, Pallas kernels for 8%

profile of v4, /device:TPU:1, one launch (start us, length us, event | category | flops | bytes accessed | tf_op | source)
XLA Modules:
  0.0 158.8 jit_solution(10730376776983187576)
XLA Ops:
  7.2 0.0 copy-start.4
  7.2 0.0 copy-start.5
  7.2 0.0 all-gather.2.cloned.1.call-start
  7.2 1.8 %fusion.5 = (bf16[96,384]{1,0:T(8,128)(2,1)S(1)}, f32[96,384]{1,0:T(8,128)}, bf16[96,384]{1,0:T(8,128)(2,1)S(1)}) fusion(f32[96,384]{1,0:T(8,128)} %param.7, f32[96,384]{1,0:T(8,128)} %param.6), kind=kLoop, calls=%fused_computation.21 | loop fusion | flops 184320 | bytes 589824 | tf_op jit(solution)/shard_map/convert
  9.0 15.4 %all_gather.9 = bf16[384,768]{1,0:T(8,128)(2,1)} all-gather(bf16[96,768]{1,0:T(8,128)(2,1)S(1)} %pad_maximum_fusion), channel_id=1, replica_groups=mesh['yl'=4,'z'=8,'c'=2,'x'=4,'yh'=2] {'yl'}, dimensions={0}, use_global_device_ids=true | all-gather | bytes 737280 | tf_op jit(solution)/shard_map/all_gather | solution.py:109
  24.4 0.0 all-gather.2.cloned.1.call-update
  24.5 0.0 copy-done.4
  24.5 6.1 %collective-permute-start = (bf16[256,768]{1,0:T(8,128)(2,1)S(1)}, bf16[256,768]{1,0:T(8,128)(2,1)S(1)}, u32[]{:S(2)}, u32[]{:S(2)}) collective-permute-start(bf16[256,768]{1,0:T(8,128)(2,1)S(1)} %bitcast.25), channel_id=1, source_target_pairs={{0,1},{1,0},{2,3},{3,2},{4,5},{5,4},{6,7},{7,6},{8,9},{9,8},{10,11... | collective-permute-start | bytes 1179656 | tf_op jit(solution)/shard_map/ppermute | solution.py:113
  30.6 0.1 convert_reduce_fusion
  30.7 0.2 fusion.1
  31.0 0.6 broadcast_in_dim.4
  31.6 5.7 %all-to-all-start = ((f32[8,2,256]{2,1,0:T(2,128)}), f32[8,2,256]{2,1,0:T(2,128)S(1)}, u32[]{:S(2)}, u32[]{:S(2)}) async-start(f32[8,2,256]{2,1,0:T(2,128)} %broadcast_in_dim.4), calls=%async_computation | async-start | bytes 32768 | tf_op jit(solution)/shard_map/all_to_all | solution.py:98
  37.3 0.0 copy-done.5
  37.3 0.1 fusion.2.select_ref
  37.4 13.9 %all-to-all-done = f32[8,2,256]{2,1,0:T(2,128)S(1)} async-done(((f32[8,2,256]{2,1,0:T(2,128)}), f32[8,2,256]{2,1,0:T(2,128)S(1)}, u32[]{:S(2)}, u32[]{:S(2)}) %all-to-all-start) | async-done | bytes 16416 | tf_op jit(solution)/shard_map/all_to_all | solution.py:98
  51.3 0.0 collective-permute-done
  51.3 0.2 maximum_select_fusion.image_ref
  51.5 2.2 %collective-permute-start.1 = (bf16[256,1536]{1,0:T(8,128)(2,1)S(1)}, bf16[256,1536]{1,0:T(8,128)(2,1)S(1)}, u32[]{:S(2)}, u32[]{:S(2)}) collective-permute-start(bf16[256,1536]{1,0:T(8,128)(2,1)S(1)} %maximum_select_fusion.image_ref), channel_id=1, source_target_pairs={{0,2},{2,4},{4,6},{6,0},{1,3},{3,5},{5,7},{7,1},{8,10},{10,12},{12... | collective-permute-start | bytes 2359304 | tf_op jit(solution)/shard_map/ppermute | solution.py:119
  53.8 3.6 %collective-permute-start.2 = (bf16[256,1536]{1,0:T(8,128)(2,1)S(1)}, bf16[256,1536]{1,0:T(8,128)(2,1)}, u32[]{:S(2)}, u32[]{:S(2)}) collective-permute-start(bf16[256,1536]{1,0:T(8,128)(2,1)S(1)} %maximum_select_fusion.image_ref), channel_id=1, source_target_pairs={{0,4},{2,6},{4,0},{6,2},{1,5},{3,7},{5,1},{7,3},{8,12},{10,14},{12... | collective-permute-start | bytes 2359304 | tf_op jit(solution)/shard_map/ppermute | solution.py:119
  57.4 2.9 %collective-permute-start.3 = (bf16[256,1536]{1,0:T(8,128)(2,1)S(1)}, bf16[256,1536]{1,0:T(8,128)(2,1)}, u32[]{:S(2)}, u32[]{:S(2)}) collective-permute-start(bf16[256,1536]{1,0:T(8,128)(2,1)S(1)} %maximum_select_fusion.image_ref), channel_id=1, source_target_pairs={{0,6},{2,0},{4,2},{6,4},{1,7},{3,1},{5,3},{7,5},{8,14},{10,8},{12,... | collective-permute-start | bytes 2359304 | tf_op jit(solution)/shard_map/ppermute | solution.py:119
  60.4 0.1 copy.30.scale_ref
  60.5 0.1 copy.29.centre_ref
  60.7 0.4 shard_map.59.refs_1_
  61.1 0.0 copy-start
  61.1 0.2 reshape.79
  61.4 0.1 copy.44
  61.5 28.0 %all_to_all.20 = bf16[16,64,96]{2,1,0:T(8,128)(2,1)S(1)} all-to-all(bf16[16,64,96]{2,1,0:T(8,128)(2,1)S(1)} %bitcast.30), channel_id=1, replica_groups=mesh['yl'=4,'z'=8,'c'=2,'x'=4,'yh'=2] {'z','c'}, dimensions={0} | all-to-all | bytes 393216 | tf_op jit(solution)/shard_map/all_to_all | solution.py:134
  89.4 0.0 collective-permute-done.1.image_ref
  89.4 0.0 collective-permute-done.2.image_ref
  89.4 3.0 %collective-permute-done.3.image_ref = bf16[256,1536]{1,0:T(8,128)(2,1)} collective-permute-done((bf16[256,1536]{1,0:T(8,128)(2,1)S(1)}, bf16[256,1536]{1,0:T(8,128)(2,1)}, u32[]{:S(2)}, u32[]{:S(2)}) %collective-permute-start.3) | collective-permute-done | bytes 786464 | tf_op jit(solution)/shard_map/ppermute | solution.py:119
  92.4 0.1 copy.32
  92.6 1.0 broadcast_in_dim.5
  93.6 0.0 copy-done
  93.6 4.8 %all-to-all-start.2 = ((bf16[4,96,1024]{2,1,0:T(8,128)(2,1)}), bf16[4,96,1024]{2,1,0:T(8,128)(2,1)S(1)}, u32[]{:S(2)}, u32[]{:S(2)}) async-start(bf16[4,96,1024]{2,1,0:T(8,128)(2,1)} %broadcast_in_dim.5), calls=%async_computation.2 | async-start | bytes 1572864 | tf_op jit(solution)/shard_map/all_to_all | solution.py:98
  98.4 1.6 shard_map.62.refs_4_
  99.9 0.0 copy-start.1
  99.9 0.9 copy-done.1
  100.9 1.6 shard_map.61.refs_3_
  102.4 0.0 copy-start.2
  102.4 1.0 copy-done.2
  103.4 0.4 shard_map.60.refs_2_
  103.9 0.9 copy-done.3
  104.8 8.4 %shard_map.63 = bf16[64,384]{1,0:T(8,128)(2,1)} custom-call(s32[1]{0:T(128)} %bitcast.10.refs_0_, bf16[320,1536]{1,0:T(8,128)(2,1)} %copy-done, bf16[320,1536]{1,0:T(8,128)(2,1)} %copy-done.3, bf16[320,1536]{1,0:T(8,128)(2,1)} %copy-done.2, bf16[320,1536]{1,0:T(8,128)(2,1)} %copy-done.1, bf16[16,4,96,768]{3,2,1,0:T(8,128)(2,1)} %bitcast.24), custom_call_target="tpu_custom_call" | custom-call | flops 1811939328 | bytes 13369344 | tf_op jit(solution)/shard_map/pallas_call | solution.py:73
  113.2 26.2 %all_gather.11 = bf16[1024,384]{1,0:T(8,128)(2,1)S(1)} all-gather(bf16[64,384]{1,0:T(8,128)(2,1)} %shard_map.63), channel_id=1, replica_groups=mesh['yl'=4,'z'=8,'c'=2,'x'=4,'yh'=2] {'z','c'}, dimensions={0}, use_global_device_ids=true | all-gather | bytes 835584 | tf_op jit(solution)/shard_map/all_gather | solution.py:142
  139.4 0.0 all-to-all-done.2
  139.4 0.6 convolution_convert_fusion
  140.0 11.2 %all_to_all.21 = bf16[4,96,384]{2,1,0:T(8,128)(2,1)S(1)} all-to-all(bf16[4,96,384]{2,1,0:T(8,128)(2,1)S(1)} %bitcast.32), channel_id=1, replica_groups=mesh['yl'=4,'z'=8,'c'=2,'x'=4,'yh'=2] {'yl'}, dimensions={0} | all-to-all | bytes 589824 | tf_op jit(solution)/shard_map/all_to_all | solution.py:144
  151.2 0.7 convert_reduce_fusion.1
  (10 shorter events, 0.1 us)
Async XLA Ops:
  7.2 17.3 %copy-start.4 = (bf16[1,256,768]{2,1,0:T(8,128)(2,1)S(1)}, bf16[1,256,768]{2,1,0:T(8,128)(2,1)}, u32[]{:S(2)}) copy-start(bf16[1,256,768]{2,1,0:T(8,128)(2,1)} %param.4) | copy-start | bytes 1179652
  7.2 30.1 %copy-start.5 = (s32[1,64]{1,0:T(1,128)S(1)}, s32[1,64]{1,0:T(1,128)}, u32[]{:S(2)}) copy-start(s32[1,64]{1,0:T(1,128)} %param.5) | copy-start | bytes 772
  7.2 97.6 %all-gather.2.cloned.1.call-start = ((), (), s32[]{:S(2)}) async-start(), calls=%async_computation.4 | async-start | bytes 10027008 | tf_op jit(solution)/shard_map/all_gather | solution.py:111
  24.5 26.9 %collective-permute-start = (bf16[256,768]{1,0:T(8,128)(2,1)S(1)}, bf16[256,768]{1,0:T(8,128)(2,1)S(1)}, u32[]{:S(2)}, u32[]{:S(2)}) collective-permute-start(bf16[256,768]{1,0:T(8,128)(2,1)S(1)} %bitcast.25), channel_id=1, source_target_pairs={{0,1},{1,0},{2,3},{3,2},{4,5},{5,4},{6,7},{7,6},{8,9},{9,8},{10,11... | collective-permute-start | bytes 1179656 | tf_op jit(solution)/shard_map/ppermute | solution.py:113
  31.6 19.7 %all-to-all-start = ((f32[8,2,256]{2,1,0:T(2,128)}), f32[8,2,256]{2,1,0:T(2,128)S(1)}, u32[]{:S(2)}, u32[]{:S(2)}) async-start(f32[8,2,256]{2,1,0:T(2,128)} %broadcast_in_dim.4), calls=%async_computation | async-start | bytes 32768 | tf_op jit(solution)/shard_map/all_to_all | solution.py:98
  51.5 37.9 %collective-permute-start.1 = (bf16[256,1536]{1,0:T(8,128)(2,1)S(1)}, bf16[256,1536]{1,0:T(8,128)(2,1)S(1)}, u32[]{:S(2)}, u32[]{:S(2)}) collective-permute-start(bf16[256,1536]{1,0:T(8,128)(2,1)S(1)} %maximum_select_fusion.image_ref), channel_id=1, source_target_pairs={{0,2},{2,4},{4,6},{6,0},{1,3},{3,5},{5,7},{7,1},{8,10},{10,12},{12... | collective-permute-start | bytes 2359304 | tf_op jit(solution)/shard_map/ppermute | solution.py:119
  53.8 35.6 %collective-permute-start.2 = (bf16[256,1536]{1,0:T(8,128)(2,1)S(1)}, bf16[256,1536]{1,0:T(8,128)(2,1)}, u32[]{:S(2)}, u32[]{:S(2)}) collective-permute-start(bf16[256,1536]{1,0:T(8,128)(2,1)S(1)} %maximum_select_fusion.image_ref), channel_id=1, source_target_pairs={{0,4},{2,6},{4,0},{6,2},{1,5},{3,7},{5,1},{7,3},{8,12},{10,14},{12... | collective-permute-start | bytes 2359304 | tf_op jit(solution)/shard_map/ppermute | solution.py:119
  57.4 35.0 %collective-permute-start.3 = (bf16[256,1536]{1,0:T(8,128)(2,1)S(1)}, bf16[256,1536]{1,0:T(8,128)(2,1)}, u32[]{:S(2)}, u32[]{:S(2)}) collective-permute-start(bf16[256,1536]{1,0:T(8,128)(2,1)S(1)} %maximum_select_fusion.image_ref), channel_id=1, source_target_pairs={{0,6},{2,0},{4,2},{6,4},{1,7},{3,1},{5,3},{7,5},{8,14},{10,8},{12,... | collective-permute-start | bytes 2359304 | tf_op jit(solution)/shard_map/ppermute | solution.py:119
  61.1 32.5 %copy-start = (bf16[320,1536]{1,0:T(8,128)(2,1)}, bf16[320,1536]{1,0:T(8,128)(2,1)S(1)}, u32[]{:S(2)}) copy-start(bf16[320,1536]{1,0:T(8,128)(2,1)S(1)} %shard_map.59.refs_1_) | copy-start | bytes 2949124
  93.6 45.8 %all-to-all-start.2 = ((bf16[4,96,1024]{2,1,0:T(8,128)(2,1)}), bf16[4,96,1024]{2,1,0:T(8,128)(2,1)S(1)}, u32[]{:S(2)}, u32[]{:S(2)}) async-start(bf16[4,96,1024]{2,1,0:T(8,128)(2,1)} %broadcast_in_dim.5), calls=%async_computation.2 | async-start | bytes 1572864 | tf_op jit(solution)/shard_map/all_to_all | solution.py:98
  99.9 0.9 copy-start.1
  102.4 1.0 copy-start.2
  103.9 0.9 copy-start.3
Sparse Core Ops, SparseCore 0:
  24.6 77.6 all-gather.1

commit v5 on v4

--- a/solution.py
+++ b/solution.py
@@ -12,6 +12,7 @@
 Y, Z, C, X, H = 4, 8, 2, 4, 2
 BF, F32 = jnp.bfloat16, jnp.float32
 MB = 1024 * 1024
+STREAMS = 4
 
 
 def normalise_kernel(image_ref, centre_ref, scale_ref, select_ref, normed_ref):
@@ -36,11 +37,11 @@
 
 def error_kernel(factor, patches, x_ref, *refs):
     n = pl.num_programs(0)
-    normed_refs = refs[:Y]
-    panel_ref, error_ref, teacher_acc, student_acc = refs[Y:]
+    normed_refs, panel_refs = refs[:Y], refs[Y : Y + STREAMS]
+    error_ref, teacher_acc, student_acc = refs[Y + STREAMS :]
     step = pl.program_id(0)
     columns = error_ref.shape[1]
-    panel = panel_ref[:, 0].reshape(-1, 2 * columns)
+    panel = jnp.concatenate([ref[:, 0].reshape(-1, 2 * columns) for ref in panel_refs], axis=0)
     for k in range(Y):
 
         @pl.when(step == k)
@@ -76,7 +77,10 @@
             num_scalar_prefetch=1,
             grid=(n,),
             in_specs=[pl.BlockSpec((rows_in, width), lambda k, x: (0, 0))] * n
-            + [pl.BlockSpec((blocks, 1, rows, both), lambda k, x: (0, lax.rem(x[0] + n - k, n), 0, 0))],
+            + [
+                pl.BlockSpec((blocks // STREAMS, 1, rows, both), lambda k, x, i=i: (i, lax.rem(x[0] + n - k, n), 0, 0))
+                for i in range(STREAMS)
+            ],
             out_specs=pl.BlockSpec((keep, columns), lambda k, x: (0, 0)),
             scratch_shapes=[pltpu.VMEM((rows_in, columns), F32), pltpu.VMEM((keep, columns), F32)],
         ),
@@ -87,7 +91,7 @@
             bytes_accessed=2 * n * width * (rows_in + both),
             transcendentals=columns,
         ),
-    )(x, *normed, panels)
+    )(x, *normed, *[panels] * STREAMS)
 
 
 def ring(size, step):
@@ -137,6 +141,7 @@
     owned = spread_to_all(pieces, "x", X).reshape(Y * rows, Z * C * keep_count)
 
     normed += [normalise(chunk, centre, scale, select) for chunk in arrived]
+    normed, owned = lax.optimization_barrier((normed, owned))
     total_kept = keep_count * Y * Z * C
     error = make_error(normed, patches, lax.axis_index("x").reshape(1), panels, 1.0 / math.sqrt(total_kept))
     errors = lax.all_gather(error, ("z", "c"), axis=0, tiled=True)

time: 160 us -> 165 us (1.031)
  waiting for transfers between devices: 17 us -> 22.1 us
    all_to_all x2, waiting for transfers between devices: 13.9 us -> 19.1 us  [spread_to_all(): lax.all_to_all(jnp.broadcast_to(values[None], (size, *values.shape)), axe...]
  transfers between devices with their start and end apart: 7 -> 7, of which waited for: 2 -> 3; matrix products, arithmetic and copies ran while one was open for 2% -> 2% of each run, Pallas kernels for 8% -> 2%
where the time goes in v5:
time: 165 us
  blocking collectives  81.7 us (50%)
  starting transfers between devices  25.4 us (15%)
  waiting for transfers between devices  22.1 us (13%)
  between operations  14.2 us (9%)
  Pallas kernels  12.4 us (8%)
  local copies, waits for them, and re-layouts  5.21 us (3%)
  other arithmetic  3.22 us (2%)
    all_to_all x1, blocking collectives, shards(): pieces = lax.all_to_all(pieces, ('z', 'c'), split_axis=0, concat_axis=0)  28 us
    all_gather x1, blocking collectives, shards(): errors = lax.all_gather(error, ('z', 'c'), axis=0, tiled=True)  27.1 us
    all_to_all x2, waiting for transfers between devices, spread_to_all(): lax.all_to_all(jnp.broadcast_to(values[None], (size, *values.shape)), axe...  19.1 us
    all_gather x1, blocking collectives, shards(): panels = lax.all_gather(panel, 'yl', axis=0, tiled=True)  15.4 us
    all_to_all x1, blocking collectives, shards(): partial = lax.all_to_all(partial, 'yl', split_axis=0, concat_axis=0)  11.2 us
    all_to_all x2, starting transfers between devices, spread_to_all(): lax.all_to_all(jnp.broadcast_to(values[None], (size, *values.shape)), axe...  10.5 us
    ppermute x3, starting transfers between devices, shards(): arrived = [lax.ppermute(pair, 'x', ring(X, step)) for step in range(1, X)]  8.77 us
    pallas_call x1, Pallas kernels, make_error(): pl.pallas_call(body, grid_spec=pltpu.PrefetchScalarGridSpec(num_scalar_pr...  8.44 us
  transfers between devices with their start and end apart: 7, of which 3 were waited for; matrix products, arithmetic and copies ran while one was open for 2% of the time, Pallas kernels for 2%

profile of v5, /device:TPU:1, one launch (start us, length us, event | category | flops | bytes accessed | tf_op | source)
XLA Modules:
  0.0 164.9 jit_solution(6964982119946565151)
XLA Ops:
  7.2 0.0 copy-start.4
  7.2 0.0 copy-start.5
  7.2 0.0 all-gather.2.cloned.1.call-start
  7.2 1.8 %fusion.5 = (bf16[96,384]{1,0:T(8,128)(2,1)S(1)}, f32[96,384]{1,0:T(8,128)}, bf16[96,384]{1,0:T(8,128)(2,1)S(1)}) fusion(f32[96,384]{1,0:T(8,128)} %param.7, f32[96,384]{1,0:T(8,128)} %param.6), kind=kLoop, calls=%fused_computation.21 | loop fusion | flops 184320 | bytes 589824 | tf_op jit(solution)/shard_map/convert
  9.0 15.4 %all_gather.9 = bf16[384,768]{1,0:T(8,128)(2,1)} all-gather(bf16[96,768]{1,0:T(8,128)(2,1)S(1)} %pad_maximum_fusion), channel_id=1, replica_groups=mesh['yl'=4,'z'=8,'c'=2,'x'=4,'yh'=2] {'yl'}, dimensions={0}, use_global_device_ids=true | all-gather | bytes 737280 | tf_op jit(solution)/shard_map/all_gather | solution.py:113
  24.4 0.0 all-gather.2.cloned.1.call-update
  24.5 0.0 copy-done.4
  24.5 6.1 %collective-permute-start = (bf16[256,768]{1,0:T(8,128)(2,1)S(1)}, bf16[256,768]{1,0:T(8,128)(2,1)S(1)}, u32[]{:S(2)}, u32[]{:S(2)}) collective-permute-start(bf16[256,768]{1,0:T(8,128)(2,1)S(1)} %bitcast.28), channel_id=1, source_target_pairs={{0,1},{1,0},{2,3},{3,2},{4,5},{5,4},{6,7},{7,6},{8,9},{9,8},{10,11... | collective-permute-start | bytes 1179656 | tf_op jit(solution)/shard_map/ppermute | solution.py:117
  30.6 0.1 convert_reduce_fusion
  30.7 0.2 fusion.1
  31.0 0.6 broadcast_in_dim.4
  31.6 5.7 %all-to-all-start = ((f32[8,2,256]{2,1,0:T(2,128)}), f32[8,2,256]{2,1,0:T(2,128)S(1)}, u32[]{:S(2)}, u32[]{:S(2)}) async-start(f32[8,2,256]{2,1,0:T(2,128)} %broadcast_in_dim.4), calls=%async_computation | async-start | bytes 32768 | tf_op jit(solution)/shard_map/all_to_all | solution.py:102
  37.3 0.0 copy-done.5
  37.3 0.1 fusion.2.select_ref
  37.4 13.9 %all-to-all-done = f32[8,2,256]{2,1,0:T(2,128)S(1)} async-done(((f32[8,2,256]{2,1,0:T(2,128)}), f32[8,2,256]{2,1,0:T(2,128)S(1)}, u32[]{:S(2)}, u32[]{:S(2)}) %all-to-all-start) | async-done | bytes 16416 | tf_op jit(solution)/shard_map/all_to_all | solution.py:102
  51.3 0.0 collective-permute-done
  51.3 0.2 maximum_select_fusion.image_ref
  51.5 2.2 %collective-permute-start.1 = (bf16[256,1536]{1,0:T(8,128)(2,1)S(1)}, bf16[256,1536]{1,0:T(8,128)(2,1)S(1)}, u32[]{:S(2)}, u32[]{:S(2)}) collective-permute-start(bf16[256,1536]{1,0:T(8,128)(2,1)S(1)} %maximum_select_fusion.image_ref), channel_id=1, source_target_pairs={{0,2},{2,4},{4,6},{6,0},{1,3},{3,5},{5,7},{7,1},{8,10},{10,12},{12... | collective-permute-start | bytes 2359304 | tf_op jit(solution)/shard_map/ppermute | solution.py:123
  53.8 3.6 %collective-permute-start.2 = (bf16[256,1536]{1,0:T(8,128)(2,1)S(1)}, bf16[256,1536]{1,0:T(8,128)(2,1)}, u32[]{:S(2)}, u32[]{:S(2)}) collective-permute-start(bf16[256,1536]{1,0:T(8,128)(2,1)S(1)} %maximum_select_fusion.image_ref), channel_id=1, source_target_pairs={{0,4},{2,6},{4,0},{6,2},{1,5},{3,7},{5,1},{7,3},{8,12},{10,14},{12... | collective-permute-start | bytes 2359304 | tf_op jit(solution)/shard_map/ppermute | solution.py:123
  57.4 2.9 %collective-permute-start.3 = (bf16[256,1536]{1,0:T(8,128)(2,1)S(1)}, bf16[256,1536]{1,0:T(8,128)(2,1)}, u32[]{:S(2)}, u32[]{:S(2)}) collective-permute-start(bf16[256,1536]{1,0:T(8,128)(2,1)S(1)} %maximum_select_fusion.image_ref), channel_id=1, source_target_pairs={{0,6},{2,0},{4,2},{6,4},{1,7},{3,1},{5,3},{7,5},{8,14},{10,8},{12,... | collective-permute-start | bytes 2359304 | tf_op jit(solution)/shard_map/ppermute | solution.py:123
  60.3 0.1 copy.29.centre_ref
  60.5 0.1 copy.30.scale_ref
  60.7 0.4 shard_map.59.refs_1_
  61.1 0.0 copy-start
  61.1 0.2 reshape.79
  61.4 0.1 copy.44
  61.5 28.0 %all_to_all.20 = bf16[16,64,96]{2,1,0:T(8,128)(2,1)S(1)} all-to-all(bf16[16,64,96]{2,1,0:T(8,128)(2,1)S(1)} %bitcast.33), channel_id=1, replica_groups=mesh['yl'=4,'z'=8,'c'=2,'x'=4,'yh'=2] {'z','c'}, dimensions={0} | all-to-all | bytes 393216 | tf_op jit(solution)/shard_map/all_to_all | solution.py:138
  89.4 0.0 collective-permute-done.1.image_ref
  89.4 0.0 collective-permute-done.2.image_ref
  89.4 3.0 %collective-permute-done.3.image_ref = bf16[256,1536]{1,0:T(8,128)(2,1)} collective-permute-done((bf16[256,1536]{1,0:T(8,128)(2,1)S(1)}, bf16[256,1536]{1,0:T(8,128)(2,1)}, u32[]{:S(2)}, u32[]{:S(2)}) %collective-permute-start.3) | collective-permute-done | bytes 786464 | tf_op jit(solution)/shard_map/ppermute | solution.py:123
  92.4 0.1 copy.38
  92.6 1.0 broadcast_in_dim.5
  93.6 0.0 copy-done
  93.6 4.8 %all-to-all-start.2 = ((bf16[4,96,1024]{2,1,0:T(8,128)(2,1)}), bf16[4,96,1024]{2,1,0:T(8,128)(2,1)S(1)}, u32[]{:S(2)}, u32[]{:S(2)}) async-start(bf16[4,96,1024]{2,1,0:T(8,128)(2,1)} %broadcast_in_dim.5), calls=%async_computation.2 | async-start | bytes 1572864 | tf_op jit(solution)/shard_map/all_to_all | solution.py:102
  98.4 0.4 shard_map.60.refs_2_
  98.8 0.0 copy-start.1
  98.8 0.9 copy-done.1
  99.7 1.6 shard_map.61.refs_3_
  101.3 0.9 copy-done.2
  102.2 1.6 shard_map.62.refs_4_
  103.8 0.0 copy-start.3
  103.8 1.0 copy-done.3
  104.8 5.1 %all-to-all-done.2 = bf16[4,96,1024]{2,1,0:T(8,128)(2,1)S(1)} async-done(((bf16[4,96,1024]{2,1,0:T(8,128)(2,1)}), bf16[4,96,1024]{2,1,0:T(8,128)(2,1)S(1)}, u32[]{:S(2)}, u32[]{:S(2)}) %all-to-all-start.2) | async-done | bytes 786464 | tf_op jit(solution)/shard_map/all_to_all | solution.py:102
  109.9 8.4 %shard_map.63 = bf16[64,384]{1,0:T(8,128)(2,1)} custom-call(s32[1]{0:T(128)} %bitcast.10.refs_0_, bf16[320,1536]{1,0:T(8,128)(2,1)} %copy-done, bf16[320,1536]{1,0:T(8,128)(2,1)} %copy-done.1, bf16[320,1536]{1,0:T(8,128)(2,1)} %copy-done.2, bf16[320,1536]{1,0:T(8,128)(2,1)} %copy-done.3, bf16[16,4,96,768]{3,2,1,0:T(8,128)(2,1)} %bitcast.24, ...), custom_call_target="tpu_custom_call" | custom-call | flops 1811939328 | bytes 13369344 | tf_op jit(solution)/shard_map/pallas_call | solution.py:74
  118.4 27.1 %all_gather.11 = bf16[1024,384]{1,0:T(8,128)(2,1)S(1)} all-gather(bf16[64,384]{1,0:T(8,128)(2,1)} %shard_map.63), channel_id=1, replica_groups=mesh['yl'=4,'z'=8,'c'=2,'x'=4,'yh'=2] {'z','c'}, dimensions={0}, use_global_device_ids=true | all-gather | bytes 835584 | tf_op jit(solution)/shard_map/all_gather | solution.py:147
  145.5 0.6 convolution_convert_fusion
  146.1 11.2 %all_to_all.21 = bf16[4,96,384]{2,1,0:T(8,128)(2,1)S(1)} all-to-all(bf16[4,96,384]{2,1,0:T(8,128)(2,1)S(1)} %bitcast.35), channel_id=1, replica_groups=mesh['yl'=4,'z'=8,'c'=2,'x'=4,'yh'=2] {'yl'}, dimensions={0} | all-to-all | bytes 589824 | tf_op jit(solution)/shard_map/all_to_all | solution.py:149
  157.3 0.7 convert_reduce_fusion.1
  (10 shorter events, 0.1 us)
Async XLA Ops:
  7.2 17.3 %copy-start.4 = (bf16[1,256,768]{2,1,0:T(8,128)(2,1)S(1)}, bf16[1,256,768]{2,1,0:T(8,128)(2,1)}, u32[]{:S(2)}) copy-start(bf16[1,256,768]{2,1,0:T(8,128)(2,1)} %param.4) | copy-start | bytes 1179652
  7.2 30.1 %copy-start.5 = (s32[1,64]{1,0:T(1,128)S(1)}, s32[1,64]{1,0:T(1,128)}, u32[]{:S(2)}) copy-start(s32[1,64]{1,0:T(1,128)} %param.5) | copy-start | bytes 772
  7.2 102.8 %all-gather.2.cloned.1.call-start = ((), (), s32[]{:S(2)}) async-start(), calls=%async_computation.4 | async-start | bytes 10027008 | tf_op jit(solution)/shard_map/all_gather | solution.py:115
  24.5 26.9 %collective-permute-start = (bf16[256,768]{1,0:T(8,128)(2,1)S(1)}, bf16[256,768]{1,0:T(8,128)(2,1)S(1)}, u32[]{:S(2)}, u32[]{:S(2)}) collective-permute-start(bf16[256,768]{1,0:T(8,128)(2,1)S(1)} %bitcast.28), channel_id=1, source_target_pairs={{0,1},{1,0},{2,3},{3,2},{4,5},{5,4},{6,7},{7,6},{8,9},{9,8},{10,11... | collective-permute-start | bytes 1179656 | tf_op jit(solution)/shard_map/ppermute | solution.py:117
  31.6 19.7 %all-to-all-start = ((f32[8,2,256]{2,1,0:T(2,128)}), f32[8,2,256]{2,1,0:T(2,128)S(1)}, u32[]{:S(2)}, u32[]{:S(2)}) async-start(f32[8,2,256]{2,1,0:T(2,128)} %broadcast_in_dim.4), calls=%async_computation | async-start | bytes 32768 | tf_op jit(solution)/shard_map/all_to_all | solution.py:102
  51.5 37.9 %collective-permute-start.1 = (bf16[256,1536]{1,0:T(8,128)(2,1)S(1)}, bf16[256,1536]{1,0:T(8,128)(2,1)S(1)}, u32[]{:S(2)}, u32[]{:S(2)}) collective-permute-start(bf16[256,1536]{1,0:T(8,128)(2,1)S(1)} %maximum_select_fusion.image_ref), channel_id=1, source_target_pairs={{0,2},{2,4},{4,6},{6,0},{1,3},{3,5},{5,7},{7,1},{8,10},{10,12},{12... | collective-permute-start | bytes 2359304 | tf_op jit(solution)/shard_map/ppermute | solution.py:123
  53.8 35.6 %collective-permute-start.2 = (bf16[256,1536]{1,0:T(8,128)(2,1)S(1)}, bf16[256,1536]{1,0:T(8,128)(2,1)}, u32[]{:S(2)}, u32[]{:S(2)}) collective-permute-start(bf16[256,1536]{1,0:T(8,128)(2,1)S(1)} %maximum_select_fusion.image_ref), channel_id=1, source_target_pairs={{0,4},{2,6},{4,0},{6,2},{1,5},{3,7},{5,1},{7,3},{8,12},{10,14},{12... | collective-permute-start | bytes 2359304 | tf_op jit(solution)/shard_map/ppermute | solution.py:123
  57.4 35.0 %collective-permute-start.3 = (bf16[256,1536]{1,0:T(8,128)(2,1)S(1)}, bf16[256,1536]{1,0:T(8,128)(2,1)}, u32[]{:S(2)}, u32[]{:S(2)}) collective-permute-start(bf16[256,1536]{1,0:T(8,128)(2,1)S(1)} %maximum_select_fusion.image_ref), channel_id=1, source_target_pairs={{0,6},{2,0},{4,2},{6,4},{1,7},{3,1},{5,3},{7,5},{8,14},{10,8},{12,... | collective-permute-start | bytes 2359304 | tf_op jit(solution)/shard_map/ppermute | solution.py:123
  61.1 32.5 %copy-start = (bf16[320,1536]{1,0:T(8,128)(2,1)}, bf16[320,1536]{1,0:T(8,128)(2,1)S(1)}, u32[]{:S(2)}) copy-start(bf16[320,1536]{1,0:T(8,128)(2,1)S(1)} %shard_map.59.refs_1_) | copy-start | bytes 2949124
  93.6 16.4 %all-to-all-start.2 = ((bf16[4,96,1024]{2,1,0:T(8,128)(2,1)}), bf16[4,96,1024]{2,1,0:T(8,128)(2,1)S(1)}, u32[]{:S(2)}, u32[]{:S(2)}) async-start(bf16[4,96,1024]{2,1,0:T(8,128)(2,1)} %broadcast_in_dim.5), calls=%async_computation.2 | async-start | bytes 1572864 | tf_op jit(solution)/shard_map/all_to_all | solution.py:102
  98.8 0.9 copy-start.1
  101.3 0.9 copy-start.2
  103.8 1.0 copy-start.3
Sparse Core Ops, SparseCore 0:
  24.6 77.6 all-gather.1

commit v6 on v4

--- a/solution.py
+++ b/solution.py
@@ -12,45 +12,84 @@
 Y, Z, C, X, H = 4, 8, 2, 4, 2
 BF, F32 = jnp.bfloat16, jnp.float32
 MB = 1024 * 1024
-
-
-def normalise_kernel(image_ref, centre_ref, scale_ref, select_ref, normed_ref):
-    patches = image_ref.shape[0]
-    normed = ((image_ref[...].astype(F32) - centre_ref[...]) * scale_ref[...]).astype(BF)
-    normed_ref[:patches] = normed
-    normed_ref[patches:] = jnp.dot(select_ref[...], normed, preferred_element_type=F32).astype(BF)
-
-
-def normalise(chunk, centre, scale, select):
+PARTS = 1
+
+
+def normalised(chunk_ref, centre_ref, scale_ref):
+    return ((chunk_ref[...].astype(F32) - centre_ref[...]) * scale_ref[...]).astype(BF)
+
+
+def kept(select_ref, normed):
+    return jnp.dot(select_ref[...], normed, preferred_element_type=F32).astype(BF)
+
+
+def pick_kernel(chunk_ref, centre_ref, scale_ref, select_ref, picked_ref):
+    picked_ref[...] = kept(select_ref, normalised(chunk_ref, centre_ref, scale_ref))
+
+
+def pick(chunk, centre, scale, select):
     patches, width = chunk.shape
     keep = select.shape[0]
     return pl.pallas_call(
-        normalise_kernel,
-        out_shape=jax.ShapeDtypeStruct((patches + keep, width), BF),
+        pick_kernel,
+        out_shape=jax.ShapeDtypeStruct((keep, width), BF),
         compiler_params=pltpu.CompilerParams(vmem_limit_bytes=16 * MB),
         cost_estimate=pl.CostEstimate(
-            flops=2 * keep * patches * width, bytes_accessed=2 * width * (2 * patches + keep), transcendentals=0
+            flops=2 * keep * patches * width, bytes_accessed=2 * width * (patches + keep), transcendentals=0
         ),
     )(chunk, centre, scale, select)
 
 
-def error_kernel(factor, patches, x_ref, *refs):
-    n = pl.num_programs(0)
-    normed_refs = refs[:Y]
-    panel_ref, error_ref, teacher_acc, student_acc = refs[Y:]
+def normalise_kernel(*refs):
+    chunk_refs, (centre_ref, scale_ref, select_ref, normed_ref) = refs[:-4], refs[-4:]
+    patches = centre_ref.shape[0]
+    for k, chunk_ref in enumerate(chunk_refs):
+
+        @pl.when(pl.program_id(0) == k)
+        def _(chunk_ref=chunk_ref):
+            normed = normalised(chunk_ref, centre_ref, scale_ref)
+            normed_ref[0, :patches] = normed
+            normed_ref[0, patches:] = kept(select_ref, normed)
+
+
+def normalise(chunks, centre, scale, select):
+    n = len(chunks)
+    patches, width = chunks[0].shape
+    keep = select.shape[0]
+    whole = lambda k: (0, 0)
+    return pl.pallas_call(
+        normalise_kernel,
+        grid=(n,),
+        in_specs=[pl.BlockSpec((patches, width), whole)] * n
+        + [pl.BlockSpec((patches, 1), whole)] * 2
+        + [pl.BlockSpec((keep, patches), whole)],
+        out_specs=pl.BlockSpec((1, patches + keep, width), lambda k: (k, 0, 0)),
+        out_shape=jax.ShapeDtypeStruct((n, patches + keep, width), BF),
+        compiler_params=pltpu.CompilerParams(vmem_limit_bytes=32 * MB),
+        cost_estimate=pl.CostEstimate(
+            flops=2 * n * keep * patches * width, bytes_accessed=2 * n * width * (2 * patches + keep), transcendentals=0
+        ),
+    )(*chunks, centre, scale, select)
+
+
+def error_kernel(factor, patches, x_ref, normed_ref, panel_ref, error_ref, teacher_acc, student_acc):
     step = pl.program_id(0)
     columns = error_ref.shape[1]
     panel = panel_ref[:, 0].reshape(-1, 2 * columns)
-    for k in range(Y):
-
-        @pl.when(step == k)
-        def _(k=k):
-            teacher = jnp.dot(normed_refs[k][...], panel[:, :columns], preferred_element_type=F32)
-            student = jnp.dot(normed_refs[k][patches:], panel[:, columns:], preferred_element_type=F32)
-            teacher_acc[...] = teacher if k == 0 else teacher_acc[...] + teacher
-            student_acc[...] = student if k == 0 else student_acc[...] + student
-
-    @pl.when(step == n - 1)
+    teacher_part = jnp.dot(normed_ref[0], panel[:, :columns], preferred_element_type=F32)
+    student_part = jnp.dot(normed_ref[0, patches:], panel[:, columns:], preferred_element_type=F32)
+
+    @pl.when(step == 0)
+    def _():
+        teacher_acc[...] = teacher_part
+        student_acc[...] = student_part
+
+    @pl.when(step > 0)
+    def _():
+        teacher_acc[...] += teacher_part
+        student_acc[...] += student_part
+
+    @pl.when(step == pl.num_programs(0) - 1)
     def _():
         teacher = teacher_acc[:patches]
         centre = jnp.mean(teacher, axis=0, keepdims=True)
@@ -61,8 +100,7 @@
 
 
 def make_error(normed, patches, x, panels, factor):
-    n = len(normed)
-    rows_in, width = normed[0].shape
+    n, rows_in, width = normed.shape
     keep = rows_in - patches
     blocks, _, rows, both = panels.shape
     columns = both // 2
@@ -74,9 +112,14 @@
         body,
         grid_spec=pltpu.PrefetchScalarGridSpec(
             num_scalar_prefetch=1,
-            grid=(n,),
-            in_specs=[pl.BlockSpec((rows_in, width), lambda k, x: (0, 0))] * n
-            + [pl.BlockSpec((blocks, 1, rows, both), lambda k, x: (0, lax.rem(x[0] + n - k, n), 0, 0))],
+            grid=(n * PARTS,),
+            in_specs=[
+                pl.BlockSpec((1, rows_in, width // PARTS), lambda k, x: (k // PARTS, 0, lax.rem(k, PARTS))),
+                pl.BlockSpec(
+                    (blocks // PARTS, 1, rows, both),
+                    lambda k, x: (lax.rem(k, PARTS), lax.rem(x[0] + n - k // PARTS, n), 0, 0),
+                ),
+            ],
             out_specs=pl.BlockSpec((keep, columns), lambda k, x: (0, 0)),
             scratch_shapes=[pltpu.VMEM((rows_in, columns), F32), pltpu.VMEM((keep, columns), F32)],
         ),
@@ -87,7 +130,7 @@
             bytes_accessed=2 * n * width * (rows_in + both),
             transcendentals=columns,
         ),
-    )(x, *normed, panels)
+    )(x, normed, panels)
 
 
 def ring(size, step):
@@ -129,14 +172,13 @@
 
     select = (keep_index[0][:, None] == lax.broadcasted_iota(jnp.int32, (keep_count, patches), 1)).astype(BF)
 
-    normed = [normalise(pair, centre, scale, select)]
-    pieces = normed[0][patches:].reshape(keep_count, Z * C, rows).transpose(1, 0, 2)
+    pieces = pick(pair, centre, scale, select).reshape(keep_count, Z * C, rows).transpose(1, 0, 2)
     pieces = lax.all_to_all(pieces, ("z", "c"), split_axis=0, concat_axis=0)
     pieces = pieces.reshape(Z * C * keep_count, rows).T
     pieces, arrived = lax.optimization_barrier((pieces, arrived))
     owned = spread_to_all(pieces, "x", X).reshape(Y * rows, Z * C * keep_count)
 
-    normed += [normalise(chunk, centre, scale, select) for chunk in arrived]
+    normed = normalise([pair, *arrived], centre, scale, select)
     total_kept = keep_count * Y * Z * C
     error = make_error(normed, patches, lax.axis_index("x").reshape(1), panels, 1.0 / math.sqrt(total_kept))
     errors = lax.all_gather(error, ("z", "c"), axis=0, tiled=True)

time: 160 us -> 161 us (level)
  local copies, waits for them, and re-layouts: 5.21 us -> 10.2 us
  waiting for transfers between devices: 17 us -> 14 us
  Pallas kernels: 12.4 us -> 9.95 us
    ppermute x3, waiting for transfers between devices: 3.03 us -> 0.01 us  [shards(): arrived = [lax.ppermute(pair, 'x', ring(X, step)) for step in range(1, X)]]
    reshape x2, local copies, waits for them, and re-layouts: 0.3 us -> 2.94 us  [shards(): pick(pair, centre, scale, select).reshape(keep_count, Z * C, rows)]
    pallas_call x4 -> x2, Pallas kernels: 3.99 us -> 2.21 us  [the longest x1 1.79 us: normalise(): pl.pallas_call(normalise_kernel, grid=(n,), in_specs=[pl.BlockSpec((patch...]
    optimization_barrier x1, local copies, waits for them, and re-layouts: 0.13 us -> 1.77 us  [shards(): pieces, arrived = lax.optimization_barrier((pieces, arrived))]
  transfers between devices with their start and end apart: 7 -> 7, of which waited for: 2 -> 1; matrix products, arithmetic and copies ran while one was open for 2% -> 5% of each run, Pallas kernels for 8% -> 6%
where the time goes in v6:
time: 161 us; the launch traced here: 159 us
  blocking collectives  81.1 us (50%)
  starting transfers between devices  25 us (16%)
  between operations  14.2 us (9%)
  waiting for transfers between devices  14 us (9%)
  local copies, waits for them, and re-layouts  10.2 us (6%)
  Pallas kernels  9.95 us (6%)
  other arithmetic  3.22 us (2%)
  matrix products  1.7 us (1%)
    all_to_all x1, blocking collectives, shards(): pieces = lax.all_to_all(pieces, ('z', 'c'), split_axis=0, concat_axis=0)  28.1 us
    all_gather x1, blocking collectives, shards(): errors = lax.all_gather(error, ('z', 'c'), axis=0, tiled=True)  26.4 us
    all_gather x1, blocking collectives, shards(): panels = lax.all_gather(panel, 'yl', axis=0, tiled=True)  15.4 us
    all_to_all x2, waiting for transfers between devices, spread_to_all(): lax.all_to_all(jnp.broadcast_to(values[None], (size, *values.shape)), axe...  13.9 us
    all_to_all x1, blocking collectives, shards(): partial = lax.all_to_all(partial, 'yl', split_axis=0, concat_axis=0)  11.2 us
    all_to_all x2, starting transfers between devices, spread_to_all(): lax.all_to_all(jnp.broadcast_to(values[None], (size, *values.shape)), axe...  10.1 us
    ppermute x3, starting transfers between devices, shards(): arrived = [lax.ppermute(pair, 'x', ring(X, step)) for step in range(1, X)]  8.77 us
    pallas_call x1, Pallas kernels, make_error(): pl.pallas_call(body, grid_spec=pltpu.PrefetchScalarGridSpec(num_scalar_pr...  7.74 us
  transfers between devices with their start and end apart: 7, of which 1 were waited for; matrix products, arithmetic and copies ran while one was open for 5% of the time, Pallas kernels for 6%

profile of v6, /device:TPU:1, one launch (start us, length us, event | category | flops | bytes accessed | tf_op | source)
XLA Modules:
  0.0 159.3 jit_solution(5174784739207003901)
XLA Ops:
  7.2 0.0 copy-start.2
  7.2 0.0 copy-start.3
  7.2 0.0 all-gather.2.cloned.1.call-start
  7.2 1.8 %fusion.5 = (bf16[96,384]{1,0:T(8,128)(2,1)S(1)}, f32[96,384]{1,0:T(8,128)}, bf16[96,384]{1,0:T(8,128)(2,1)S(1)}) fusion(f32[96,384]{1,0:T(8,128)} %param.7, f32[96,384]{1,0:T(8,128)} %param.6), kind=kLoop, calls=%fused_computation.21 | loop fusion | flops 184320 | bytes 589824 | tf_op jit(solution)/shard_map/convert
  9.0 15.4 %all_gather.9 = bf16[384,768]{1,0:T(8,128)(2,1)} all-gather(bf16[96,768]{1,0:T(8,128)(2,1)S(1)} %pad_maximum_fusion), channel_id=1, replica_groups=mesh['yl'=4,'z'=8,'c'=2,'x'=4,'yh'=2] {'yl'}, dimensions={0}, use_global_device_ids=true | all-gather | bytes 737280 | tf_op jit(solution)/shard_map/all_gather | solution.py:152
  24.4 0.0 all-gather.2.cloned.1.call-update
  24.5 0.0 copy-done.2
  24.5 6.1 %collective-permute-start = (bf16[256,768]{1,0:T(8,128)(2,1)S(1)}, bf16[256,768]{1,0:T(8,128)(2,1)S(1)}, u32[]{:S(2)}, u32[]{:S(2)}) collective-permute-start(bf16[256,768]{1,0:T(8,128)(2,1)S(1)} %bitcast.25), channel_id=1, source_target_pairs={{0,1},{1,0},{2,3},{3,2},{4,5},{5,4},{6,7},{7,6},{8,9},{9,8},{10,11... | collective-permute-start | bytes 1179656 | tf_op jit(solution)/shard_map/ppermute | solution.py:156
  30.6 0.1 convert_reduce_fusion
  30.7 0.2 fusion.1
  31.0 0.6 broadcast_in_dim.4
  31.6 5.7 %all-to-all-start = ((f32[8,2,256]{2,1,0:T(2,128)}), f32[8,2,256]{2,1,0:T(2,128)S(1)}, u32[]{:S(2)}, u32[]{:S(2)}) async-start(f32[8,2,256]{2,1,0:T(2,128)} %broadcast_in_dim.4), calls=%async_computation | async-start | bytes 32768 | tf_op jit(solution)/shard_map/all_to_all | solution.py:141
  37.3 0.0 copy-done.3
  37.3 0.1 fusion.2.select_ref.refs_6_
  37.4 13.9 %all-to-all-done = f32[8,2,256]{2,1,0:T(2,128)S(1)} async-done(((f32[8,2,256]{2,1,0:T(2,128)}), f32[8,2,256]{2,1,0:T(2,128)S(1)}, u32[]{:S(2)}, u32[]{:S(2)}) %all-to-all-start) | async-done | bytes 16416 | tf_op jit(solution)/shard_map/all_to_all | solution.py:141
  51.3 0.0 collective-permute-done
  51.3 0.2 maximum_select_fusion.chunk_ref.refs_0_
  51.5 2.2 %collective-permute-start.1 = (bf16[256,1536]{1,0:T(8,128)(2,1)S(1)}, bf16[256,1536]{1,0:T(8,128)(2,1)S(1)}, u32[]{:S(2)}, u32[]{:S(2)}) collective-permute-start(bf16[256,1536]{1,0:T(8,128)(2,1)S(1)} %maximum_select_fusion.chunk_ref.refs_0_), channel_id=1, source_target_pairs={{0,2},{2,4},{4,6},{6,0},{1,3},{3,5},{5,7},{7,1},{8,10},{10,12},{12... | collective-permute-start | bytes 2359304 | tf_op jit(solution)/shard_map/ppermute | solution.py:162
  53.8 3.6 %collective-permute-start.2 = (bf16[256,1536]{1,0:T(8,128)(2,1)S(1)}, bf16[256,1536]{1,0:T(8,128)(2,1)S(1)}, u32[]{:S(2)}, u32[]{:S(2)}) collective-permute-start(bf16[256,1536]{1,0:T(8,128)(2,1)S(1)} %maximum_select_fusion.chunk_ref.refs_0_), channel_id=1, source_target_pairs={{0,4},{2,6},{4,0},{6,2},{1,5},{3,7},{5,1},{7,3},{8,12},{10,14},{12... | collective-permute-start | bytes 2359304 | tf_op jit(solution)/shard_map/ppermute | solution.py:162
  57.4 2.9 %collective-permute-start.3 = (bf16[256,1536]{1,0:T(8,128)(2,1)S(1)}, bf16[256,1536]{1,0:T(8,128)(2,1)S(1)}, u32[]{:S(2)}, u32[]{:S(2)}) collective-permute-start(bf16[256,1536]{1,0:T(8,128)(2,1)S(1)} %maximum_select_fusion.chunk_ref.refs_0_), channel_id=1, source_target_pairs={{0,6},{2,0},{4,2},{6,4},{1,7},{3,1},{5,3},{7,5},{8,14},{10,8},{12,... | collective-permute-start | bytes 2359304 | tf_op jit(solution)/shard_map/ppermute | solution.py:162
  60.4 0.1 copy.22.scale_ref.refs_5_
  60.5 0.1 copy.21.centre_ref.refs_4_
  60.7 0.4 shard_map.59
  61.1 0.0 copy-start.1
  61.1 0.7 copy-done.1
  61.8 1.9 %reshape.79 = bf16[64,16,96]{2,1,0:T(8,128)(2,1)} reshape(bf16[64,1536]{1,0:T(8,128)(2,1)} %copy-done.1) | data formatting | bytes 393216 | tf_op jit(solution)/shard_map/reshape | solution.py:175
  63.7 1.0 copy.32
  64.7 28.1 %all_to_all.20 = bf16[16,64,96]{2,1,0:T(8,128)(2,1)} all-to-all(bf16[16,64,96]{2,1,0:T(8,128)(2,1)S(1)} %bitcast.30), channel_id=1, replica_groups=mesh['yl'=4,'z'=8,'c'=2,'x'=4,'yh'=2] {'z','c'}, dimensions={0} | all-to-all | bytes 393216 | tf_op jit(solution)/shard_map/all_to_all | solution.py:176
  92.8 0.0 collective-permute-done.1.refs_1_
  92.8 0.0 collective-permute-done.2.refs_2_
  92.8 0.0 collective-permute-done.3.refs_3_
  92.8 1.8 %copy.24 = bf16[96,1024]{1,0:T(8,128)(2,1)} copy(bf16[96,1024]{0,1:T(8,128)(2,1)} %bitcast.29) | data formatting | bytes 393216 | tf_op jit(solution)/shard_map/optimization_barrier | solution.py:178
  94.6 1.9 %broadcast_in_dim.5 = bf16[4,96,1024]{2,1,0:T(8,128)(2,1)} broadcast(bf16[96,1024]{1,0:T(8,128)(2,1)} %copy.24), dimensions={1,2} | broadcast | bytes 983040 | tf_op jit(solution)/shard_map/broadcast_in_dim | solution.py:141
  96.5 4.4 %all-to-all-start.2 = ((bf16[4,96,1024]{2,1,0:T(8,128)(2,1)}), bf16[4,96,1024]{2,1,0:T(8,128)(2,1)}, u32[]{:S(2)}, u32[]{:S(2)}) async-start(bf16[4,96,1024]{2,1,0:T(8,128)(2,1)} %broadcast_in_dim.5), calls=%async_computation.2 | async-start | bytes 1572864 | tf_op jit(solution)/shard_map/all_to_all | solution.py:141
  100.9 1.8 %shard_map.60.refs_1_ = bf16[4,320,1536]{2,1,0:T(8,128)(2,1)S(1)} custom-call(bf16[256,1536]{1,0:T(8,128)(2,1)S(1)} %maximum_select_fusion.chunk_ref.refs_0_, bf16[256,1536]{1,0:T(8,128)(2,1)S(1)} %collective-permute-done.1.refs_1_, bf16[256,1536]{1,0:T(8,128)(2,1)S(1)} %collective-permute-done.2.refs_2_, ...), custom_call_target="tpu_custom_call" | custom-call | flops 201326592 | bytes 7077888 | tf_op jit(solution)/shard_map/pallas_call | solution.py:60
  102.7 0.0 copy-start
  102.7 2.0 %copy-done = bf16[4,320,1536]{2,1,0:T(8,128)(2,1)} copy-done((bf16[4,320,1536]{2,1,0:T(8,128)(2,1)}, bf16[4,320,1536]{2,1,0:T(8,128)(2,1)S(1)}, u32[]{:S(2)}) %copy-start) | copy-done | bytes 3932184
  104.6 0.0 all-gather.2.cloned.1.call-done
  104.7 7.7 %shard_map.61 = bf16[64,384]{1,0:T(8,128)(2,1)} custom-call(s32[1]{0:T(128)} %bitcast.10.refs_0_, bf16[4,320,1536]{2,1,0:T(8,128)(2,1)} %copy-done, bf16[16,4,96,768]{3,2,1,0:T(8,128)(2,1)} %bitcast.24), custom_call_target="tpu_custom_call" | custom-call | flops 1811939328 | bytes 13369344 | tf_op jit(solution)/shard_map/pallas_call | solution.py:111
  112.4 26.4 %all_gather.11 = bf16[1024,384]{1,0:T(8,128)(2,1)S(1)} all-gather(bf16[64,384]{1,0:T(8,128)(2,1)} %shard_map.61), channel_id=1, replica_groups=mesh['yl'=4,'z'=8,'c'=2,'x'=4,'yh'=2] {'z','c'}, dimensions={0}, use_global_device_ids=true | all-gather | bytes 835584 | tf_op jit(solution)/shard_map/all_gather | solution.py:184
  138.8 0.0 all-to-all-done.2
  138.8 1.7 %convolution_convert_fusion = bf16[384,384]{1,0:T(8,128)(2,1)S(1)} fusion(bf16[384,1024]{1,0:T(8,128)(2,1)} %bitcast.9, bf16[1024,384]{1,0:T(8,128)(2,1)S(1)} %all_gather.11), kind=kOutput, calls=%fused_computation | convolution fusion | flops 302137344 | bytes 1867776 | tf_op jit(solution)/shard_map/dot_general | solution.py:185
  140.5 11.2 %all_to_all.21 = bf16[4,96,384]{2,1,0:T(8,128)(2,1)S(1)} all-to-all(bf16[4,96,384]{2,1,0:T(8,128)(2,1)S(1)} %bitcast.31), channel_id=1, replica_groups=mesh['yl'=4,'z'=8,'c'=2,'x'=4,'yh'=2] {'yl'}, dimensions={0} | all-to-all | bytes 589824 | tf_op jit(solution)/shard_map/all_to_all | solution.py:186
  151.8 0.7 convert_reduce_fusion.1
  (7 shorter events, 0.1 us)
Async XLA Ops:
  7.2 17.3 %copy-start.2 = (bf16[1,256,768]{2,1,0:T(8,128)(2,1)S(1)}, bf16[1,256,768]{2,1,0:T(8,128)(2,1)}, u32[]{:S(2)}) copy-start(bf16[1,256,768]{2,1,0:T(8,128)(2,1)} %param.4) | copy-start | bytes 1179652
  7.2 30.1 %copy-start.3 = (s32[1,64]{1,0:T(1,128)S(1)}, s32[1,64]{1,0:T(1,128)}, u32[]{:S(2)}) copy-start(s32[1,64]{1,0:T(1,128)} %param.5) | copy-start | bytes 772
  7.2 97.5 %all-gather.2.cloned.1.call-start = ((), (), s32[]{:S(2)}) async-start(), calls=%async_computation.4 | async-start | bytes 10027008 | tf_op jit(solution)/shard_map/all_gather | solution.py:154
  24.5 26.9 %collective-permute-start = (bf16[256,768]{1,0:T(8,128)(2,1)S(1)}, bf16[256,768]{1,0:T(8,128)(2,1)S(1)}, u32[]{:S(2)}, u32[]{:S(2)}) collective-permute-start(bf16[256,768]{1,0:T(8,128)(2,1)S(1)} %bitcast.25), channel_id=1, source_target_pairs={{0,1},{1,0},{2,3},{3,2},{4,5},{5,4},{6,7},{7,6},{8,9},{9,8},{10,11... | collective-permute-start | bytes 1179656 | tf_op jit(solution)/shard_map/ppermute | solution.py:156
  31.6 19.7 %all-to-all-start = ((f32[8,2,256]{2,1,0:T(2,128)}), f32[8,2,256]{2,1,0:T(2,128)S(1)}, u32[]{:S(2)}, u32[]{:S(2)}) async-start(f32[8,2,256]{2,1,0:T(2,128)} %broadcast_in_dim.4), calls=%async_computation | async-start | bytes 32768 | tf_op jit(solution)/shard_map/all_to_all | solution.py:141
  51.5 41.2 %collective-permute-start.1 = (bf16[256,1536]{1,0:T(8,128)(2,1)S(1)}, bf16[256,1536]{1,0:T(8,128)(2,1)S(1)}, u32[]{:S(2)}, u32[]{:S(2)}) collective-permute-start(bf16[256,1536]{1,0:T(8,128)(2,1)S(1)} %maximum_select_fusion.chunk_ref.refs_0_), channel_id=1, source_target_pairs={{0,2},{2,4},{4,6},{6,0},{1,3},{3,5},{5,7},{7,1},{8,10},{10,12},{12... | collective-permute-start | bytes 2359304 | tf_op jit(solution)/shard_map/ppermute | solution.py:162
  53.8 39.0 %collective-permute-start.2 = (bf16[256,1536]{1,0:T(8,128)(2,1)S(1)}, bf16[256,1536]{1,0:T(8,128)(2,1)S(1)}, u32[]{:S(2)}, u32[]{:S(2)}) collective-permute-start(bf16[256,1536]{1,0:T(8,128)(2,1)S(1)} %maximum_select_fusion.chunk_ref.refs_0_), channel_id=1, source_target_pairs={{0,4},{2,6},{4,0},{6,2},{1,5},{3,7},{5,1},{7,3},{8,12},{10,14},{12... | collective-permute-start | bytes 2359304 | tf_op jit(solution)/shard_map/ppermute | solution.py:162
  57.4 35.4 %collective-permute-start.3 = (bf16[256,1536]{1,0:T(8,128)(2,1)S(1)}, bf16[256,1536]{1,0:T(8,128)(2,1)S(1)}, u32[]{:S(2)}, u32[]{:S(2)}) collective-permute-start(bf16[256,1536]{1,0:T(8,128)(2,1)S(1)} %maximum_select_fusion.chunk_ref.refs_0_), channel_id=1, source_target_pairs={{0,6},{2,0},{4,2},{6,4},{1,7},{3,1},{5,3},{7,5},{8,14},{10,8},{12,... | collective-permute-start | bytes 2359304 | tf_op jit(solution)/shard_map/ppermute | solution.py:162
  61.1 0.7 copy-start.1
  96.5 42.4 %all-to-all-start.2 = ((bf16[4,96,1024]{2,1,0:T(8,128)(2,1)}), bf16[4,96,1024]{2,1,0:T(8,128)(2,1)}, u32[]{:S(2)}, u32[]{:S(2)}) async-start(bf16[4,96,1024]{2,1,0:T(8,128)(2,1)} %broadcast_in_dim.5), calls=%async_computation.2 | async-start | bytes 1572864 | tf_op jit(solution)/shard_map/all_to_all | solution.py:141
  102.7 2.0 %copy-start = (bf16[4,320,1536]{2,1,0:T(8,128)(2,1)}, bf16[4,320,1536]{2,1,0:T(8,128)(2,1)S(1)}, u32[]{:S(2)}) copy-start(bf16[4,320,1536]{2,1,0:T(8,128)(2,1)S(1)} %shard_map.60.refs_1_) | copy-start | bytes 11796484
Sparse Core Ops, SparseCore 0:
  24.6 77.6 all-gather.1

commit v7 on v4

v7 whole, which is shorter than its diff:
```python
import math

import jax
import jax.numpy as jnp
from jax import lax
from jax.experimental import pallas as pl
from jax.experimental.pallas import tpu as pltpu
from jax.sharding import Mesh
from jax.sharding import PartitionSpec as P

D = 6144
Y, Z, C, X, H = 4, 8, 2, 4, 2
BF, F32 = jnp.bfloat16, jnp.float32
MB = 1024 * 1024


def normalise_kernel(rows, x_ref, *refs):
    count = (len(refs) - 6)
    chunk_refs, (centre_ref, scale_ref, select_ref, normed_ref, pieces_ref, picked_ref) = refs[:count], refs[count:]
    patches = centre_ref.shape[0]
    step = pl.program_id(0)
    for k, chunk_ref in enumerate(chunk_refs):

        @pl.when(lax.rem(x_ref[0] + count - step, count) == k)
        def _(chunk_ref=chunk_ref):
            normed = ((chunk_ref[...].astype(F32) - centre_ref[...]) * scale_ref[...]).astype(BF)
            picked = jnp.dot(select_ref[...], normed, preferred_element_type=F32)
            normed_ref[0, :patches] = normed
            normed_ref[0, patches:] = picked.astype(BF)
            picked_ref[...] = picked

    for i in range(count):

        @pl.when(step == i)
        def _(i=i):
            for piece in range(pieces_ref.shape[0]):
                pieces_ref[piece, :, i * rows : (i + 1) * rows] = picked_ref[:, piece * rows : (piece + 1) * rows].astype(BF)


def normalise(chunks, x, centre, scale, select, rows):
    n = len(chunks)
    patches, width = chunks[0].shape
    keep = select.shape[0]
    whole = lambda k, x: (0, 0)

    def body(*refs):
        normalise_kernel(rows, *refs)

    return pl.pallas_call(
        body,
        grid_spec=pltpu.PrefetchScalarGridSpec(
            num_scalar_prefetch=1,
            grid=(n,),
            in_specs=[pl.BlockSpec((patches, width), whole)] * n
            + [pl.BlockSpec((patches, 1), whole)] * 2
            + [pl.BlockSpec((keep, patches), whole)],
            out_specs=[
                pl.BlockSpec((1, patches + keep, width), lambda k, x: (k, 0, 0)),
                pl.BlockSpec((width // rows, keep, n * rows), lambda k, x: (0, 0, 0)),
            ],
            scratch_shapes=[pltpu.VMEM((keep, width), F32)],
        ),
        out_shape=[
            jax.ShapeDtypeStruct((n, patches + keep, width), BF),
            jax.ShapeDtypeStruct((width // rows, keep, n * rows), BF),
        ],
        compiler_params=pltpu.CompilerParams(vmem_limit_bytes=32 * MB),
        cost_estimate=pl.CostEstimate(
            flops=2 * n * keep * patches * width, bytes_accessed=4 * n * width * (patches + keep), transcendentals=0
        ),
    )(x, *chunks, centre, scale, select)


def error_kernel(factor, patches, normed_ref, panel_ref, error_ref, teacher_acc, student_acc):
    step = pl.program_id(0)
    columns = error_ref.shape[1]
    panel = panel_ref[:, 0].reshape(-1, 2 * columns)
    teacher_part = jnp.dot(normed_ref[0], panel[:, :columns], preferred_element_type=F32)
    student_part = jnp.dot(normed_ref[0, patches:], panel[:, columns:], preferred_element_type=F32)

    @pl.when(step == 0)
    def _():
        teacher_acc[...] = teacher_part
        student_acc[...] = student_part

    @pl.when(step > 0)
    def _():
        teacher_acc[...] += teacher_part
        student_acc[...] += student_part

    @pl.when(step == pl.num_programs(0) - 1)
    def _():
        teacher = teacher_acc[:patches]
        centre = jnp.mean(teacher, axis=0, keepdims=True)
        centred = teacher - centre
        spread = jnp.mean(centred * centred, axis=0, keepdims=True)
        target = (teacher_acc[patches:] - centre) * lax.rsqrt(spread + 1e-05)
        error_ref[...] = ((student_acc[...] - target) * factor).astype(BF)


def make_error(normed, patches, panels, factor):
    n, rows_in, width = normed.shape
    keep = rows_in - patches
    blocks, _, rows, both = panels.shape
    columns = both // 2

    def body(*refs):
        error_kernel(factor, patches, *refs)

    return pl.pallas_call(
        body,
        grid=(n,),
        in_specs=[
            pl.BlockSpec((1, rows_in, width), lambda k: (k, 0, 0)),
            pl.BlockSpec((blocks, 1, rows, both), lambda k: (0, k, 0, 0)),
        ],
        out_specs=pl.BlockSpec((keep, columns), lambda k: (0, 0)),
        out_shape=jax.ShapeDtypeStruct((keep, columns), BF),
        scratch_shapes=[pltpu.VMEM((rows_in, columns), F32), pltpu.VMEM((keep, columns), F32)],
        compiler_params=pltpu.CompilerParams(vmem_limit_bytes=56 * MB),
        cost_estimate=pl.CostEstimate(
            flops=2 * n * width * (rows_in + keep) * columns,
            bytes_accessed=2 * n * width * (rows_in + both),
            transcendentals=columns,
        ),
    )(normed, panels)


def ring(size, step):
    return [(i, (i + step) % size) for i in range(size)]


def spread_to_all(values, axes, size):
    return lax.all_to_all(jnp.broadcast_to(values[None], (size, *values.shape)), axes, split_axis=0, concat_axis=0)


def shards(images, keep_index, teacher_weight, student_weight):
    patches, slice_width = images.shape[1:]
    keep_count = keep_index.shape[1]
    rows, columns = teacher_weight.shape
    image = images[0]

    teacher_next = 0.999 * teacher_weight + (1.0 - 0.999) * student_weight
    panel = jnp.concatenate([teacher_next, student_weight], axis=1).astype(BF)
    panels = lax.all_gather(panel, "yl", axis=0, tiled=True)
    panels, image = lax.optimization_barrier((panels, image))
    panels = lax.all_gather(panels, ("z", "c"), axis=0, tiled=True).reshape(Z * C, Y, rows, 2 * columns)

    other = lax.ppermute(image, "yh", ring(H, 1))
    pair = jnp.where(
        lax.axis_index("yh") == 0,
        jnp.concatenate([image, other], axis=1),
        jnp.concatenate([other, image], axis=1),
    )
    arrived = [lax.ppermute(pair, "x", ring(X, step)) for step in range(1, X)]

    floats = image.astype(F32)
    own_mean = jnp.mean(floats, axis=1)
    own_moment = jnp.sum(jnp.square(floats - own_mean[:, None]), axis=1)
    parts = spread_to_all(jnp.stack([own_mean, own_moment]), ("x", "yh"), X * H)
    centre = jnp.mean(parts[:, 0], axis=0)
    moment = jnp.sum(parts[:, 1], axis=0) + slice_width * jnp.sum(jnp.square(parts[:, 0] - centre), axis=0)
    scale = lax.rsqrt(moment / D + 1e-06)
    centre, scale = centre[:, None], scale[:, None]

    select = (keep_index[0][:, None] == lax.broadcasted_iota(jnp.int32, (keep_count, patches), 1)).astype(BF)

    x = lax.axis_index("x").reshape(1)
    normed, pieces = normalise([pair, *arrived], x, centre, scale, select, rows)
    owned = lax.all_to_all(pieces, ("z", "c"), split_axis=0, concat_axis=0).reshape(Z * C * keep_count, Y * rows)

    total_kept = keep_count * Y * Z * C
    error = make_error(normed, patches, panels, 1.0 / math.sqrt(total_kept))
    errors = lax.all_gather(error, ("z", "c"), axis=0, tiled=True)
    partial = lax.dot_general(owned, errors, (((0,), (0,)), ((), ())), preferred_element_type=F32)
    partial = partial.astype(BF).reshape(Y, rows, columns)
    partial = lax.all_to_all(partial, "yl", split_axis=0, concat_axis=0)
    student_grad = jnp.sum(partial.astype(F32), axis=0)
    return (teacher_next, student_grad)


def solution(mesh):
    fine = Mesh(mesh.devices.reshape(Y, Z, C, X, H), ("yl", "z", "c", "x", "yh"))
    rows, cols = ("yl", "z", "c"), ("x", "yh")
    return jax.shard_map(
        shards,
        mesh=fine,
        in_specs=(P(rows, None, cols), P(rows, None), P(rows, cols), P(rows, cols)),
        out_specs=(P(rows, cols), P(rows, cols)),
        check_vma=False,
    )
```

time: 160 us -> 162 us (1.012)
  blocking collectives: 80.8 us -> 52.8 us
  waiting for transfers between devices: 17 us -> 35.4 us
  starting transfers between devices: 25.4 us -> 39.9 us
  local copies, waits for them, and re-layouts: 5.21 us -> 2.86 us
    all_to_all x1 -> x0, blocking collectives: 28 us -> none  [shards(): pieces = lax.all_to_all(pieces, ('z', 'c'), split_axis=0, concat_axis=0)]
    ppermute x3, waiting for transfers between devices: 3.03 us -> 29 us  [shards(): arrived = [lax.ppermute(pair, 'x', ring(X, step)) for step in range(1, X)]]
    all_to_all x2 -> x1, waiting for transfers between devices: 13.9 us -> 0.01 us  [spread_to_all(): lax.all_to_all(jnp.broadcast_to(values[None], (size, *values.shape)), axe...]
    all_to_all x0 -> x1, starting transfers between devices: none -> 12.1 us  [shards(): lax.all_to_all(pieces, ('z', 'c'), split_axis=0, concat_axis=0)]
    ppermute x3, starting transfers between devices: 8.77 us -> 15.9 us  [shards(): arrived = [lax.ppermute(pair, 'x', ring(X, step)) for step in range(1, X)]]
    ppermute x1, waiting for transfers between devices: 0.01 us -> 6.33 us  [shards(): other = lax.ppermute(image, 'yh', ring(H, 1))]
    all_to_all x2 -> x1, starting transfers between devices: 10.5 us -> 5.68 us  [spread_to_all(): lax.all_to_all(jnp.broadcast_to(values[None], (size, *values.shape)), axe...]
    pallas_call x5 -> x2, Pallas kernels: 12.4 us -> 11.2 us  [the longest x1 7.75 us: make_error(): pl.pallas_call(body, grid=(n,), in_specs=[pl.BlockSpec((1, rows_in, width...]
  transfers between devices with their start and end apart: 7 -> 7, of which waited for: 2 -> 4; matrix products, arithmetic and copies ran while one was open for 2% -> 1% of each run, Pallas kernels for 8% -> 7%
where the time goes in v7:
time: 162 us; the launch traced here: 161 us
  blocking collectives  52.8 us (33%)
  starting transfers between devices  39.9 us (25%)
  waiting for transfers between devices  35.4 us (22%)
  between operations  14.2 us (9%)
  Pallas kernels  11.2 us (7%)
  other arithmetic  3.87 us (2%)
  local copies, waits for them, and re-layouts  2.86 us (2%)
    ppermute x3, waiting for transfers between devices, shards(): arrived = [lax.ppermute(pair, 'x', ring(X, step)) for step in range(1, X)]  29 us
    all_gather x1, blocking collectives, shards(): errors = lax.all_gather(error, ('z', 'c'), axis=0, tiled=True)  26.2 us
    ppermute x3, starting transfers between devices, shards(): arrived = [lax.ppermute(pair, 'x', ring(X, step)) for step in range(1, X)]  15.9 us
    all_gather x1, blocking collectives, shards(): panels = lax.all_gather(panel, 'yl', axis=0, tiled=True)  15.4 us
    all_to_all x1, starting transfers between devices, shards(): lax.all_to_all(pieces, ('z', 'c'), split_axis=0, concat_axis=0)  12.1 us
    all_to_all x1, blocking collectives, shards(): partial = lax.all_to_all(partial, 'yl', split_axis=0, concat_axis=0)  11.2 us
    pallas_call x1, Pallas kernels, make_error(): pl.pallas_call(body, grid=(n,), in_specs=[pl.BlockSpec((1, rows_in, width...  7.75 us
    ppermute x1, waiting for transfers between devices, shards(): other = lax.ppermute(image, 'yh', ring(H, 1))  6.33 us
  transfers between devices with their start and end apart: 7, of which 4 were waited for; matrix products, arithmetic and copies ran while one was open for 1% of the time, Pallas kernels for 7%

profile of v7, /device:TPU:1, one launch (start us, length us, event | category | flops | bytes accessed | tf_op | source)
XLA Modules:
  0.0 160.8 jit_solution(10371522530886929031)
XLA Ops:
  7.2 0.0 copy-start.1
  7.2 0.0 all-gather.2.cloned.1.call-start
  7.2 1.8 %fusion.5 = (bf16[96,384]{1,0:T(8,128)(2,1)S(1)}, f32[96,384]{1,0:T(8,128)}, bf16[96,384]{1,0:T(8,128)(2,1)S(1)}) fusion(f32[96,384]{1,0:T(8,128)} %param.7, f32[96,384]{1,0:T(8,128)} %param.6), kind=kLoop, calls=%fused_computation.20 | loop fusion | flops 184320 | bytes 589824 | tf_op jit(solution)/shard_map/convert
  9.0 15.4 %all_gather.9 = bf16[384,768]{1,0:T(8,128)(2,1)} all-gather(bf16[96,768]{1,0:T(8,128)(2,1)S(1)} %pad_maximum_fusion), channel_id=1, replica_groups=mesh['yl'=4,'z'=8,'c'=2,'x'=4,'yh'=2] {'yl'}, dimensions={0}, use_global_device_ids=true | all-gather | bytes 737280 | tf_op jit(solution)/shard_map/all_gather | solution.py:145
  24.4 0.0 all-gather.2.cloned.1.call-update
  24.5 0.0 copy-done.1
  24.5 6.1 %collective-permute-start = (bf16[256,768]{1,0:T(8,128)(2,1)S(1)}, bf16[256,768]{1,0:T(8,128)(2,1)S(1)}, u32[]{:S(2)}, u32[]{:S(2)}) collective-permute-start(bf16[256,768]{1,0:T(8,128)(2,1)S(1)} %bitcast.19), channel_id=1, source_target_pairs={{0,1},{1,0},{2,3},{3,2},{4,5},{5,4},{6,7},{7,6},{8,9},{9,8},{10,11... | collective-permute-start | bytes 1179656 | tf_op jit(solution)/shard_map/ppermute | solution.py:149
  30.6 0.1 convert_reduce_fusion
  30.7 0.2 fusion.1
  31.0 0.6 broadcast_in_dim.2
  31.6 5.7 %all-to-all-start = ((f32[8,2,256]{2,1,0:T(2,128)}), f32[8,2,256]{2,1,0:T(2,128)S(1)}, u32[]{:S(2)}, u32[]{:S(2)}) async-start(f32[8,2,256]{2,1,0:T(2,128)} %broadcast_in_dim.2), calls=%async_computation | async-start | bytes 32768 | tf_op jit(solution)/shard_map/all_to_all | solution.py:134
  37.3 6.3 %collective-permute-done = bf16[256,768]{1,0:T(8,128)(2,1)S(1)} collective-permute-done((bf16[256,768]{1,0:T(8,128)(2,1)S(1)}, bf16[256,768]{1,0:T(8,128)(2,1)S(1)}, u32[]{:S(2)}, u32[]{:S(2)}) %collective-permute-start) | collective-permute-done | bytes 393248 | tf_op jit(solution)/shard_map/ppermute | solution.py:149
  43.6 0.2 maximum_select_fusion.refs_1_
  43.8 8.5 %collective-permute-start.1 = (bf16[256,1536]{1,0:T(8,128)(2,1)S(1)}, bf16[256,1536]{1,0:T(8,128)(2,1)S(1)}, u32[]{:S(2)}, u32[]{:S(2)}) collective-permute-start(bf16[256,1536]{1,0:T(8,128)(2,1)S(1)} %maximum_select_fusion.refs_1_), channel_id=1, source_target_pairs={{0,2},{2,4},{4,6},{6,0},{1,3},{3,5},{5,7},{7,1},{8,10},{10,12},{12... | collective-permute-start | bytes 2359304 | tf_op jit(solution)/shard_map/ppermute | solution.py:155
  52.3 4.4 %collective-permute-start.2 = (bf16[256,1536]{1,0:T(8,128)(2,1)S(1)}, bf16[256,1536]{1,0:T(8,128)(2,1)S(1)}, u32[]{:S(2)}, u32[]{:S(2)}) collective-permute-start(bf16[256,1536]{1,0:T(8,128)(2,1)S(1)} %maximum_select_fusion.refs_1_), channel_id=1, source_target_pairs={{0,4},{2,6},{4,0},{6,2},{1,5},{3,7},{5,1},{7,3},{8,12},{10,14},{12... | collective-permute-start | bytes 2359304 | tf_op jit(solution)/shard_map/ppermute | solution.py:155
  56.7 3.1 %collective-permute-start.3 = (bf16[256,1536]{1,0:T(8,128)(2,1)S(1)}, bf16[256,1536]{1,0:T(8,128)(2,1)S(1)}, u32[]{:S(2)}, u32[]{:S(2)}) collective-permute-start(bf16[256,1536]{1,0:T(8,128)(2,1)S(1)} %maximum_select_fusion.refs_1_), channel_id=1, source_target_pairs={{0,6},{2,0},{4,2},{6,4},{1,7},{3,1},{5,3},{7,5},{8,14},{10,8},{12,... | collective-permute-start | bytes 2359304 | tf_op jit(solution)/shard_map/ppermute | solution.py:155
  59.7 0.7 fusion.2.refs_7_
  60.5 0.0 all-to-all-done
  60.5 0.1 copy.12.refs_5_
  60.7 0.1 copy.13.refs_6_
  60.9 8.3 %collective-permute-done.1.refs_2_ = bf16[256,1536]{1,0:T(8,128)(2,1)S(1)} collective-permute-done((bf16[256,1536]{1,0:T(8,128)(2,1)S(1)}, bf16[256,1536]{1,0:T(8,128)(2,1)S(1)}, u32[]{:S(2)}, u32[]{:S(2)}) %collective-permute-start.1) | collective-permute-done | bytes 786464 | tf_op jit(solution)/shard_map/ppermute | solution.py:155
  69.1 17.7 %collective-permute-done.2.refs_3_ = bf16[256,1536]{1,0:T(8,128)(2,1)S(1)} collective-permute-done((bf16[256,1536]{1,0:T(8,128)(2,1)S(1)}, bf16[256,1536]{1,0:T(8,128)(2,1)S(1)}, u32[]{:S(2)}, u32[]{:S(2)}) %collective-permute-start.2) | collective-permute-done | bytes 786464 | tf_op jit(solution)/shard_map/ppermute | solution.py:155
  86.8 3.0 %collective-permute-done.3.refs_4_ = bf16[256,1536]{1,0:T(8,128)(2,1)S(1)} collective-permute-done((bf16[256,1536]{1,0:T(8,128)(2,1)S(1)}, bf16[256,1536]{1,0:T(8,128)(2,1)S(1)}, u32[]{:S(2)}, u32[]{:S(2)}) %collective-permute-start.3) | collective-permute-done | bytes 786464 | tf_op jit(solution)/shard_map/ppermute | solution.py:155
  89.9 3.5 %shard_map.59 = (bf16[4,320,1536]{2,1,0:T(8,128)(2,1)S(1)}, bf16[16,64,384]{2,1,0:T(8,128)(2,1)}) custom-call(s32[1]{0:T(128)} %bitcast.refs_0_, bf16[256,1536]{1,0:T(8,128)(2,1)S(1)} %maximum_select_fusion.refs_1_, bf16[256,1536]{1,0:T(8,128)(2,1)S(1)} %collective-permute-done.1.refs_2_, bf16[256,1536]{1,0:T(8,128)(2,1)S(1)} %collective-permute-done.2.refs_3_, ...), custom_call_target="tpu_custom_call" | custom-call | flops 201326592 | bytes 7864320 | tf_op jit(solution)/shard_map/pallas_call | solution.py:49
  93.4 0.0 copy-start
  93.4 2.0 %copy-done = bf16[4,320,1536]{2,1,0:T(8,128)(2,1)} copy-done((bf16[4,320,1536]{2,1,0:T(8,128)(2,1)}, bf16[4,320,1536]{2,1,0:T(8,128)(2,1)S(1)}, u32[]{:S(2)}) %copy-start) | copy-done | bytes 3932184
  95.3 12.1 %all-to-all-start.1 = ((bf16[16,64,384]{2,1,0:T(8,128)(2,1)}), bf16[16,64,384]{2,1,0:T(8,128)(2,1)S(1)}, u32[]{:S(2)}, u32[]{:S(2)}) async-start(bf16[16,64,384]{2,1,0:T(8,128)(2,1)} %get-tuple-element.7), calls=%async_computation.1 | async-start | bytes 1572864 | tf_op jit(solution)/shard_map/all_to_all | solution.py:170
  107.5 0.0 all-gather.2.cloned.1.call-done
  107.5 7.7 %shard_map.60 = bf16[64,384]{1,0:T(8,128)(2,1)} custom-call(bf16[4,320,1536]{2,1,0:T(8,128)(2,1)} %copy-done, bf16[16,4,96,768]{3,2,1,0:T(8,128)(2,1)} %bitcast.18), custom_call_target="tpu_custom_call" | custom-call | flops 1811939328 | bytes 13369344 | tf_op jit(solution)/shard_map/pallas_call | solution.py:110
  115.3 26.2 %all_gather.11 = bf16[1024,384]{1,0:T(8,128)(2,1)S(1)} all-gather(bf16[64,384]{1,0:T(8,128)(2,1)} %shard_map.60), channel_id=1, replica_groups=mesh['yl'=4,'z'=8,'c'=2,'x'=4,'yh'=2] {'z','c'}, dimensions={0}, use_global_device_ids=true | all-gather | bytes 835584 | tf_op jit(solution)/shard_map/all_gather | solution.py:174
  141.4 0.0 all-to-all-done.1
  141.4 0.6 convolution_convert_fusion
  142.0 11.2 %all_to_all.15 = bf16[4,96,384]{2,1,0:T(8,128)(2,1)S(1)} all-to-all(bf16[4,96,384]{2,1,0:T(8,128)(2,1)S(1)} %bitcast.24), channel_id=1, replica_groups=mesh['yl'=4,'z'=8,'c'=2,'x'=4,'yh'=2] {'yl'}, dimensions={0} | all-to-all | bytes 589824 | tf_op jit(solution)/shard_map/all_to_all | solution.py:177
  153.3 0.7 convert_reduce_fusion.1
  (7 shorter events, 0.1 us)
Async XLA Ops:
  7.2 17.3 %copy-start.1 = (bf16[1,256,768]{2,1,0:T(8,128)(2,1)S(1)}, bf16[1,256,768]{2,1,0:T(8,128)(2,1)}, u32[]{:S(2)}) copy-start(bf16[1,256,768]{2,1,0:T(8,128)(2,1)} %param.4) | copy-start | bytes 1179652
  7.2 100.3 %all-gather.2.cloned.1.call-start = ((), (), s32[]{:S(2)}) async-start(), calls=%async_computation.3 | async-start | bytes 10027008 | tf_op jit(solution)/shard_map/all_gather | solution.py:147
  24.5 19.1 %collective-permute-start = (bf16[256,768]{1,0:T(8,128)(2,1)S(1)}, bf16[256,768]{1,0:T(8,128)(2,1)S(1)}, u32[]{:S(2)}, u32[]{:S(2)}) collective-permute-start(bf16[256,768]{1,0:T(8,128)(2,1)S(1)} %bitcast.19), channel_id=1, source_target_pairs={{0,1},{1,0},{2,3},{3,2},{4,5},{5,4},{6,7},{7,6},{8,9},{9,8},{10,11... | collective-permute-start | bytes 1179656 | tf_op jit(solution)/shard_map/ppermute | solution.py:149
  31.6 28.9 %all-to-all-start = ((f32[8,2,256]{2,1,0:T(2,128)}), f32[8,2,256]{2,1,0:T(2,128)S(1)}, u32[]{:S(2)}, u32[]{:S(2)}) async-start(f32[8,2,256]{2,1,0:T(2,128)} %broadcast_in_dim.2), calls=%async_computation | async-start | bytes 32768 | tf_op jit(solution)/shard_map/all_to_all | solution.py:134
  43.8 25.4 %collective-permute-start.1 = (bf16[256,1536]{1,0:T(8,128)(2,1)S(1)}, bf16[256,1536]{1,0:T(8,128)(2,1)S(1)}, u32[]{:S(2)}, u32[]{:S(2)}) collective-permute-start(bf16[256,1536]{1,0:T(8,128)(2,1)S(1)} %maximum_select_fusion.refs_1_), channel_id=1, source_target_pairs={{0,2},{2,4},{4,6},{6,0},{1,3},{3,5},{5,7},{7,1},{8,10},{10,12},{12... | collective-permute-start | bytes 2359304 | tf_op jit(solution)/shard_map/ppermute | solution.py:155
  52.3 34.6 %collective-permute-start.2 = (bf16[256,1536]{1,0:T(8,128)(2,1)S(1)}, bf16[256,1536]{1,0:T(8,128)(2,1)S(1)}, u32[]{:S(2)}, u32[]{:S(2)}) collective-permute-start(bf16[256,1536]{1,0:T(8,128)(2,1)S(1)} %maximum_select_fusion.refs_1_), channel_id=1, source_target_pairs={{0,4},{2,6},{4,0},{6,2},{1,5},{3,7},{5,1},{7,3},{8,12},{10,14},{12... | collective-permute-start | bytes 2359304 | tf_op jit(solution)/shard_map/ppermute | solution.py:155
  56.7 33.2 %collective-permute-start.3 = (bf16[256,1536]{1,0:T(8,128)(2,1)S(1)}, bf16[256,1536]{1,0:T(8,128)(2,1)S(1)}, u32[]{:S(2)}, u32[]{:S(2)}) collective-permute-start(bf16[256,1536]{1,0:T(8,128)(2,1)S(1)} %maximum_select_fusion.refs_1_), channel_id=1, source_target_pairs={{0,6},{2,0},{4,2},{6,4},{1,7},{3,1},{5,3},{7,5},{8,14},{10,8},{12,... | collective-permute-start | bytes 2359304 | tf_op jit(solution)/shard_map/ppermute | solution.py:155
  93.4 2.0 %copy-start = (bf16[4,320,1536]{2,1,0:T(8,128)(2,1)}, bf16[4,320,1536]{2,1,0:T(8,128)(2,1)S(1)}, u32[]{:S(2)}) copy-start(bf16[4,320,1536]{2,1,0:T(8,128)(2,1)S(1)} %get-tuple-element.8.refs_0_) | copy-start | bytes 11796484
  95.3 46.1 %all-to-all-start.1 = ((bf16[16,64,384]{2,1,0:T(8,128)(2,1)}), bf16[16,64,384]{2,1,0:T(8,128)(2,1)S(1)}, u32[]{:S(2)}, u32[]{:S(2)}) async-start(bf16[16,64,384]{2,1,0:T(8,128)(2,1)} %get-tuple-element.7), calls=%async_computation.1 | async-start | bytes 1572864 | tf_op jit(solution)/shard_map/all_to_all | solution.py:170
Sparse Core Ops, SparseCore 0:
  24.6 71.9 all-gather.1

commit v8 on v6

--- a/solution.py
+++ b/solution.py
@@ -176,9 +176,10 @@
     pieces = lax.all_to_all(pieces, ("z", "c"), split_axis=0, concat_axis=0)
     pieces = pieces.reshape(Z * C * keep_count, rows).T
     pieces, arrived = lax.optimization_barrier((pieces, arrived))
+    normed = normalise([pair, *arrived], centre, scale, select)
+    pieces, normed = lax.optimization_barrier((pieces, normed))
     owned = spread_to_all(pieces, "x", X).reshape(Y * rows, Z * C * keep_count)
 
-    normed = normalise([pair, *arrived], centre, scale, select)
     total_kept = keep_count * Y * Z * C
     error = make_error(normed, patches, lax.axis_index("x").reshape(1), panels, 1.0 / math.sqrt(total_kept))
     errors = lax.all_gather(error, ("z", "c"), axis=0, tiled=True)

time: 161 us -> 158 us (0.981)
  local copies, waits for them, and re-layouts: 10.2 us -> 8.53 us
  transfers between devices with their start and end apart: 7 -> 7, of which waited for: 1 -> 1; matrix products, arithmetic and copies ran while one was open for 5% -> 4% of each run, Pallas kernels for 6% -> 6%
where the time goes in v8:
time: 158 us; the launch traced here: 156 us
  blocking collectives  80.8 us (51%)
  starting transfers between devices  25 us (16%)
  between operations  14.2 us (9%)
  waiting for transfers between devices  14 us (9%)
  Pallas kernels  9.98 us (6%)
  local copies, waits for them, and re-layouts  8.53 us (5%)
  other arithmetic  3.22 us (2%)
    all_to_all x1, blocking collectives, shards(): pieces = lax.all_to_all(pieces, ('z', 'c'), split_axis=0, concat_axis=0)  28.1 us
    all_gather x1, blocking collectives, shards(): errors = lax.all_gather(error, ('z', 'c'), axis=0, tiled=True)  26.1 us
    all_gather x1, blocking collectives, shards(): panels = lax.all_gather(panel, 'yl', axis=0, tiled=True)  15.4 us
    all_to_all x2, waiting for transfers between devices, spread_to_all(): lax.all_to_all(jnp.broadcast_to(values[None], (size, *values.shape)), axe...  13.9 us
    all_to_all x1, blocking collectives, shards(): partial = lax.all_to_all(partial, 'yl', split_axis=0, concat_axis=0)  11.2 us
    all_to_all x2, starting transfers between devices, spread_to_all(): lax.all_to_all(jnp.broadcast_to(values[None], (size, *values.shape)), axe...  10.1 us
    ppermute x3, starting transfers between devices, shards(): arrived = [lax.ppermute(pair, 'x', ring(X, step)) for step in range(1, X)]  8.77 us
    pallas_call x1, Pallas kernels, make_error(): pl.pallas_call(body, grid_spec=pltpu.PrefetchScalarGridSpec(num_scalar_pr...  7.74 us
  transfers between devices with their start and end apart: 7, of which 1 were waited for; matrix products, arithmetic and copies ran while one was open for 4% of the time, Pallas kernels for 6%

profile of v8, /device:TPU:1, one launch (start us, length us, event | category | flops | bytes accessed | tf_op | source)
XLA Modules:
  0.0 156.3 jit_solution(14562927564627660265)
XLA Ops:
  7.2 0.0 copy-start.2
  7.2 0.0 copy-start.3
  7.2 0.0 all-gather.2.cloned.1.call-start
  7.2 1.8 %fusion.5 = (bf16[96,384]{1,0:T(8,128)(2,1)S(1)}, f32[96,384]{1,0:T(8,128)}, bf16[96,384]{1,0:T(8,128)(2,1)S(1)}) fusion(f32[96,384]{1,0:T(8,128)} %param.7, f32[96,384]{1,0:T(8,128)} %param.6), kind=kLoop, calls=%fused_computation.21 | loop fusion | flops 184320 | bytes 589824 | tf_op jit(solution)/shard_map/convert
  9.0 15.4 %all_gather.9 = bf16[384,768]{1,0:T(8,128)(2,1)} all-gather(bf16[96,768]{1,0:T(8,128)(2,1)S(1)} %pad_maximum_fusion), channel_id=1, replica_groups=mesh['yl'=4,'z'=8,'c'=2,'x'=4,'yh'=2] {'yl'}, dimensions={0}, use_global_device_ids=true | all-gather | bytes 737280 | tf_op jit(solution)/shard_map/all_gather | solution.py:152
  24.4 0.0 all-gather.2.cloned.1.call-update
  24.5 0.0 copy-done.2
  24.5 6.1 %collective-permute-start = (bf16[256,768]{1,0:T(8,128)(2,1)S(1)}, bf16[256,768]{1,0:T(8,128)(2,1)S(1)}, u32[]{:S(2)}, u32[]{:S(2)}) collective-permute-start(bf16[256,768]{1,0:T(8,128)(2,1)S(1)} %bitcast.25), channel_id=1, source_target_pairs={{0,1},{1,0},{2,3},{3,2},{4,5},{5,4},{6,7},{7,6},{8,9},{9,8},{10,11... | collective-permute-start | bytes 1179656 | tf_op jit(solution)/shard_map/ppermute | solution.py:156
  30.6 0.1 convert_reduce_fusion
  30.7 0.2 fusion.1
  31.0 0.6 broadcast_in_dim.4
  31.6 5.7 %all-to-all-start = ((f32[8,2,256]{2,1,0:T(2,128)}), f32[8,2,256]{2,1,0:T(2,128)S(1)}, u32[]{:S(2)}, u32[]{:S(2)}) async-start(f32[8,2,256]{2,1,0:T(2,128)} %broadcast_in_dim.4), calls=%async_computation | async-start | bytes 32768 | tf_op jit(solution)/shard_map/all_to_all | solution.py:141
  37.3 0.0 copy-done.3
  37.3 0.1 fusion.2.select_ref.refs_6_
  37.4 13.9 %all-to-all-done = f32[8,2,256]{2,1,0:T(2,128)S(1)} async-done(((f32[8,2,256]{2,1,0:T(2,128)}), f32[8,2,256]{2,1,0:T(2,128)S(1)}, u32[]{:S(2)}, u32[]{:S(2)}) %all-to-all-start) | async-done | bytes 16416 | tf_op jit(solution)/shard_map/all_to_all | solution.py:141
  51.3 0.0 collective-permute-done
  51.3 0.2 maximum_select_fusion.chunk_ref.refs_0_
  51.5 2.2 %collective-permute-start.1 = (bf16[256,1536]{1,0:T(8,128)(2,1)S(1)}, bf16[256,1536]{1,0:T(8,128)(2,1)S(1)}, u32[]{:S(2)}, u32[]{:S(2)}) collective-permute-start(bf16[256,1536]{1,0:T(8,128)(2,1)S(1)} %maximum_select_fusion.chunk_ref.refs_0_), channel_id=1, source_target_pairs={{0,2},{2,4},{4,6},{6,0},{1,3},{3,5},{5,7},{7,1},{8,10},{10,12},{12... | collective-permute-start | bytes 2359304 | tf_op jit(solution)/shard_map/ppermute | solution.py:162
  53.8 3.6 %collective-permute-start.2 = (bf16[256,1536]{1,0:T(8,128)(2,1)S(1)}, bf16[256,1536]{1,0:T(8,128)(2,1)S(1)}, u32[]{:S(2)}, u32[]{:S(2)}) collective-permute-start(bf16[256,1536]{1,0:T(8,128)(2,1)S(1)} %maximum_select_fusion.chunk_ref.refs_0_), channel_id=1, source_target_pairs={{0,4},{2,6},{4,0},{6,2},{1,5},{3,7},{5,1},{7,3},{8,12},{10,14},{12... | collective-permute-start | bytes 2359304 | tf_op jit(solution)/shard_map/ppermute | solution.py:162
  57.4 2.9 %collective-permute-start.3 = (bf16[256,1536]{1,0:T(8,128)(2,1)S(1)}, bf16[256,1536]{1,0:T(8,128)(2,1)S(1)}, u32[]{:S(2)}, u32[]{:S(2)}) collective-permute-start(bf16[256,1536]{1,0:T(8,128)(2,1)S(1)} %maximum_select_fusion.chunk_ref.refs_0_), channel_id=1, source_target_pairs={{0,6},{2,0},{4,2},{6,4},{1,7},{3,1},{5,3},{7,5},{8,14},{10,8},{12,... | collective-permute-start | bytes 2359304 | tf_op jit(solution)/shard_map/ppermute | solution.py:162
  60.4 0.1 copy.22.scale_ref.refs_5_
  60.5 0.1 copy.21.centre_ref.refs_4_
  60.7 0.4 shard_map.59
  61.1 0.0 copy-start.1
  61.1 0.7 copy-done.1
  61.8 1.9 %reshape.79 = bf16[64,16,96]{2,1,0:T(8,128)(2,1)} reshape(bf16[64,1536]{1,0:T(8,128)(2,1)} %copy-done.1) | data formatting | bytes 393216 | tf_op jit(solution)/shard_map/reshape | solution.py:175
  63.7 1.0 copy.32
  64.7 28.1 %all_to_all.20 = bf16[16,64,96]{2,1,0:T(8,128)(2,1)} all-to-all(bf16[16,64,96]{2,1,0:T(8,128)(2,1)S(1)} %bitcast.30), channel_id=1, replica_groups=mesh['yl'=4,'z'=8,'c'=2,'x'=4,'yh'=2] {'z','c'}, dimensions={0} | all-to-all | bytes 393216 | tf_op jit(solution)/shard_map/all_to_all | solution.py:176
  92.8 0.0 collective-permute-done.1.refs_1_
  92.8 0.0 collective-permute-done.2.refs_2_
  92.8 0.0 collective-permute-done.3.refs_3_
  92.8 1.8 %shard_map.60.refs_1_ = bf16[4,320,1536]{2,1,0:T(8,128)(2,1)S(1)} custom-call(bf16[256,1536]{1,0:T(8,128)(2,1)S(1)} %maximum_select_fusion.chunk_ref.refs_0_, bf16[256,1536]{1,0:T(8,128)(2,1)S(1)} %collective-permute-done.1.refs_1_, bf16[256,1536]{1,0:T(8,128)(2,1)S(1)} %collective-permute-done.2.refs_2_, ...), custom_call_target="tpu_custom_call" | custom-call | flops 201326592 | bytes 7077888 | tf_op jit(solution)/shard_map/pallas_call | solution.py:60
  94.6 0.0 copy-start
  94.6 2.0 %copy-done = bf16[4,320,1536]{2,1,0:T(8,128)(2,1)} copy-done((bf16[4,320,1536]{2,1,0:T(8,128)(2,1)}, bf16[4,320,1536]{2,1,0:T(8,128)(2,1)S(1)}, u32[]{:S(2)}) %copy-start) | copy-done | bytes 3932184
  96.6 1.1 copy.26
  97.7 1.0 broadcast_in_dim.5
  98.6 4.4 %all-to-all-start.2 = ((bf16[4,96,1024]{2,1,0:T(8,128)(2,1)}), bf16[4,96,1024]{2,1,0:T(8,128)(2,1)S(1)}, u32[]{:S(2)}, u32[]{:S(2)}) async-start(bf16[4,96,1024]{2,1,0:T(8,128)(2,1)} %broadcast_in_dim.5), calls=%async_computation.2 | async-start | bytes 1572864 | tf_op jit(solution)/shard_map/all_to_all | solution.py:141
  103.1 0.0 all-gather.2.cloned.1.call-done
  103.1 7.7 %shard_map.61 = bf16[64,384]{1,0:T(8,128)(2,1)} custom-call(s32[1]{0:T(128)} %bitcast.10.refs_0_, bf16[4,320,1536]{2,1,0:T(8,128)(2,1)} %copy-done, bf16[16,4,96,768]{3,2,1,0:T(8,128)(2,1)} %bitcast.24), custom_call_target="tpu_custom_call" | custom-call | flops 1811939328 | bytes 13369344 | tf_op jit(solution)/shard_map/pallas_call | solution.py:111
  110.8 26.1 %all_gather.11 = bf16[1024,384]{1,0:T(8,128)(2,1)S(1)} all-gather(bf16[64,384]{1,0:T(8,128)(2,1)} %shard_map.61), channel_id=1, replica_groups=mesh['yl'=4,'z'=8,'c'=2,'x'=4,'yh'=2] {'z','c'}, dimensions={0}, use_global_device_ids=true | all-gather | bytes 835584 | tf_op jit(solution)/shard_map/all_gather | solution.py:185
  136.9 0.0 all-to-all-done.2
  136.9 0.6 convolution_convert_fusion
  137.5 11.2 %all_to_all.21 = bf16[4,96,384]{2,1,0:T(8,128)(2,1)S(1)} all-to-all(bf16[4,96,384]{2,1,0:T(8,128)(2,1)S(1)} %bitcast.32), channel_id=1, replica_groups=mesh['yl'=4,'z'=8,'c'=2,'x'=4,'yh'=2] {'yl'}, dimensions={0} | all-to-all | bytes 589824 | tf_op jit(solution)/shard_map/all_to_all | solution.py:187
  148.7 0.7 convert_reduce_fusion.1
  (7 shorter events, 0.1 us)
Async XLA Ops:
  7.2 17.3 %copy-start.2 = (bf16[1,256,768]{2,1,0:T(8,128)(2,1)S(1)}, bf16[1,256,768]{2,1,0:T(8,128)(2,1)}, u32[]{:S(2)}) copy-start(bf16[1,256,768]{2,1,0:T(8,128)(2,1)} %param.4) | copy-start | bytes 1179652
  7.2 30.1 %copy-start.3 = (s32[1,64]{1,0:T(1,128)S(1)}, s32[1,64]{1,0:T(1,128)}, u32[]{:S(2)}) copy-start(s32[1,64]{1,0:T(1,128)} %param.5) | copy-start | bytes 772
  7.2 95.9 %all-gather.2.cloned.1.call-start = ((), (), s32[]{:S(2)}) async-start(), calls=%async_computation.4 | async-start | bytes 10027008 | tf_op jit(solution)/shard_map/all_gather | solution.py:154
  24.5 26.9 %collective-permute-start = (bf16[256,768]{1,0:T(8,128)(2,1)S(1)}, bf16[256,768]{1,0:T(8,128)(2,1)S(1)}, u32[]{:S(2)}, u32[]{:S(2)}) collective-permute-start(bf16[256,768]{1,0:T(8,128)(2,1)S(1)} %bitcast.25), channel_id=1, source_target_pairs={{0,1},{1,0},{2,3},{3,2},{4,5},{5,4},{6,7},{7,6},{8,9},{9,8},{10,11... | collective-permute-start | bytes 1179656 | tf_op jit(solution)/shard_map/ppermute | solution.py:156
  31.6 19.7 %all-to-all-start = ((f32[8,2,256]{2,1,0:T(2,128)}), f32[8,2,256]{2,1,0:T(2,128)S(1)}, u32[]{:S(2)}, u32[]{:S(2)}) async-start(f32[8,2,256]{2,1,0:T(2,128)} %broadcast_in_dim.4), calls=%async_computation | async-start | bytes 32768 | tf_op jit(solution)/shard_map/all_to_all | solution.py:141
  51.5 41.2 %collective-permute-start.1 = (bf16[256,1536]{1,0:T(8,128)(2,1)S(1)}, bf16[256,1536]{1,0:T(8,128)(2,1)S(1)}, u32[]{:S(2)}, u32[]{:S(2)}) collective-permute-start(bf16[256,1536]{1,0:T(8,128)(2,1)S(1)} %maximum_select_fusion.chunk_ref.refs_0_), channel_id=1, source_target_pairs={{0,2},{2,4},{4,6},{6,0},{1,3},{3,5},{5,7},{7,1},{8,10},{10,12},{12... | collective-permute-start | bytes 2359304 | tf_op jit(solution)/shard_map/ppermute | solution.py:162
  53.8 39.0 %collective-permute-start.2 = (bf16[256,1536]{1,0:T(8,128)(2,1)S(1)}, bf16[256,1536]{1,0:T(8,128)(2,1)S(1)}, u32[]{:S(2)}, u32[]{:S(2)}) collective-permute-start(bf16[256,1536]{1,0:T(8,128)(2,1)S(1)} %maximum_select_fusion.chunk_ref.refs_0_), channel_id=1, source_target_pairs={{0,4},{2,6},{4,0},{6,2},{1,5},{3,7},{5,1},{7,3},{8,12},{10,14},{12... | collective-permute-start | bytes 2359304 | tf_op jit(solution)/shard_map/ppermute | solution.py:162
  57.4 35.4 %collective-permute-start.3 = (bf16[256,1536]{1,0:T(8,128)(2,1)S(1)}, bf16[256,1536]{1,0:T(8,128)(2,1)S(1)}, u32[]{:S(2)}, u32[]{:S(2)}) collective-permute-start(bf16[256,1536]{1,0:T(8,128)(2,1)S(1)} %maximum_select_fusion.chunk_ref.refs_0_), channel_id=1, source_target_pairs={{0,6},{2,0},{4,2},{6,4},{1,7},{3,1},{5,3},{7,5},{8,14},{10,8},{12,... | collective-permute-start | bytes 2359304 | tf_op jit(solution)/shard_map/ppermute | solution.py:162
  61.1 0.7 copy-start.1
  94.6 2.0 %copy-start = (bf16[4,320,1536]{2,1,0:T(8,128)(2,1)}, bf16[4,320,1536]{2,1,0:T(8,128)(2,1)S(1)}, u32[]{:S(2)}) copy-start(bf16[4,320,1536]{2,1,0:T(8,128)(2,1)S(1)} %shard_map.60.refs_1_) | copy-start | bytes 11796484
  98.6 38.3 %all-to-all-start.2 = ((bf16[4,96,1024]{2,1,0:T(8,128)(2,1)}), bf16[4,96,1024]{2,1,0:T(8,128)(2,1)S(1)}, u32[]{:S(2)}, u32[]{:S(2)}) async-start(bf16[4,96,1024]{2,1,0:T(8,128)(2,1)} %broadcast_in_dim.5), calls=%async_computation.2 | async-start | bytes 1572864 | tf_op jit(solution)/shard_map/all_to_all | solution.py:141
Sparse Core Ops, SparseCore 0:
  24.6 77.6 all-gather.1

commit v9 on v8

--- a/solution.py
+++ b/solution.py
@@ -70,6 +70,22 @@
             flops=2 * n * keep * patches * width, bytes_accessed=2 * n * width * (2 * patches + keep), transcendentals=0
         ),
     )(*chunks, centre, scale, select)
+
+
+def turn_kernel(rows_ref, copies_ref):
+    turned = rows_ref[...].reshape(-1, rows_ref.shape[-1]).T
+    for k in range(copies_ref.shape[0]):
+        copies_ref[k] = turned
+
+
+def turned_copies(values, count):
+    width = values.shape[-1]
+    return pl.pallas_call(
+        turn_kernel,
+        out_shape=jax.ShapeDtypeStruct((count, width, values.size // width), values.dtype),
+        compiler_params=pltpu.CompilerParams(vmem_limit_bytes=16 * MB),
+        cost_estimate=pl.CostEstimate(flops=0, bytes_accessed=2 * (count + 1) * values.size, transcendentals=0),
+    )(values)
 
 
 def error_kernel(factor, patches, x_ref, normed_ref, panel_ref, error_ref, teacher_acc, student_acc):
@@ -174,11 +190,11 @@
 
     pieces = pick(pair, centre, scale, select).reshape(keep_count, Z * C, rows).transpose(1, 0, 2)
     pieces = lax.all_to_all(pieces, ("z", "c"), split_axis=0, concat_axis=0)
-    pieces = pieces.reshape(Z * C * keep_count, rows).T
+    copies = turned_copies(pieces, X)
     pieces, arrived = lax.optimization_barrier((pieces, arrived))
     normed = normalise([pair, *arrived], centre, scale, select)
-    pieces, normed = lax.optimization_barrier((pieces, normed))
-    owned = spread_to_all(pieces, "x", X).reshape(Y * rows, Z * C * keep_count)
+    copies, _ = lax.optimization_barrier((copies, normed))
+    owned = lax.all_to_all(copies, "x", split_axis=0, concat_axis=0).reshape(Y * rows, Z * C * keep_count)
 
     total_kept = keep_count * Y * Z * C
     error = make_error(normed, patches, lax.axis_index("x").reshape(1), panels, 1.0 / math.sqrt(total_kept))

time: 158 us -> 156 us (0.987)
  local copies, waits for them, and re-layouts: 8.53 us -> 6.48 us
    all_to_all x2 -> x1, starting transfers between devices: 10.1 us -> 5.68 us  [spread_to_all(): lax.all_to_all(jnp.broadcast_to(values[None], (size, *values.shape)), axe...]
    all_to_all x0 -> x1, starting transfers between devices: none -> 3.49 us  [shards(): lax.all_to_all(copies, 'x', split_axis=0, concat_axis=0)]
    all_to_all x2 -> x1, waiting for transfers between devices: 13.9 us -> 13.9 us  [spread_to_all(): lax.all_to_all(jnp.broadcast_to(values[None], (size, *values.shape)), axe...]
  transfers between devices with their start and end apart: 7 -> 7, of which waited for: 1 -> 2; matrix products, arithmetic and copies ran while one was open for 4% -> 3% of each run, Pallas kernels for 6% -> 7%
where the time goes in v9:
time: 156 us; the launch traced here: 154 us
  blocking collectives  79.4 us (51%)
  starting transfers between devices  24.1 us (15%)
  waiting for transfers between devices  15.2 us (10%)
  between operations  14.2 us (9%)
  Pallas kernels  11 us (7%)
  local copies, waits for them, and re-layouts  6.48 us (4%)
  other arithmetic  3.22 us (2%)
    all_to_all x1, blocking collectives, shards(): pieces = lax.all_to_all(pieces, ('z', 'c'), split_axis=0, concat_axis=0)  27.9 us
    all_gather x1, blocking collectives, shards(): errors = lax.all_gather(error, ('z', 'c'), axis=0, tiled=True)  24.9 us
    all_gather x1, blocking collectives, shards(): panels = lax.all_gather(panel, 'yl', axis=0, tiled=True)  15.4 us
    all_to_all x1, waiting for transfers between devices, spread_to_all(): lax.all_to_all(jnp.broadcast_to(values[None], (size, *values.shape)), axe...  13.9 us
    all_to_all x1, blocking collectives, shards(): partial = lax.all_to_all(partial, 'yl', split_axis=0, concat_axis=0)  11.2 us
    ppermute x3, starting transfers between devices, shards(): arrived = [lax.ppermute(pair, 'x', ring(X, step)) for step in range(1, X)]  8.77 us
    pallas_call x1, Pallas kernels, make_error(): pl.pallas_call(body, grid_spec=pltpu.PrefetchScalarGridSpec(num_scalar_pr...  7.74 us
    ppermute x1, starting transfers between devices, shards(): other = lax.ppermute(image, 'yh', ring(H, 1))  6.09 us
  transfers between devices with their start and end apart: 7, of which 2 were waited for; matrix products, arithmetic and copies ran while one was open for 3% of the time, Pallas kernels for 7%

profile of v9, /device:TPU:1, one launch (start us, length us, event | category | flops | bytes accessed | tf_op | source)
XLA Modules:
  0.0 154.2 jit_solution(5588318158251880217)
XLA Ops:
  7.2 0.0 copy-start.2
  7.2 0.0 copy-start.3
  7.2 0.0 all-gather.2.cloned.1.call-start
  7.2 1.8 %fusion.5 = (bf16[96,384]{1,0:T(8,128)(2,1)S(1)}, f32[96,384]{1,0:T(8,128)}, bf16[96,384]{1,0:T(8,128)(2,1)S(1)}) fusion(f32[96,384]{1,0:T(8,128)} %param.7, f32[96,384]{1,0:T(8,128)} %param.6), kind=kLoop, calls=%fused_computation.21 | loop fusion | flops 184320 | bytes 589824 | tf_op jit(solution)/shard_map/convert
  9.0 15.4 %all_gather.9 = bf16[384,768]{1,0:T(8,128)(2,1)} all-gather(bf16[96,768]{1,0:T(8,128)(2,1)S(1)} %pad_maximum_fusion), channel_id=1, replica_groups=mesh['yl'=4,'z'=8,'c'=2,'x'=4,'yh'=2] {'yl'}, dimensions={0}, use_global_device_ids=true | all-gather | bytes 737280 | tf_op jit(solution)/shard_map/all_gather | solution.py:168
  24.4 0.0 all-gather.2.cloned.1.call-update
  24.5 0.0 copy-done.2
  24.5 6.1 %collective-permute-start = (bf16[256,768]{1,0:T(8,128)(2,1)S(1)}, bf16[256,768]{1,0:T(8,128)(2,1)S(1)}, u32[]{:S(2)}, u32[]{:S(2)}) collective-permute-start(bf16[256,768]{1,0:T(8,128)(2,1)S(1)} %bitcast.22), channel_id=1, source_target_pairs={{0,1},{1,0},{2,3},{3,2},{4,5},{5,4},{6,7},{7,6},{8,9},{9,8},{10,11... | collective-permute-start | bytes 1179656 | tf_op jit(solution)/shard_map/ppermute | solution.py:172
  30.6 0.1 convert_reduce_fusion
  30.7 0.2 fusion.1
  31.0 0.6 broadcast_in_dim.2
  31.6 5.7 %all-to-all-start = ((f32[8,2,256]{2,1,0:T(2,128)}), f32[8,2,256]{2,1,0:T(2,128)S(1)}, u32[]{:S(2)}, u32[]{:S(2)}) async-start(f32[8,2,256]{2,1,0:T(2,128)} %broadcast_in_dim.2), calls=%async_computation | async-start | bytes 32768 | tf_op jit(solution)/shard_map/all_to_all | solution.py:157
  37.3 0.0 copy-done.3
  37.3 0.1 fusion.2.select_ref.refs_6_
  37.4 13.9 %all-to-all-done = f32[8,2,256]{2,1,0:T(2,128)S(1)} async-done(((f32[8,2,256]{2,1,0:T(2,128)}), f32[8,2,256]{2,1,0:T(2,128)S(1)}, u32[]{:S(2)}, u32[]{:S(2)}) %all-to-all-start) | async-done | bytes 16416 | tf_op jit(solution)/shard_map/all_to_all | solution.py:157
  51.3 0.0 collective-permute-done
  51.3 0.2 maximum_select_fusion.chunk_ref.refs_0_
  51.5 2.2 %collective-permute-start.1 = (bf16[256,1536]{1,0:T(8,128)(2,1)S(1)}, bf16[256,1536]{1,0:T(8,128)(2,1)S(1)}, u32[]{:S(2)}, u32[]{:S(2)}) collective-permute-start(bf16[256,1536]{1,0:T(8,128)(2,1)S(1)} %maximum_select_fusion.chunk_ref.refs_0_), channel_id=1, source_target_pairs={{0,2},{2,4},{4,6},{6,0},{1,3},{3,5},{5,7},{7,1},{8,10},{10,12},{12... | collective-permute-start | bytes 2359304 | tf_op jit(solution)/shard_map/ppermute | solution.py:178
  53.8 3.6 %collective-permute-start.2 = (bf16[256,1536]{1,0:T(8,128)(2,1)S(1)}, bf16[256,1536]{1,0:T(8,128)(2,1)S(1)}, u32[]{:S(2)}, u32[]{:S(2)}) collective-permute-start(bf16[256,1536]{1,0:T(8,128)(2,1)S(1)} %maximum_select_fusion.chunk_ref.refs_0_), channel_id=1, source_target_pairs={{0,4},{2,6},{4,0},{6,2},{1,5},{3,7},{5,1},{7,3},{8,12},{10,14},{12... | collective-permute-start | bytes 2359304 | tf_op jit(solution)/shard_map/ppermute | solution.py:178
  57.4 2.9 %collective-permute-start.3 = (bf16[256,1536]{1,0:T(8,128)(2,1)S(1)}, bf16[256,1536]{1,0:T(8,128)(2,1)S(1)}, u32[]{:S(2)}, u32[]{:S(2)}) collective-permute-start(bf16[256,1536]{1,0:T(8,128)(2,1)S(1)} %maximum_select_fusion.chunk_ref.refs_0_), channel_id=1, source_target_pairs={{0,6},{2,0},{4,2},{6,4},{1,7},{3,1},{5,3},{7,5},{8,14},{10,8},{12,... | collective-permute-start | bytes 2359304 | tf_op jit(solution)/shard_map/ppermute | solution.py:178
  60.4 0.1 copy.19.scale_ref.refs_5_
  60.5 0.1 copy.18.centre_ref.refs_4_
  60.7 0.4 shard_map.59
  61.1 0.0 copy-start.1
  61.1 0.7 copy-done.1
  61.8 1.9 %reshape.75 = bf16[64,16,96]{2,1,0:T(8,128)(2,1)} reshape(bf16[64,1536]{1,0:T(8,128)(2,1)} %copy-done.1) | data formatting | bytes 393216 | tf_op jit(solution)/shard_map/reshape | solution.py:191
  63.7 1.0 copy.28
  64.7 27.9 %all_to_all.20.rows_ref = bf16[16,64,96]{2,1,0:T(8,128)(2,1)S(1)} all-to-all(bf16[16,64,96]{2,1,0:T(8,128)(2,1)S(1)} %bitcast.26), channel_id=1, replica_groups=mesh['yl'=4,'z'=8,'c'=2,'x'=4,'yh'=2] {'z','c'}, dimensions={0} | all-to-all | bytes 393216 | tf_op jit(solution)/shard_map/all_to_all | solution.py:192
  92.7 1.0 shard_map.60
  93.7 0.0 collective-permute-done.1.refs_1_
  93.7 0.0 collective-permute-done.2.refs_2_
  93.7 0.0 collective-permute-done.3.refs_3_
  93.7 1.8 %shard_map.61.refs_1_ = bf16[4,320,1536]{2,1,0:T(8,128)(2,1)S(1)} custom-call(bf16[256,1536]{1,0:T(8,128)(2,1)S(1)} %maximum_select_fusion.chunk_ref.refs_0_, bf16[256,1536]{1,0:T(8,128)(2,1)S(1)} %collective-permute-done.1.refs_1_, bf16[256,1536]{1,0:T(8,128)(2,1)S(1)} %collective-permute-done.2.refs_2_, ...), custom_call_target="tpu_custom_call" | custom-call | flops 201326592 | bytes 7077888 | tf_op jit(solution)/shard_map/pallas_call | solution.py:60
  95.5 0.0 copy-start
  95.5 2.0 %copy-done = bf16[4,320,1536]{2,1,0:T(8,128)(2,1)} copy-done((bf16[4,320,1536]{2,1,0:T(8,128)(2,1)}, bf16[4,320,1536]{2,1,0:T(8,128)(2,1)S(1)}, u32[]{:S(2)}) %copy-start) | copy-done | bytes 3932184
  97.5 3.5 %all-to-all-start.2 = ((bf16[4,96,1024]{2,1,0:T(8,128)(2,1)}), bf16[4,96,1024]{2,1,0:T(8,128)(2,1)S(1)}, u32[]{:S(2)}, u32[]{:S(2)}) async-start(bf16[4,96,1024]{2,1,0:T(8,128)(2,1)} %shard_map.60), calls=%async_computation.2 | async-start | bytes 1572864 | tf_op jit(solution)/shard_map/all_to_all | solution.py:197
  101.0 1.2 all-gather.2.cloned.1.call-done
  102.3 7.7 %shard_map.62 = bf16[64,384]{1,0:T(8,128)(2,1)} custom-call(s32[1]{0:T(128)} %bitcast.8.refs_0_, bf16[4,320,1536]{2,1,0:T(8,128)(2,1)} %copy-done, bf16[16,4,96,768]{3,2,1,0:T(8,128)(2,1)} %bitcast.21), custom_call_target="tpu_custom_call" | custom-call | flops 1811939328 | bytes 13369344 | tf_op jit(solution)/shard_map/pallas_call | solution.py:127
  110.0 24.9 %all_gather.11 = bf16[1024,384]{1,0:T(8,128)(2,1)S(1)} all-gather(bf16[64,384]{1,0:T(8,128)(2,1)} %shard_map.62), channel_id=1, replica_groups=mesh['yl'=4,'z'=8,'c'=2,'x'=4,'yh'=2] {'z','c'}, dimensions={0}, use_global_device_ids=true | all-gather | bytes 835584 | tf_op jit(solution)/shard_map/all_gather | solution.py:201
  134.8 0.0 all-to-all-done.2
  134.8 0.6 convolution_convert_fusion
  135.4 11.2 %all_to_all.21 = bf16[4,96,384]{2,1,0:T(8,128)(2,1)S(1)} all-to-all(bf16[4,96,384]{2,1,0:T(8,128)(2,1)S(1)} %bitcast.28), channel_id=1, replica_groups=mesh['yl'=4,'z'=8,'c'=2,'x'=4,'yh'=2] {'yl'}, dimensions={0} | all-to-all | bytes 589824 | tf_op jit(solution)/shard_map/all_to_all | solution.py:203
  146.7 0.7 convert_reduce_fusion.1
  (7 shorter events, 0.1 us)
Async XLA Ops:
  7.2 17.3 %copy-start.2 = (bf16[1,256,768]{2,1,0:T(8,128)(2,1)S(1)}, bf16[1,256,768]{2,1,0:T(8,128)(2,1)}, u32[]{:S(2)}) copy-start(bf16[1,256,768]{2,1,0:T(8,128)(2,1)} %param.4) | copy-start | bytes 1179652
  7.2 30.1 %copy-start.3 = (s32[1,64]{1,0:T(1,128)S(1)}, s32[1,64]{1,0:T(1,128)}, u32[]{:S(2)}) copy-start(s32[1,64]{1,0:T(1,128)} %param.5) | copy-start | bytes 772
  7.2 95.1 %all-gather.2.cloned.1.call-start = ((), (), s32[]{:S(2)}) async-start(), calls=%async_computation.4 | async-start | bytes 10027008 | tf_op jit(solution)/shard_map/all_gather | solution.py:170
  24.5 26.9 %collective-permute-start = (bf16[256,768]{1,0:T(8,128)(2,1)S(1)}, bf16[256,768]{1,0:T(8,128)(2,1)S(1)}, u32[]{:S(2)}, u32[]{:S(2)}) collective-permute-start(bf16[256,768]{1,0:T(8,128)(2,1)S(1)} %bitcast.22), channel_id=1, source_target_pairs={{0,1},{1,0},{2,3},{3,2},{4,5},{5,4},{6,7},{7,6},{8,9},{9,8},{10,11... | collective-permute-start | bytes 1179656 | tf_op jit(solution)/shard_map/ppermute | solution.py:172
  31.6 19.7 %all-to-all-start = ((f32[8,2,256]{2,1,0:T(2,128)}), f32[8,2,256]{2,1,0:T(2,128)S(1)}, u32[]{:S(2)}, u32[]{:S(2)}) async-start(f32[8,2,256]{2,1,0:T(2,128)} %broadcast_in_dim.2), calls=%async_computation | async-start | bytes 32768 | tf_op jit(solution)/shard_map/all_to_all | solution.py:157
  51.5 42.2 %collective-permute-start.1 = (bf16[256,1536]{1,0:T(8,128)(2,1)S(1)}, bf16[256,1536]{1,0:T(8,128)(2,1)S(1)}, u32[]{:S(2)}, u32[]{:S(2)}) collective-permute-start(bf16[256,1536]{1,0:T(8,128)(2,1)S(1)} %maximum_select_fusion.chunk_ref.refs_0_), channel_id=1, source_target_pairs={{0,2},{2,4},{4,6},{6,0},{1,3},{3,5},{5,7},{7,1},{8,10},{10,12},{12... | collective-permute-start | bytes 2359304 | tf_op jit(solution)/shard_map/ppermute | solution.py:178
  53.8 39.9 %collective-permute-start.2 = (bf16[256,1536]{1,0:T(8,128)(2,1)S(1)}, bf16[256,1536]{1,0:T(8,128)(2,1)S(1)}, u32[]{:S(2)}, u32[]{:S(2)}) collective-permute-start(bf16[256,1536]{1,0:T(8,128)(2,1)S(1)} %maximum_select_fusion.chunk_ref.refs_0_), channel_id=1, source_target_pairs={{0,4},{2,6},{4,0},{6,2},{1,5},{3,7},{5,1},{7,3},{8,12},{10,14},{12... | collective-permute-start | bytes 2359304 | tf_op jit(solution)/shard_map/ppermute | solution.py:178
  57.4 36.3 %collective-permute-start.3 = (bf16[256,1536]{1,0:T(8,128)(2,1)S(1)}, bf16[256,1536]{1,0:T(8,128)(2,1)S(1)}, u32[]{:S(2)}, u32[]{:S(2)}) collective-permute-start(bf16[256,1536]{1,0:T(8,128)(2,1)S(1)} %maximum_select_fusion.chunk_ref.refs_0_), channel_id=1, source_target_pairs={{0,6},{2,0},{4,2},{6,4},{1,7},{3,1},{5,3},{7,5},{8,14},{10,8},{12,... | collective-permute-start | bytes 2359304 | tf_op jit(solution)/shard_map/ppermute | solution.py:178
  61.1 0.7 copy-start.1
  95.5 2.0 %copy-start = (bf16[4,320,1536]{2,1,0:T(8,128)(2,1)}, bf16[4,320,1536]{2,1,0:T(8,128)(2,1)S(1)}, u32[]{:S(2)}) copy-start(bf16[4,320,1536]{2,1,0:T(8,128)(2,1)S(1)} %shard_map.61.refs_1_) | copy-start | bytes 11796484
  97.5 37.3 %all-to-all-start.2 = ((bf16[4,96,1024]{2,1,0:T(8,128)(2,1)}), bf16[4,96,1024]{2,1,0:T(8,128)(2,1)S(1)}, u32[]{:S(2)}, u32[]{:S(2)}) async-start(bf16[4,96,1024]{2,1,0:T(8,128)(2,1)} %shard_map.60), calls=%async_computation.2 | async-start | bytes 1572864 | tf_op jit(solution)/shard_map/all_to_all | solution.py:197
Sparse Core Ops, SparseCore 0:
  24.6 77.6 all-gather.1

commit v10 on v9

--- a/solution.py
+++ b/solution.py
@@ -23,16 +23,21 @@
     return jnp.dot(select_ref[...], normed, preferred_element_type=F32).astype(BF)
 
 
-def pick_kernel(chunk_ref, centre_ref, scale_ref, select_ref, picked_ref):
-    picked_ref[...] = kept(select_ref, normalised(chunk_ref, centre_ref, scale_ref))
-
-
-def pick(chunk, centre, scale, select):
+def pick_kernel(chunk_ref, centre_ref, scale_ref, select_ref, pieces_ref, picked_ref):
+    normed = normalised(chunk_ref, centre_ref, scale_ref)
+    picked_ref[...] = jnp.dot(select_ref[...], normed, preferred_element_type=F32)
+    count, _, rows = pieces_ref.shape
+    for piece in range(count):
+        pieces_ref[piece] = picked_ref[:, piece * rows : (piece + 1) * rows].astype(BF)
+
+
+def pick(chunk, centre, scale, select, rows):
     patches, width = chunk.shape
     keep = select.shape[0]
     return pl.pallas_call(
         pick_kernel,
-        out_shape=jax.ShapeDtypeStruct((keep, width), BF),
+        out_shape=jax.ShapeDtypeStruct((width // rows, keep, rows), BF),
+        scratch_shapes=[pltpu.VMEM((keep, width), F32)],
         compiler_params=pltpu.CompilerParams(vmem_limit_bytes=16 * MB),
         cost_estimate=pl.CostEstimate(
             flops=2 * keep * patches * width, bytes_accessed=2 * width * (patches + keep), transcendentals=0
@@ -188,7 +193,7 @@
 
     select = (keep_index[0][:, None] == lax.broadcasted_iota(jnp.int32, (keep_count, patches), 1)).astype(BF)
 
-    pieces = pick(pair, centre, scale, select).reshape(keep_count, Z * C, rows).transpose(1, 0, 2)
+    pieces = pick(pair, centre, scale, select, rows)
     pieces = lax.all_to_all(pieces, ("z", "c"), split_axis=0, concat_axis=0)
     copies = turned_copies(pieces, X)
     pieces, arrived = lax.optimization_barrier((pieces, arrived))

time: 156 us -> 155 us (level)
  local copies, waits for them, and re-layouts: 6.48 us -> 2.85 us
  waiting for transfers between devices: 15.2 us -> 17.5 us
    reshape x2 -> x0, local copies, waits for them, and re-layouts: 2.94 us -> none  [shards(): pick(pair, centre, scale, select).reshape(keep_count, Z * C, rows)]
    ppermute x3, waiting for transfers between devices: 0.01 us -> 2.27 us  [shards(): arrived = [lax.ppermute(pair, 'x', ring(X, step)) for step in range(1, X)]]
  transfers between devices with their start and end apart: 7 -> 7, of which waited for: 2 -> 3; matrix products, arithmetic and copies ran while one was open for 3% -> 1% of each run, Pallas kernels for 7% -> 7%
where the time goes in v10:
time: 155 us; the launch traced here: 154 us
  blocking collectives  79.5 us (51%)
  starting transfers between devices  25.4 us (16%)
  waiting for transfers between devices  17.5 us (11%)
  between operations  14.2 us (9%)
  Pallas kernels  11.1 us (7%)
  other arithmetic  3.22 us (2%)
  local copies, waits for them, and re-layouts  2.85 us (2%)
    all_to_all x1, blocking collectives, shards(): pieces = lax.all_to_all(pieces, ('z', 'c'), split_axis=0, concat_axis=0)  27.9 us
    all_gather x1, blocking collectives, shards(): errors = lax.all_gather(error, ('z', 'c'), axis=0, tiled=True)  24.9 us
    all_gather x1, blocking collectives, shards(): panels = lax.all_gather(panel, 'yl', axis=0, tiled=True)  15.4 us
    all_to_all x1, waiting for transfers between devices, spread_to_all(): lax.all_to_all(jnp.broadcast_to(values[None], (size, *values.shape)), axe...  13.9 us
    all_to_all x1, blocking collectives, shards(): partial = lax.all_to_all(partial, 'yl', split_axis=0, concat_axis=0)  11.2 us
    ppermute x3, starting transfers between devices, shards(): arrived = [lax.ppermute(pair, 'x', ring(X, step)) for step in range(1, X)]  8.77 us
    pallas_call x1, Pallas kernels, make_error(): pl.pallas_call(body, grid_spec=pltpu.PrefetchScalarGridSpec(num_scalar_pr...  7.74 us
    ppermute x1, starting transfers between devices, shards(): other = lax.ppermute(image, 'yh', ring(H, 1))  6.09 us
  transfers between devices with their start and end apart: 7, of which 3 were waited for; matrix products, arithmetic and copies ran while one was open for 1% of the time, Pallas kernels for 7%

profile of v10, /device:TPU:1, one launch (start us, length us, event | category | flops | bytes accessed | tf_op | source)
XLA Modules:
  0.0 154.2 jit_solution(2629089381479416797)
XLA Ops:
  7.2 0.0 copy-start.1
  7.2 0.0 copy-start.2
  7.2 0.0 all-gather.2.cloned.1.call-start
  7.2 1.8 %fusion.5 = (bf16[96,384]{1,0:T(8,128)(2,1)S(1)}, f32[96,384]{1,0:T(8,128)}, bf16[96,384]{1,0:T(8,128)(2,1)S(1)}) fusion(f32[96,384]{1,0:T(8,128)} %param.7, f32[96,384]{1,0:T(8,128)} %param.6), kind=kLoop, calls=%fused_computation.20 | loop fusion | flops 184320 | bytes 589824 | tf_op jit(solution)/shard_map/convert
  9.0 15.4 %all_gather.9 = bf16[384,768]{1,0:T(8,128)(2,1)} all-gather(bf16[96,768]{1,0:T(8,128)(2,1)S(1)} %pad_maximum_fusion), channel_id=1, replica_groups=mesh['yl'=4,'z'=8,'c'=2,'x'=4,'yh'=2] {'yl'}, dimensions={0}, use_global_device_ids=true | all-gather | bytes 737280 | tf_op jit(solution)/shard_map/all_gather | solution.py:173
  24.4 0.0 all-gather.2.cloned.1.call-update
  24.5 0.0 copy-done.1
  24.5 6.1 %collective-permute-start = (bf16[256,768]{1,0:T(8,128)(2,1)S(1)}, bf16[256,768]{1,0:T(8,128)(2,1)S(1)}, u32[]{:S(2)}, u32[]{:S(2)}) collective-permute-start(bf16[256,768]{1,0:T(8,128)(2,1)S(1)} %bitcast.19), channel_id=1, source_target_pairs={{0,1},{1,0},{2,3},{3,2},{4,5},{5,4},{6,7},{7,6},{8,9},{9,8},{10,11... | collective-permute-start | bytes 1179656 | tf_op jit(solution)/shard_map/ppermute | solution.py:177
  30.6 0.1 convert_reduce_fusion
  30.7 0.2 fusion.1
  31.0 0.6 broadcast_in_dim.2
  31.6 5.7 %all-to-all-start = ((f32[8,2,256]{2,1,0:T(2,128)}), f32[8,2,256]{2,1,0:T(2,128)S(1)}, u32[]{:S(2)}, u32[]{:S(2)}) async-start(f32[8,2,256]{2,1,0:T(2,128)} %broadcast_in_dim.2), calls=%async_computation | async-start | bytes 32768 | tf_op jit(solution)/shard_map/all_to_all | solution.py:162
  37.3 0.0 copy-done.2
  37.3 0.1 fusion.2.select_ref.refs_6_
  37.4 13.9 %all-to-all-done = f32[8,2,256]{2,1,0:T(2,128)S(1)} async-done(((f32[8,2,256]{2,1,0:T(2,128)}), f32[8,2,256]{2,1,0:T(2,128)S(1)}, u32[]{:S(2)}, u32[]{:S(2)}) %all-to-all-start) | async-done | bytes 16416 | tf_op jit(solution)/shard_map/all_to_all | solution.py:162
  51.3 0.0 collective-permute-done
  51.3 0.2 maximum_select_fusion.chunk_ref.refs_0_
  51.5 2.2 %collective-permute-start.1 = (bf16[256,1536]{1,0:T(8,128)(2,1)S(1)}, bf16[256,1536]{1,0:T(8,128)(2,1)S(1)}, u32[]{:S(2)}, u32[]{:S(2)}) collective-permute-start(bf16[256,1536]{1,0:T(8,128)(2,1)S(1)} %maximum_select_fusion.chunk_ref.refs_0_), channel_id=1, source_target_pairs={{0,2},{2,4},{4,6},{6,0},{1,3},{3,5},{5,7},{7,1},{8,10},{10,12},{12... | collective-permute-start | bytes 2359304 | tf_op jit(solution)/shard_map/ppermute | solution.py:183
  53.8 3.6 %collective-permute-start.2 = (bf16[256,1536]{1,0:T(8,128)(2,1)S(1)}, bf16[256,1536]{1,0:T(8,128)(2,1)S(1)}, u32[]{:S(2)}, u32[]{:S(2)}) collective-permute-start(bf16[256,1536]{1,0:T(8,128)(2,1)S(1)} %maximum_select_fusion.chunk_ref.refs_0_), channel_id=1, source_target_pairs={{0,4},{2,6},{4,0},{6,2},{1,5},{3,7},{5,1},{7,3},{8,12},{10,14},{12... | collective-permute-start | bytes 2359304 | tf_op jit(solution)/shard_map/ppermute | solution.py:183
  57.4 2.9 %collective-permute-start.3 = (bf16[256,1536]{1,0:T(8,128)(2,1)S(1)}, bf16[256,1536]{1,0:T(8,128)(2,1)S(1)}, u32[]{:S(2)}, u32[]{:S(2)}) collective-permute-start(bf16[256,1536]{1,0:T(8,128)(2,1)S(1)} %maximum_select_fusion.chunk_ref.refs_0_), channel_id=1, source_target_pairs={{0,6},{2,0},{4,2},{6,4},{1,7},{3,1},{5,3},{7,5},{8,14},{10,8},{12,... | collective-permute-start | bytes 2359304 | tf_op jit(solution)/shard_map/ppermute | solution.py:183
  60.4 0.1 copy.17.scale_ref.refs_5_
  60.5 0.1 copy.16.centre_ref.refs_4_
  60.7 0.5 shard_map.59
  61.2 27.9 %all_to_all.20.rows_ref = bf16[16,64,96]{2,1,0:T(8,128)(2,1)S(1)} all-to-all(bf16[16,64,96]{2,1,0:T(8,128)(2,1)S(1)} %shard_map.59), channel_id=1, replica_groups=mesh['yl'=4,'z'=8,'c'=2,'x'=4,'yh'=2] {'z','c'}, dimensions={0} | all-to-all | bytes 393216 | tf_op jit(solution)/shard_map/all_to_all | solution.py:197
  89.1 1.0 shard_map.60
  90.2 0.0 collective-permute-done.1.refs_1_
  90.2 0.0 collective-permute-done.2.refs_2_
  90.2 2.3 %collective-permute-done.3.refs_3_ = bf16[256,1536]{1,0:T(8,128)(2,1)S(1)} collective-permute-done((bf16[256,1536]{1,0:T(8,128)(2,1)S(1)}, bf16[256,1536]{1,0:T(8,128)(2,1)S(1)}, u32[]{:S(2)}, u32[]{:S(2)}) %collective-permute-start.3) | collective-permute-done | bytes 786464 | tf_op jit(solution)/shard_map/ppermute | solution.py:183
  92.4 1.8 %shard_map.61.refs_1_ = bf16[4,320,1536]{2,1,0:T(8,128)(2,1)S(1)} custom-call(bf16[256,1536]{1,0:T(8,128)(2,1)S(1)} %maximum_select_fusion.chunk_ref.refs_0_, bf16[256,1536]{1,0:T(8,128)(2,1)S(1)} %collective-permute-done.1.refs_1_, bf16[256,1536]{1,0:T(8,128)(2,1)S(1)} %collective-permute-done.2.refs_2_, ...), custom_call_target="tpu_custom_call" | custom-call | flops 201326592 | bytes 7077888 | tf_op jit(solution)/shard_map/pallas_call | solution.py:65
  94.2 0.0 copy-start
  94.2 2.0 %copy-done = bf16[4,320,1536]{2,1,0:T(8,128)(2,1)} copy-done((bf16[4,320,1536]{2,1,0:T(8,128)(2,1)}, bf16[4,320,1536]{2,1,0:T(8,128)(2,1)S(1)}, u32[]{:S(2)}) %copy-start) | copy-done | bytes 3932184
  96.2 4.8 %all-to-all-start.2 = ((bf16[4,96,1024]{2,1,0:T(8,128)(2,1)}), bf16[4,96,1024]{2,1,0:T(8,128)(2,1)S(1)}, u32[]{:S(2)}, u32[]{:S(2)}) async-start(bf16[4,96,1024]{2,1,0:T(8,128)(2,1)} %shard_map.60), calls=%async_computation.2 | async-start | bytes 1572864 | tf_op jit(solution)/shard_map/all_to_all | solution.py:202
  101.0 1.3 all-gather.2.cloned.1.call-done
  102.3 7.7 %shard_map.62 = bf16[64,384]{1,0:T(8,128)(2,1)} custom-call(s32[1]{0:T(128)} %bitcast.7.refs_0_, bf16[4,320,1536]{2,1,0:T(8,128)(2,1)} %copy-done, bf16[16,4,96,768]{3,2,1,0:T(8,128)(2,1)} %bitcast.18), custom_call_target="tpu_custom_call" | custom-call | flops 1811939328 | bytes 13369344 | tf_op jit(solution)/shard_map/pallas_call | solution.py:132
  110.0 24.9 %all_gather.11 = bf16[1024,384]{1,0:T(8,128)(2,1)S(1)} all-gather(bf16[64,384]{1,0:T(8,128)(2,1)} %shard_map.62), channel_id=1, replica_groups=mesh['yl'=4,'z'=8,'c'=2,'x'=4,'yh'=2] {'z','c'}, dimensions={0}, use_global_device_ids=true | all-gather | bytes 835584 | tf_op jit(solution)/shard_map/all_gather | solution.py:206
  134.8 0.0 all-to-all-done.2
  134.8 0.6 convolution_convert_fusion
  135.4 11.2 %all_to_all.21 = bf16[4,96,384]{2,1,0:T(8,128)(2,1)S(1)} all-to-all(bf16[4,96,384]{2,1,0:T(8,128)(2,1)S(1)} %bitcast.24), channel_id=1, replica_groups=mesh['yl'=4,'z'=8,'c'=2,'x'=4,'yh'=2] {'yl'}, dimensions={0} | all-to-all | bytes 589824 | tf_op jit(solution)/shard_map/all_to_all | solution.py:208
  146.7 0.7 convert_reduce_fusion.1
  (7 shorter events, 0.1 us)
Async XLA Ops:
  7.2 17.3 %copy-start.1 = (bf16[1,256,768]{2,1,0:T(8,128)(2,1)S(1)}, bf16[1,256,768]{2,1,0:T(8,128)(2,1)}, u32[]{:S(2)}) copy-start(bf16[1,256,768]{2,1,0:T(8,128)(2,1)} %param.4) | copy-start | bytes 1179652
  7.2 30.1 %copy-start.2 = (s32[1,64]{1,0:T(1,128)S(1)}, s32[1,64]{1,0:T(1,128)}, u32[]{:S(2)}) copy-start(s32[1,64]{1,0:T(1,128)} %param.5) | copy-start | bytes 772
  7.2 95.1 %all-gather.2.cloned.1.call-start = ((), (), s32[]{:S(2)}) async-start(), calls=%async_computation.4 | async-start | bytes 10027008 | tf_op jit(solution)/shard_map/all_gather | solution.py:175
  24.5 26.9 %collective-permute-start = (bf16[256,768]{1,0:T(8,128)(2,1)S(1)}, bf16[256,768]{1,0:T(8,128)(2,1)S(1)}, u32[]{:S(2)}, u32[]{:S(2)}) collective-permute-start(bf16[256,768]{1,0:T(8,128)(2,1)S(1)} %bitcast.19), channel_id=1, source_target_pairs={{0,1},{1,0},{2,3},{3,2},{4,5},{5,4},{6,7},{7,6},{8,9},{9,8},{10,11... | collective-permute-start | bytes 1179656 | tf_op jit(solution)/shard_map/ppermute | solution.py:177
  31.6 19.7 %all-to-all-start = ((f32[8,2,256]{2,1,0:T(2,128)}), f32[8,2,256]{2,1,0:T(2,128)S(1)}, u32[]{:S(2)}, u32[]{:S(2)}) async-start(f32[8,2,256]{2,1,0:T(2,128)} %broadcast_in_dim.2), calls=%async_computation | async-start | bytes 32768 | tf_op jit(solution)/shard_map/all_to_all | solution.py:162
  51.5 38.6 %collective-permute-start.1 = (bf16[256,1536]{1,0:T(8,128)(2,1)S(1)}, bf16[256,1536]{1,0:T(8,128)(2,1)S(1)}, u32[]{:S(2)}, u32[]{:S(2)}) collective-permute-start(bf16[256,1536]{1,0:T(8,128)(2,1)S(1)} %maximum_select_fusion.chunk_ref.refs_0_), channel_id=1, source_target_pairs={{0,2},{2,4},{4,6},{6,0},{1,3},{3,5},{5,7},{7,1},{8,10},{10,12},{12... | collective-permute-start | bytes 2359304 | tf_op jit(solution)/shard_map/ppermute | solution.py:183
  53.8 36.4 %collective-permute-start.2 = (bf16[256,1536]{1,0:T(8,128)(2,1)S(1)}, bf16[256,1536]{1,0:T(8,128)(2,1)S(1)}, u32[]{:S(2)}, u32[]{:S(2)}) collective-permute-start(bf16[256,1536]{1,0:T(8,128)(2,1)S(1)} %maximum_select_fusion.chunk_ref.refs_0_), channel_id=1, source_target_pairs={{0,4},{2,6},{4,0},{6,2},{1,5},{3,7},{5,1},{7,3},{8,12},{10,14},{12... | collective-permute-start | bytes 2359304 | tf_op jit(solution)/shard_map/ppermute | solution.py:183
  57.4 35.0 %collective-permute-start.3 = (bf16[256,1536]{1,0:T(8,128)(2,1)S(1)}, bf16[256,1536]{1,0:T(8,128)(2,1)S(1)}, u32[]{:S(2)}, u32[]{:S(2)}) collective-permute-start(bf16[256,1536]{1,0:T(8,128)(2,1)S(1)} %maximum_select_fusion.chunk_ref.refs_0_), channel_id=1, source_target_pairs={{0,6},{2,0},{4,2},{6,4},{1,7},{3,1},{5,3},{7,5},{8,14},{10,8},{12,... | collective-permute-start | bytes 2359304 | tf_op jit(solution)/shard_map/ppermute | solution.py:183
  94.2 2.0 %copy-start = (bf16[4,320,1536]{2,1,0:T(8,128)(2,1)}, bf16[4,320,1536]{2,1,0:T(8,128)(2,1)S(1)}, u32[]{:S(2)}) copy-start(bf16[4,320,1536]{2,1,0:T(8,128)(2,1)S(1)} %shard_map.61.refs_1_) | copy-start | bytes 11796484
  96.2 38.6 %all-to-all-start.2 = ((bf16[4,96,1024]{2,1,0:T(8,128)(2,1)}), bf16[4,96,1024]{2,1,0:T(8,128)(2,1)S(1)}, u32[]{:S(2)}, u32[]{:S(2)}) async-start(bf16[4,96,1024]{2,1,0:T(8,128)(2,1)} %shard_map.60), calls=%async_computation.2 | async-start | bytes 1572864 | tf_op jit(solution)/shard_map/all_to_all | solution.py:202
Sparse Core Ops, SparseCore 0:
  24.6 77.6 all-gather.1

commit v11 on v10

--- a/solution.py
+++ b/solution.py
@@ -12,7 +12,6 @@
 Y, Z, C, X, H = 4, 8, 2, 4, 2
 BF, F32 = jnp.bfloat16, jnp.float32
 MB = 1024 * 1024
-PARTS = 1
 
 
 def normalised(chunk_ref, centre_ref, scale_ref):
@@ -93,10 +92,10 @@
     )(values)
 
 
-def error_kernel(factor, patches, x_ref, normed_ref, panel_ref, error_ref, teacher_acc, student_acc):
+def error_kernel(factor, patches, x_ref, normed_ref, near_ref, far_ref, error_ref, teacher_acc, student_acc):
     step = pl.program_id(0)
     columns = error_ref.shape[1]
-    panel = panel_ref[:, 0].reshape(-1, 2 * columns)
+    panel = jnp.concatenate([ref[:, 0].reshape(-1, 2 * columns) for ref in (near_ref, far_ref)], axis=0)
     teacher_part = jnp.dot(normed_ref[0], panel[:, :columns], preferred_element_type=F32)
     student_part = jnp.dot(normed_ref[0, patches:], panel[:, columns:], preferred_element_type=F32)
 
@@ -133,13 +132,13 @@
         body,
         grid_spec=pltpu.PrefetchScalarGridSpec(
             num_scalar_prefetch=1,
-            grid=(n * PARTS,),
+            grid=(n,),
             in_specs=[
-                pl.BlockSpec((1, rows_in, width // PARTS), lambda k, x: (k // PARTS, 0, lax.rem(k, PARTS))),
-                pl.BlockSpec(
-                    (blocks // PARTS, 1, rows, both),
-                    lambda k, x: (lax.rem(k, PARTS), lax.rem(x[0] + n - k // PARTS, n), 0, 0),
-                ),
+                pl.BlockSpec((1, rows_in, width), lambda k, x: (k, 0, 0)),
+            ]
+            + [
+                pl.BlockSpec((blocks // 2, 1, rows, both), lambda k, x, i=i: (i, lax.rem(x[0] + n - k, n), 0, 0))
+                for i in range(2)
             ],
             out_specs=pl.BlockSpec((keep, columns), lambda k, x: (0, 0)),
             scratch_shapes=[pltpu.VMEM((rows_in, columns), F32), pltpu.VMEM((keep, columns), F32)],
@@ -151,7 +150,7 @@
             bytes_accessed=2 * n * width * (rows_in + both),
             transcendentals=columns,
         ),
-    )(x, normed, panels)
+    )(x, normed, panels, panels)
 
 
 def ring(size, step):

time: 155 us -> 155 us (level)
  no operation moved by 1% of the time
where the time goes in v11:
time: 155 us; the launch traced here: 154 us
  blocking collectives  79.5 us (51%)
  starting transfers between devices  25.4 us (16%)
  waiting for transfers between devices  17.5 us (11%)
  between operations  14.2 us (9%)
  Pallas kernels  11 us (7%)
  other arithmetic  3.22 us (2%)
  local copies, waits for them, and re-layouts  2.85 us (2%)
    all_to_all x1, blocking collectives, shards(): pieces = lax.all_to_all(pieces, ('z', 'c'), split_axis=0, concat_axis=0)  27.9 us
    all_gather x1, blocking collectives, shards(): errors = lax.all_gather(error, ('z', 'c'), axis=0, tiled=True)  24.9 us
    all_gather x1, blocking collectives, shards(): panels = lax.all_gather(panel, 'yl', axis=0, tiled=True)  15.4 us
    all_to_all x1, waiting for transfers between devices, spread_to_all(): lax.all_to_all(jnp.broadcast_to(values[None], (size, *values.shape)), axe...  13.9 us
    all_to_all x1, blocking collectives, shards(): partial = lax.all_to_all(partial, 'yl', split_axis=0, concat_axis=0)  11.2 us
    ppermute x3, starting transfers between devices, shards(): arrived = [lax.ppermute(pair, 'x', ring(X, step)) for step in range(1, X)]  8.77 us
    pallas_call x1, Pallas kernels, make_error(): pl.pallas_call(body, grid_spec=pltpu.PrefetchScalarGridSpec(num_scalar_pr...  7.63 us
    ppermute x1, starting transfers between devices, shards(): other = lax.ppermute(image, 'yh', ring(H, 1))  6.09 us
  transfers between devices with their start and end apart: 7, of which 3 were waited for; matrix products, arithmetic and copies ran while one was open for 1% of the time, Pallas kernels for 7%

profile of v11, /device:TPU:1, one launch (start us, length us, event | category | flops | bytes accessed | tf_op | source)
XLA Modules:
  0.0 154.1 jit_solution(9352769136442381933)
XLA Ops:
  7.2 0.0 copy-start.1
  7.2 0.0 copy-start.2
  7.2 0.0 all-gather.2.cloned.1.call-start
  7.2 1.8 %fusion.5 = (bf16[96,384]{1,0:T(8,128)(2,1)S(1)}, f32[96,384]{1,0:T(8,128)}, bf16[96,384]{1,0:T(8,128)(2,1)S(1)}) fusion(f32[96,384]{1,0:T(8,128)} %param.7, f32[96,384]{1,0:T(8,128)} %param.6), kind=kLoop, calls=%fused_computation.20 | loop fusion | flops 184320 | bytes 589824 | tf_op jit(solution)/shard_map/convert
  9.0 15.4 %all_gather.9 = bf16[384,768]{1,0:T(8,128)(2,1)} all-gather(bf16[96,768]{1,0:T(8,128)(2,1)S(1)} %pad_maximum_fusion), channel_id=1, replica_groups=mesh['yl'=4,'z'=8,'c'=2,'x'=4,'yh'=2] {'yl'}, dimensions={0}, use_global_device_ids=true | all-gather | bytes 737280 | tf_op jit(solution)/shard_map/all_gather | solution.py:172
  24.4 0.0 all-gather.2.cloned.1.call-update
  24.5 0.0 copy-done.1
  24.5 6.1 %collective-permute-start = (bf16[256,768]{1,0:T(8,128)(2,1)S(1)}, bf16[256,768]{1,0:T(8,128)(2,1)S(1)}, u32[]{:S(2)}, u32[]{:S(2)}) collective-permute-start(bf16[256,768]{1,0:T(8,128)(2,1)S(1)} %bitcast.20), channel_id=1, source_target_pairs={{0,1},{1,0},{2,3},{3,2},{4,5},{5,4},{6,7},{7,6},{8,9},{9,8},{10,11... | collective-permute-start | bytes 1179656 | tf_op jit(solution)/shard_map/ppermute | solution.py:176
  30.6 0.1 convert_reduce_fusion
  30.7 0.2 fusion.1
  31.0 0.6 broadcast_in_dim.2
  31.6 5.7 %all-to-all-start = ((f32[8,2,256]{2,1,0:T(2,128)}), f32[8,2,256]{2,1,0:T(2,128)S(1)}, u32[]{:S(2)}, u32[]{:S(2)}) async-start(f32[8,2,256]{2,1,0:T(2,128)} %broadcast_in_dim.2), calls=%async_computation | async-start | bytes 32768 | tf_op jit(solution)/shard_map/all_to_all | solution.py:161
  37.3 0.0 copy-done.2
  37.3 0.1 fusion.2.select_ref.refs_6_
  37.4 13.9 %all-to-all-done = f32[8,2,256]{2,1,0:T(2,128)S(1)} async-done(((f32[8,2,256]{2,1,0:T(2,128)}), f32[8,2,256]{2,1,0:T(2,128)S(1)}, u32[]{:S(2)}, u32[]{:S(2)}) %all-to-all-start) | async-done | bytes 16416 | tf_op jit(solution)/shard_map/all_to_all | solution.py:161
  51.3 0.0 collective-permute-done
  51.3 0.2 maximum_select_fusion.chunk_ref.refs_0_
  51.5 2.2 %collective-permute-start.1 = (bf16[256,1536]{1,0:T(8,128)(2,1)S(1)}, bf16[256,1536]{1,0:T(8,128)(2,1)S(1)}, u32[]{:S(2)}, u32[]{:S(2)}) collective-permute-start(bf16[256,1536]{1,0:T(8,128)(2,1)S(1)} %maximum_select_fusion.chunk_ref.refs_0_), channel_id=1, source_target_pairs={{0,2},{2,4},{4,6},{6,0},{1,3},{3,5},{5,7},{7,1},{8,10},{10,12},{12... | collective-permute-start | bytes 2359304 | tf_op jit(solution)/shard_map/ppermute | solution.py:182
  53.8 3.6 %collective-permute-start.2 = (bf16[256,1536]{1,0:T(8,128)(2,1)S(1)}, bf16[256,1536]{1,0:T(8,128)(2,1)S(1)}, u32[]{:S(2)}, u32[]{:S(2)}) collective-permute-start(bf16[256,1536]{1,0:T(8,128)(2,1)S(1)} %maximum_select_fusion.chunk_ref.refs_0_), channel_id=1, source_target_pairs={{0,4},{2,6},{4,0},{6,2},{1,5},{3,7},{5,1},{7,3},{8,12},{10,14},{12... | collective-permute-start | bytes 2359304 | tf_op jit(solution)/shard_map/ppermute | solution.py:182
  57.4 2.9 %collective-permute-start.3 = (bf16[256,1536]{1,0:T(8,128)(2,1)S(1)}, bf16[256,1536]{1,0:T(8,128)(2,1)S(1)}, u32[]{:S(2)}, u32[]{:S(2)}) collective-permute-start(bf16[256,1536]{1,0:T(8,128)(2,1)S(1)} %maximum_select_fusion.chunk_ref.refs_0_), channel_id=1, source_target_pairs={{0,6},{2,0},{4,2},{6,4},{1,7},{3,1},{5,3},{7,5},{8,14},{10,8},{12,... | collective-permute-start | bytes 2359304 | tf_op jit(solution)/shard_map/ppermute | solution.py:182
  60.4 0.1 copy.17.scale_ref.refs_5_
  60.5 0.1 copy.16.centre_ref.refs_4_
  60.7 0.5 shard_map.59
  61.2 27.9 %all_to_all.20.rows_ref = bf16[16,64,96]{2,1,0:T(8,128)(2,1)S(1)} all-to-all(bf16[16,64,96]{2,1,0:T(8,128)(2,1)S(1)} %shard_map.59), channel_id=1, replica_groups=mesh['yl'=4,'z'=8,'c'=2,'x'=4,'yh'=2] {'z','c'}, dimensions={0} | all-to-all | bytes 393216 | tf_op jit(solution)/shard_map/all_to_all | solution.py:196
  89.1 1.0 shard_map.60
  90.2 0.0 collective-permute-done.1.refs_1_
  90.2 0.0 collective-permute-done.2.refs_2_
  90.2 2.3 %collective-permute-done.3.refs_3_ = bf16[256,1536]{1,0:T(8,128)(2,1)S(1)} collective-permute-done((bf16[256,1536]{1,0:T(8,128)(2,1)S(1)}, bf16[256,1536]{1,0:T(8,128)(2,1)S(1)}, u32[]{:S(2)}, u32[]{:S(2)}) %collective-permute-start.3) | collective-permute-done | bytes 786464 | tf_op jit(solution)/shard_map/ppermute | solution.py:182
  92.4 1.8 %shard_map.61.refs_1_ = bf16[4,320,1536]{2,1,0:T(8,128)(2,1)S(1)} custom-call(bf16[256,1536]{1,0:T(8,128)(2,1)S(1)} %maximum_select_fusion.chunk_ref.refs_0_, bf16[256,1536]{1,0:T(8,128)(2,1)S(1)} %collective-permute-done.1.refs_1_, bf16[256,1536]{1,0:T(8,128)(2,1)S(1)} %collective-permute-done.2.refs_2_, ...), custom_call_target="tpu_custom_call" | custom-call | flops 201326592 | bytes 7077888 | tf_op jit(solution)/shard_map/pallas_call | solution.py:64
  94.2 0.0 copy-start
  94.2 2.0 %copy-done = bf16[4,320,1536]{2,1,0:T(8,128)(2,1)} copy-done((bf16[4,320,1536]{2,1,0:T(8,128)(2,1)}, bf16[4,320,1536]{2,1,0:T(8,128)(2,1)S(1)}, u32[]{:S(2)}) %copy-start) | copy-done | bytes 3932184
  96.2 4.8 %all-to-all-start.2 = ((bf16[4,96,1024]{2,1,0:T(8,128)(2,1)}), bf16[4,96,1024]{2,1,0:T(8,128)(2,1)S(1)}, u32[]{:S(2)}, u32[]{:S(2)}) async-start(bf16[4,96,1024]{2,1,0:T(8,128)(2,1)} %shard_map.60), calls=%async_computation.2 | async-start | bytes 1572864 | tf_op jit(solution)/shard_map/all_to_all | solution.py:201
  101.0 1.3 all-gather.2.cloned.1.call-done
  102.3 7.6 %shard_map.62 = bf16[64,384]{1,0:T(8,128)(2,1)} custom-call(s32[1]{0:T(128)} %bitcast.7.refs_0_, bf16[4,320,1536]{2,1,0:T(8,128)(2,1)} %copy-done, bf16[16,4,96,768]{3,2,1,0:T(8,128)(2,1)} %bitcast.18, bf16[16,4,96,768]{3,2,1,0:T(8,128)(2,1)} %bitcast.19), custom_call_target="tpu_custom_call" | custom-call | flops 1811939328 | bytes 13369344 | tf_op jit(solution)/shard_map/pallas_call | solution.py:131
  109.9 24.9 %all_gather.11 = bf16[1024,384]{1,0:T(8,128)(2,1)S(1)} all-gather(bf16[64,384]{1,0:T(8,128)(2,1)} %shard_map.62), channel_id=1, replica_groups=mesh['yl'=4,'z'=8,'c'=2,'x'=4,'yh'=2] {'z','c'}, dimensions={0}, use_global_device_ids=true | all-gather | bytes 835584 | tf_op jit(solution)/shard_map/all_gather | solution.py:205
  134.7 0.0 all-to-all-done.2
  134.8 0.6 convolution_convert_fusion
  135.3 11.2 %all_to_all.21 = bf16[4,96,384]{2,1,0:T(8,128)(2,1)S(1)} all-to-all(bf16[4,96,384]{2,1,0:T(8,128)(2,1)S(1)} %bitcast.25), channel_id=1, replica_groups=mesh['yl'=4,'z'=8,'c'=2,'x'=4,'yh'=2] {'yl'}, dimensions={0} | all-to-all | bytes 589824 | tf_op jit(solution)/shard_map/all_to_all | solution.py:207
  146.6 0.7 convert_reduce_fusion.1
  (7 shorter events, 0.1 us)
Async XLA Ops:
  7.2 17.3 %copy-start.1 = (bf16[1,256,768]{2,1,0:T(8,128)(2,1)S(1)}, bf16[1,256,768]{2,1,0:T(8,128)(2,1)}, u32[]{:S(2)}) copy-start(bf16[1,256,768]{2,1,0:T(8,128)(2,1)} %param.4) | copy-start | bytes 1179652
  7.2 30.1 %copy-start.2 = (s32[1,64]{1,0:T(1,128)S(1)}, s32[1,64]{1,0:T(1,128)}, u32[]{:S(2)}) copy-start(s32[1,64]{1,0:T(1,128)} %param.5) | copy-start | bytes 772
  7.2 95.1 %all-gather.2.cloned.1.call-start = ((), (), s32[]{:S(2)}) async-start(), calls=%async_computation.4 | async-start | bytes 10027008 | tf_op jit(solution)/shard_map/all_gather | solution.py:174
  24.5 26.9 %collective-permute-start = (bf16[256,768]{1,0:T(8,128)(2,1)S(1)}, bf16[256,768]{1,0:T(8,128)(2,1)S(1)}, u32[]{:S(2)}, u32[]{:S(2)}) collective-permute-start(bf16[256,768]{1,0:T(8,128)(2,1)S(1)} %bitcast.20), channel_id=1, source_target_pairs={{0,1},{1,0},{2,3},{3,2},{4,5},{5,4},{6,7},{7,6},{8,9},{9,8},{10,11... | collective-permute-start | bytes 1179656 | tf_op jit(solution)/shard_map/ppermute | solution.py:176
  31.6 19.7 %all-to-all-start = ((f32[8,2,256]{2,1,0:T(2,128)}), f32[8,2,256]{2,1,0:T(2,128)S(1)}, u32[]{:S(2)}, u32[]{:S(2)}) async-start(f32[8,2,256]{2,1,0:T(2,128)} %broadcast_in_dim.2), calls=%async_computation | async-start | bytes 32768 | tf_op jit(solution)/shard_map/all_to_all | solution.py:161
  51.5 38.6 %collective-permute-start.1 = (bf16[256,1536]{1,0:T(8,128)(2,1)S(1)}, bf16[256,1536]{1,0:T(8,128)(2,1)S(1)}, u32[]{:S(2)}, u32[]{:S(2)}) collective-permute-start(bf16[256,1536]{1,0:T(8,128)(2,1)S(1)} %maximum_select_fusion.chunk_ref.refs_0_), channel_id=1, source_target_pairs={{0,2},{2,4},{4,6},{6,0},{1,3},{3,5},{5,7},{7,1},{8,10},{10,12},{12... | collective-permute-start | bytes 2359304 | tf_op jit(solution)/shard_map/ppermute | solution.py:182
  53.8 36.4 %collective-permute-start.2 = (bf16[256,1536]{1,0:T(8,128)(2,1)S(1)}, bf16[256,1536]{1,0:T(8,128)(2,1)S(1)}, u32[]{:S(2)}, u32[]{:S(2)}) collective-permute-start(bf16[256,1536]{1,0:T(8,128)(2,1)S(1)} %maximum_select_fusion.chunk_ref.refs_0_), channel_id=1, source_target_pairs={{0,4},{2,6},{4,0},{6,2},{1,5},{3,7},{5,1},{7,3},{8,12},{10,14},{12... | collective-permute-start | bytes 2359304 | tf_op jit(solution)/shard_map/ppermute | solution.py:182
  57.4 35.0 %collective-permute-start.3 = (bf16[256,1536]{1,0:T(8,128)(2,1)S(1)}, bf16[256,1536]{1,0:T(8,128)(2,1)S(1)}, u32[]{:S(2)}, u32[]{:S(2)}) collective-permute-start(bf16[256,1536]{1,0:T(8,128)(2,1)S(1)} %maximum_select_fusion.chunk_ref.refs_0_), channel_id=1, source_target_pairs={{0,6},{2,0},{4,2},{6,4},{1,7},{3,1},{5,3},{7,5},{8,14},{10,8},{12,... | collective-permute-start | bytes 2359304 | tf_op jit(solution)/shard_map/ppermute | solution.py:182
  94.2 2.0 %copy-start = (bf16[4,320,1536]{2,1,0:T(8,128)(2,1)}, bf16[4,320,1536]{2,1,0:T(8,128)(2,1)S(1)}, u32[]{:S(2)}) copy-start(bf16[4,320,1536]{2,1,0:T(8,128)(2,1)S(1)} %shard_map.61.refs_1_) | copy-start | bytes 11796484
  96.2 38.5 %all-to-all-start.2 = ((bf16[4,96,1024]{2,1,0:T(8,128)(2,1)}), bf16[4,96,1024]{2,1,0:T(8,128)(2,1)S(1)}, u32[]{:S(2)}, u32[]{:S(2)}) async-start(bf16[4,96,1024]{2,1,0:T(8,128)(2,1)} %shard_map.60), calls=%async_computation.2 | async-start | bytes 1572864 | tf_op jit(solution)/shard_map/all_to_all | solution.py:201
Sparse Core Ops, SparseCore 0:
  24.6 77.6 all-gather.1
